TPU v7x, 32 devices: a whole 2x2x4 slice. The times are simulated.
32 devices in a mesh: dp: 4 (over z), context: 8 (over y, x, core).
Axes of the slice: x: 2, y: 2, z: 4, core: 2. Of those that a mesh axis runs over, the one named last changes fastest.
Arguments:
- inputs: float32 [4096, 2560], P(('dp', 'context')), may hold values from -6 to 6
- segment_ids: int32 [4, 1024], P('dp'), may hold values from 0 to 5, never falling along the last dimension, each value on 1 to 512 neighbouring positions
- first_gain: bfloat16 [2560], P(('dp', 'context')), may hold values from 0.5 to 1.5
- gelu_in_w: bfloat16 [2560, 2560], P(('dp', 'context')), may hold values from -0.125 to 0.125
- linear_in_w: bfloat16 [2560, 2560], P(('dp', 'context')), may hold values from -0.125 to 0.125
- conv_weight: bfloat16 [4, 2560], P(None, ('dp', 'context')), may hold values from -3 to 3
- conv_bias: bfloat16 [2560], P(('dp', 'context')), may hold values from -3 to 3
- recur_gate_w: bfloat16 [2560, 256], P(('dp', 'context')), may hold values from -0.375 to 0.375
- recur_gate_b: bfloat16 [2560], P(('dp', 'context')), may hold values from -4 to 4
- input_gate_w: bfloat16 [2560, 256], P(('dp', 'context')), may hold values from -0.375 to 0.375
- input_gate_b: bfloat16 [2560], P(('dp', 'context')), may hold values from -4 to 4
- decay_param: bfloat16 [2560], P(('dp', 'context')), may hold values from -13 to -4
- out_proj_w: bfloat16 [2560, 2560], P(('dp', 'context')), may hold values from -0.5 to 0.5
- second_gain: bfloat16 [2560], P(('dp', 'context')), may hold values from 0.5 to 1.5
- mlp_gate_w: bfloat16 [2560, 7680], P(('dp', 'context')), may hold values from -0.125 to 0.125
- mlp_up_w: bfloat16 [2560, 7680], P(('dp', 'context')), may hold values from -0.125 to 0.125
- mlp_down_w: bfloat16 [7680, 2560], P(('dp', 'context')), may hold values from -0.0625 to 0.0625
- out_grad: float32 [4096, 2560], P(('dp', 'context')), may hold values from -6 to 6
Outputs:
- output: float32 [4096, 2560], P(('dp', 'context'))
- input_grad: float32 [4096, 2560], P(('dp', 'context'))
- grad_first_gain: float32 [2560], P(('dp', 'context'))
- grad_gelu_in_w: float32 [2560, 2560], P('dp', 'context')
- grad_linear_in_w: float32 [2560, 2560], P('dp', 'context')
- grad_conv_weight: float32 [4, 2560], P(None, ('dp', 'context'))
- grad_conv_bias: float32 [2560], P(('dp', 'context'))
- grad_recur_gate_w: float32 [2560, 256], P(('dp', 'context'))
- grad_recur_gate_b: float32 [2560], P(('dp', 'context'))
- grad_input_gate_w: float32 [2560, 256], P(('dp', 'context'))
- grad_input_gate_b: float32 [2560], P(('dp', 'context'))
- grad_decay_param: float32 [2560], P(('dp', 'context'))
- grad_out_proj_w: float32 [2560, 2560], P('dp', 'context')
- grad_second_gain: float32 [2560], P(('dp', 'context'))
- grad_mlp_gate_w: float32 [2560, 7680], P('dp', 'context')
- grad_mlp_up_w: float32 [2560, 7680], P('dp', 'context')
- grad_mlp_down_w: float32 [7680, 2560], P('context', 'dp')
Inputs may be any that keep to these rules, and one draw needn't show every extreme that they name: `segment_ids`: within each sequence the ids never fall; each of the 6 ids names 1 to 512 positions, and one names exactly 512.
All inputs are finite; a program needn't handle non-finite values.
Results may differ from a plain program's by a relative error of at most 0.013.
Values may be sent and summed in bfloat16 or wider, within the bound.
A program may use at most 512 MiB of HBM per device.

v0:
```python
import jax
import jax.numpy as jnp
from jax import lax
from jax.sharding import PartitionSpec as P

HEADS = 10
CONV = 4


def shifted(value, axis, steps):
    count = lax.axis_size(axis)
    first, last = (max(0, -steps), min(count, count - steps))
    return lax.ppermute(value, axis, [(source, source + steps) for source in range(first, last)])


def rms_scale(values, gain_vec):
    return values * lax.rsqrt(jnp.mean(values * values, axis=-1, keepdims=True) + 1e-06) * gain_vec


def combine_pair(earlier, latter):
    return (earlier[0] * latter[0], latter[0] * earlier[1] + latter[1])


def gate_values(recur_in, input_in, conv_out, decay_vals, is_reset):
    rec_gate = jax.nn.sigmoid(recur_in)
    in_gate = jax.nn.sigmoid(input_in)
    log_decay = -8.0 * jax.nn.softplus(decay_vals) * rec_gate
    decays = jnp.where(is_reset, 0.0, jnp.exp(log_decay))
    in_scale = jnp.where(is_reset, 1.0, jnp.sqrt(-jnp.expm1(2.0 * log_decay)))
    return (decays, in_scale * in_gate * conv_out)


def block_dot(values, weight):
    row_count = values.shape[0]
    width_block = weight.shape[1]
    result = jnp.einsum(
        "thi,hio->tho",
        values.reshape(row_count, HEADS, width_block),
        weight.reshape(HEADS, width_block, width_block),
        preferred_element_type=jnp.float32,
    )
    return result.reshape(row_count, HEADS * width_block)


def block_back(grads_low, weight):
    row_count = grads_low.shape[0]
    width_block = weight.shape[1]
    result = jnp.einsum(
        "tho,hio->thi",
        grads_low.reshape(row_count, HEADS, width_block),
        weight.reshape(HEADS, width_block, width_block),
        preferred_element_type=jnp.float32,
    )
    return result.reshape(row_count, HEADS * width_block)


def block_grad(values, grads_low):
    row_count = values.shape[0]
    width_block = values.shape[1] // HEADS
    result = jnp.einsum(
        "thi,tho->hio",
        values.reshape(row_count, HEADS, width_block),
        grads_low.reshape(row_count, HEADS, width_block),
        preferred_element_type=jnp.float32,
    )
    return result.reshape(HEADS * width_block, width_block)


def inner_rows(left, right):
    return lax.dot_general(
        left, right, (((0,), (0,)), ((), ())), preferred_element_type=jnp.float32
    )


def per_device(
    inputs,
    segment_ids,
    first_gain,
    gelu_in_w,
    linear_in_w,
    conv_weight,
    conv_bias,
    recur_gate_w,
    recur_gate_b,
    input_gate_w,
    input_gate_b,
    decay_param,
    out_proj_w,
    second_gain,
    mlp_gate_w,
    mlp_up_w,
    mlp_down_w,
    out_grad,
):
    tok_rows = inputs.shape[0]
    reach = CONV - 1
    place = lax.axis_index("context")
    padded_ids = jnp.concatenate([jnp.full((reach,), -1, jnp.int32), segment_ids[0]])
    local_ids = lax.dynamic_slice_in_dim(padded_ids, place * tok_rows, tok_rows + reach)
    own_ids = local_ids[reach:]
    same_doc = [
        (local_ids[reach - offset : reach - offset + tok_rows] == own_ids).astype(jnp.float32)[
            :, None
        ]
        for offset in range(CONV)
    ]
    is_reset = (local_ids[reach - 1 : reach - 1 + tok_rows] != own_ids)[:, None]
    (
        gain_one,
        gelu_w,
        linear_w,
        conv_w,
        conv_b,
        recur_w,
        recur_b,
        input_w,
        input_b,
        decay_w,
        proj_w,
    ) = (
        lax.all_gather(first_gain, ("dp", "context"), axis=0, tiled=True),
        lax.all_gather(gelu_in_w, ("dp", "context"), axis=0, tiled=True),
        lax.all_gather(linear_in_w, ("dp", "context"), axis=0, tiled=True),
        lax.all_gather(conv_weight, ("dp", "context"), axis=1, tiled=True),
        lax.all_gather(conv_bias, ("dp", "context"), axis=0, tiled=True),
        lax.all_gather(recur_gate_w, ("dp", "context"), axis=0, tiled=True),
        lax.all_gather(recur_gate_b, ("dp", "context"), axis=0, tiled=True),
        lax.all_gather(input_gate_w, ("dp", "context"), axis=0, tiled=True),
        lax.all_gather(input_gate_b, ("dp", "context"), axis=0, tiled=True),
        lax.all_gather(decay_param, ("dp", "context"), axis=0, tiled=True),
        lax.all_gather(out_proj_w, ("dp", "context"), axis=0, tiled=True),
    )
    gain_first = gain_one.astype(jnp.float32)
    normed = rms_scale(inputs, gain_first).astype(jnp.bfloat16)
    gelu_pre = jnp.dot(normed, gelu_w, preferred_element_type=jnp.float32)
    linear_out = jnp.dot(normed, linear_w, preferred_element_type=jnp.float32).astype(jnp.bfloat16)
    prev_rows = shifted(linear_out[tok_rows - reach :], "context", 1)
    linear_ext = jnp.concatenate([prev_rows, linear_out], axis=0).astype(jnp.float32)
    conv_wf = conv_w.astype(jnp.float32)
    window_rows = [
        linear_ext[reach - offset : reach - offset + tok_rows] * same_doc[offset]
        for offset in range(CONV)
    ]
    conv_out = conv_b.astype(jnp.float32)[None, :] + conv_wf[0][None, :] * window_rows[0]
    for offset in range(1, CONV):
        conv_out = conv_out + conv_wf[offset][None, :] * window_rows[offset]
    conv_low = conv_out.astype(jnp.bfloat16)
    recur_pre = block_dot(conv_low, recur_w)
    input_pre = block_dot(conv_low, input_w)

    def gate_piece(recur_val, input_val, recur_bias, input_bias, conv_vals, decay_vals):
        return gate_values(
            recur_val + recur_bias, input_val + input_bias, conv_vals, decay_vals, is_reset
        )

    (decays, driven), gate_pull = jax.vjp(
        gate_piece,
        recur_pre,
        input_pre,
        recur_b.astype(jnp.float32),
        input_b.astype(jnp.float32),
        conv_out,
        decay_w.astype(jnp.float32),
    )
    decay_cum, state_local = lax.associative_scan(combine_pair, (decays, driven), axis=0)
    head_decay = decay_cum[-1]
    head_state = state_local[-1]

    def pass_along(step_idx, held):
        return shifted(head_decay * held + head_state, "context", 1)

    carry_in = lax.fori_loop(
        0, lax.axis_size("context") - 1, pass_along, jnp.zeros_like(head_state)
    )
    states = state_local + decay_cum * carry_in[None, :]
    gelu_out, gelu_pull = jax.vjp(jax.nn.gelu, gelu_pre)
    mixed_rows = (gelu_out * states).astype(jnp.bfloat16)
    hidden = inputs + jnp.dot(mixed_rows, proj_w, preferred_element_type=jnp.float32)
    gain_two, mlp_gate, mlp_up, mlp_down = (
        lax.all_gather(second_gain, ("dp", "context"), axis=0, tiled=True),
        lax.all_gather(mlp_gate_w, ("dp", "context"), axis=0, tiled=True),
        lax.all_gather(mlp_up_w, ("dp", "context"), axis=0, tiled=True),
        lax.all_gather(mlp_down_w, ("dp", "context"), axis=0, tiled=True),
    )
    gain_second = gain_two.astype(jnp.float32)
    second_normed = rms_scale(hidden, gain_second).astype(jnp.bfloat16)
    gate_pre = jnp.dot(second_normed, mlp_gate, preferred_element_type=jnp.float32)
    up_pre = jnp.dot(second_normed, mlp_up, preferred_element_type=jnp.float32)
    activation_full, mlp_pull = jax.vjp(
        lambda first_in, second_in: jax.nn.gelu(first_in) * second_in, gate_pre, up_pre
    )
    activation = activation_full.astype(jnp.bfloat16)
    output = hidden + jnp.dot(activation, mlp_down, preferred_element_type=jnp.float32)
    back_gate, back_up, back_down = (mlp_gate, mlp_up, mlp_down)
    down_grad = out_grad.astype(jnp.bfloat16)
    act_grad = jnp.dot(down_grad, back_down.T, preferred_element_type=jnp.float32)
    gate_grad, up_grad = mlp_pull(act_grad)
    gate_low = gate_grad.astype(jnp.bfloat16)
    up_low = up_grad.astype(jnp.bfloat16)
    second_grad = jnp.dot(gate_low, back_gate.T, preferred_element_type=jnp.float32) + jnp.dot(
        up_low, back_up.T, preferred_element_type=jnp.float32
    )
    norm_two_out, norm_two_pull = jax.vjp(rms_scale, hidden, gain_second)
    hidden_part, grad_gain_two = norm_two_pull(second_grad)
    hidden_grad = out_grad + hidden_part
    branch_grad = hidden_grad.astype(jnp.bfloat16)
    mixed_grad = jnp.dot(branch_grad, proj_w.T, preferred_element_type=jnp.float32)
    state_grad = mixed_grad * gelu_out
    (gelu_grad,) = gelu_pull(mixed_grad * states)
    gelu_low = gelu_grad.astype(jnp.bfloat16)
    next_decay = jnp.concatenate([decays[1:], jnp.ones((1, decays.shape[1]), jnp.float32)], axis=0)
    back_cum, lam_local = lax.associative_scan(
        combine_pair, (next_decay, state_grad), reverse=True, axis=0
    )
    tail_decay = decays[0] * back_cum[0]
    tail_value = decays[0] * lam_local[0]

    def pass_back(step_idx, held):
        return shifted(tail_decay * held + tail_value, "context", -1)

    carry_back = lax.fori_loop(
        0, lax.axis_size("context") - 1, pass_back, jnp.zeros_like(tail_value)
    )
    lam_full = lam_local + back_cum * carry_back[None, :]
    prev_states = jnp.concatenate([carry_in[None, :], states[:-1]], axis=0)
    recur_grad, input_pre_grad, grad_recur_bias, grad_input_bias, conv_gate_grad, grad_decay = (
        gate_pull((lam_full * prev_states, lam_full))
    )
    recur_low = recur_grad.astype(jnp.bfloat16)
    input_low = input_pre_grad.astype(jnp.bfloat16)
    grad_recur_w = block_grad(conv_low, recur_low)
    grad_input_w = block_grad(conv_low, input_low)
    conv_grad = conv_gate_grad + block_back(recur_low, recur_w) + block_back(input_low, input_w)
    grad_conv_b = jnp.sum(conv_grad, axis=0)
    tap_grads = []
    linear_ext_grad = jnp.zeros_like(linear_ext)
    for offset in range(CONV):
        masked = conv_grad * same_doc[offset]
        tap_grads.append(
            jnp.sum(masked * linear_ext[reach - offset : reach - offset + tok_rows], axis=0)
        )
        linear_ext_grad = linear_ext_grad + jnp.pad(
            masked * conv_wf[offset][None, :], ((reach - offset, offset), (0, 0))
        )
    grad_conv_w = jnp.stack(tap_grads)
    from_next = shifted(linear_ext_grad[:reach], "context", -1)
    linear_grad = linear_ext_grad[reach:] + jnp.pad(from_next, ((tok_rows - reach, 0), (0, 0)))
    linear_low = linear_grad.astype(jnp.bfloat16)
    first_grad = jnp.dot(gelu_low, gelu_w.T, preferred_element_type=jnp.float32) + jnp.dot(
        linear_low, linear_w.T, preferred_element_type=jnp.float32
    )
    norm_one_out, norm_one_pull = jax.vjp(rms_scale, inputs, gain_first)
    input_part, grad_gain_one = norm_one_pull(first_grad)
    input_grad = hidden_grad + input_part
    gelu_cols, linear_cols, branch_cols, gate_cols, up_cols, act_cols = (
        lax.all_to_all(gelu_low, "context", split_axis=1, concat_axis=0, tiled=True),
        lax.all_to_all(linear_low, "context", split_axis=1, concat_axis=0, tiled=True),
        lax.all_to_all(branch_grad, "context", split_axis=1, concat_axis=0, tiled=True),
        lax.all_to_all(gate_low, "context", split_axis=1, concat_axis=0, tiled=True),
        lax.all_to_all(up_low, "context", split_axis=1, concat_axis=0, tiled=True),
        lax.all_to_all(activation, "context", split_axis=1, concat_axis=0, tiled=True),
    )
    pieces = (
        lax.all_gather(normed, "context", axis=0, tiled=True),
        lax.all_gather(mixed_rows, "context", axis=0, tiled=True),
        lax.all_gather(second_normed, "context", axis=0, tiled=True),
        lax.all_gather(down_grad, "context", axis=0, tiled=True),
    )
    weight_sums = (
        lax.psum_scatter(
            inner_rows(pieces[0], gelu_cols).astype(jnp.bfloat16),
            "dp",
            scatter_dimension=0,
            tiled=True,
        ).astype(jnp.float32),
        lax.psum_scatter(
            inner_rows(pieces[0], linear_cols).astype(jnp.bfloat16),
            "dp",
            scatter_dimension=0,
            tiled=True,
        ).astype(jnp.float32),
        lax.psum_scatter(
            inner_rows(pieces[1], branch_cols).astype(jnp.bfloat16),
            "dp",
            scatter_dimension=0,
            tiled=True,
        ).astype(jnp.float32),
        lax.psum_scatter(
            inner_rows(pieces[2], gate_cols).astype(jnp.bfloat16),
            "dp",
            scatter_dimension=0,
            tiled=True,
        ).astype(jnp.float32),
        lax.psum_scatter(
            inner_rows(pieces[2], up_cols).astype(jnp.bfloat16),
            "dp",
            scatter_dimension=0,
            tiled=True,
        ).astype(jnp.float32),
        lax.psum_scatter(
            inner_rows(act_cols, pieces[3]).astype(jnp.bfloat16),
            "dp",
            scatter_dimension=1,
            tiled=True,
        ).astype(jnp.float32),
    )
    small_sums = (
        lax.psum_scatter(grad_gain_one, ("dp", "context"), scatter_dimension=0, tiled=True),
        lax.psum_scatter(grad_conv_w, ("dp", "context"), scatter_dimension=1, tiled=True),
        lax.psum_scatter(grad_conv_b, ("dp", "context"), scatter_dimension=0, tiled=True),
        lax.psum_scatter(grad_recur_w, ("dp", "context"), scatter_dimension=0, tiled=True),
        lax.psum_scatter(grad_recur_bias, ("dp", "context"), scatter_dimension=0, tiled=True),
        lax.psum_scatter(grad_input_w, ("dp", "context"), scatter_dimension=0, tiled=True),
        lax.psum_scatter(grad_input_bias, ("dp", "context"), scatter_dimension=0, tiled=True),
        lax.psum_scatter(grad_decay, ("dp", "context"), scatter_dimension=0, tiled=True),
        lax.psum_scatter(grad_gain_two, ("dp", "context"), scatter_dimension=0, tiled=True),
    )
    return (
        output,
        input_grad,
        small_sums[0],
        weight_sums[0],
        weight_sums[1],
        small_sums[1],
        small_sums[2],
        small_sums[3],
        small_sums[4],
        small_sums[5],
        small_sums[6],
        small_sums[7],
        weight_sums[2],
        small_sums[8],
        weight_sums[3],
        weight_sums[4],
        weight_sums[5],
    )


def solution(mesh):
    return jax.shard_map(
        per_device,
        mesh=mesh,
        in_specs=(
            P(("dp", "context"), None),
            P("dp", None),
            P(("dp", "context")),
            P(("dp", "context"), None),
            P(("dp", "context"), None),
            P(None, ("dp", "context")),
            P(("dp", "context")),
            P(("dp", "context"), None),
            P(("dp", "context")),
            P(("dp", "context"), None),
            P(("dp", "context")),
            P(("dp", "context")),
            P(("dp", "context"), None),
            P(("dp", "context")),
            P(("dp", "context"), None),
            P(("dp", "context"), None),
            P(("dp", "context"), None),
            P(("dp", "context"), None),
        ),
        out_specs=(
            P(("dp", "context"), None),
            P(("dp", "context"), None),
            P(("dp", "context")),
            P("dp", "context"),
            P("dp", "context"),
            P(None, ("dp", "context")),
            P(("dp", "context")),
            P(("dp", "context"), None),
            P(("dp", "context")),
            P(("dp", "context"), None),
            P(("dp", "context")),
            P(("dp", "context")),
            P("dp", "context"),
            P(("dp", "context")),
            P("dp", "context"),
            P("dp", "context"),
            P("context", "dp"),
        ),
        check_vma=False,
    )
```

profile of v0, /device:TPU:1, one launch (start us, length us, event | category | flops | bytes accessed | tf_op | source)
XLA Modules:
  0.0 2212.9 jit_solution(9310291381522308719)
XLA Ops:
  14.3 44.0 %all-reduce.77 = (bf16[2560]{0:T(1024)(128)(2,1)S(1)}, bf16[2560]{0:T(1024)(128)(2,1)S(1)}, bf16[2560]{0:T(1024)(128)(2,1)S(1)}, bf16[2560]{0:T(1024)(128)(2,1)S...) all-reduce(bf16[2560]{0:T(1024)(128)(2,1)S(1)} %dynamic-update-slic, ...), channel_id=1, replica_groups=mesh['dp'=4,'context'=8] {'dp','context'}, use_global_device_ids=true, to_apply=%add.65 | all-reduce | flops 15360 | bytes 61440
  58.4 40.0 %all-gather = bf16[32,80,4]{1,2,0:T(4,128)(2,1)S(1)} all-gather(bf16[1,80,4]{1,2,0:T(4,128)(2,1)S(1)} %bitcast.161), channel_id=1, replica_groups=mesh['dp'=4,'context'=8] {'dp','context'}, dimensions={0}, use_global_device_ids=true | all-gather | bytes 21120 | tf_op jit(solution)/shard_map/all_gather | solution.py:124
  99.1 13.7 all-gather.16.cloned.1.call-done
  125.9 42.3 %all-gather.18.cloned.1.call-done = bf16[2560,256]{1,0:T(8,128)(2,1)} async-done(((bf16[80,256]{1,0:T(8,128)(2,1)}), bf16[2560,256]{1,0:T(8,128)(2,1)}) %all-gather.18.cloned.1.call-update) | async-done | bytes 1310736 | tf_op jit(solution)/shard_map/all_gather | solution.py:126
  173.1 51.2 %all-gather.20.cloned.1.call-done = bf16[2560,256]{1,0:T(8,128)(2,1)} async-done(((bf16[80,256]{1,0:T(8,128)(2,1)}), bf16[2560,256]{1,0:T(8,128)(2,1)}) %all-gather.20.cloned.1.call-update) | async-done | bytes 1310736 | tf_op jit(solution)/shard_map/all_gather | solution.py:128
  370.5 35.3 %while.20 = (s32[]{:T(128)}, f32[2560]{0:T(1024)S(1)}, f32[2560]{0:T(1024)S(1)}, f32[2560]{0:T(1024)S(1)}, s32[]{:T(128)}) while((s32[]{:T(128)}, f32[2560]{0:T(1024)S(1)}, f32[2560]{0:T(1024)S(1)}, f32[2560]{0:T(1024)S(1)}, s32[]{:T(128)}) %tuple.109), condition=%wide.region_2.3_spmd, body=%wide.region_1.2_spmd.sunk | while | flops 5122 | bytes 82021 | solution.py:172
  405.8 10.9 multiply_convert_fusion.3
  459.4 188.6 %all-gather.24.cloned.1.call-done = bf16[2560,7680]{1,0:T(8,128)(2,1)} async-done(((bf16[80,7680]{1,0:T(8,128)(2,1)}), bf16[2560,7680]{1,0:T(8,128)(2,1)}) %all-gather.24.cloned.1.call-update) | async-done | bytes 39321616 | tf_op jit(solution)/shard_map/all_gather | solution.py:181
  647.9 18.1 fusion.85
  666.1 205.4 %all-gather.26.cloned.1.call-done = bf16[2560,7680]{1,0:T(8,128)(2,1)} async-done(((bf16[80,7680]{1,0:T(8,128)(2,1)}), bf16[2560,7680]{1,0:T(8,128)(2,1)}) %all-gather.26.cloned.1.call-update) | async-done | bytes 39321616 | tf_op jit(solution)/shard_map/all_gather | solution.py:182
  871.5 18.3 fusion.86
  889.8 205.3 %all-gather.28.cloned.1.call-done = bf16[7680,2560]{1,0:T(8,128)(2,1)} async-done(((bf16[240,2560]{1,0:T(8,128)(2,1)}), bf16[7680,2560]{1,0:T(8,128)(2,1)}) %all-gather.28.cloned.1.call-update) | async-done | bytes 39321616 | tf_op jit(solution)/shard_map/all_gather | solution.py:183
  1095.1 24.8 %multiply_convert_fusion = (bf16[128,7680]{1,0:T(8,128)(2,1)}, bf16[128,7680]{1,0:T(8,128)(2,1)}, bf16[128,7680]{1,0:T(8,128)(2,1)}) fusion(f32[128,7680]{1,0:T(8,128)} %fusion.85, f32[128,7680]{1,0:T(8,128)} %fusion.86, bf16[128,2560]{1,0:T(8,128)(2,1)S(1)} %copy-done.48, bf16[7680,2560]{1,0:T(8,128)(2,1)} %all-gather.28.cloned.1.call-done), kind=kOutput, calls=%fused_computation.17 | convolution fusion | flops 5058723840 | bytes 53739520 | tf_op jit(solution)/shard_map/dot_general | solution.py:196
  1120.0 19.8 fusion.87
  1139.7 21.0 multiply_reduce_fusion
  1164.6 10.7 fusion.38
  1177.3 9.9 slice.581
  1272.5 10.8 rev.9
  1294.0 10.8 rev.8
  1306.0 36.5 %while.21 = (s32[]{:T(128)}, f32[2560]{0:T(1024)S(1)}, f32[2560]{0:T(1024)S(1)}, f32[2560]{0:T(1024)S(1)}, s32[]{:T(128)}) while((s32[]{:T(128)}, f32[2560]{0:T(1024)S(1)}, f32[2560]{0:T(1024)S(1)}, f32[2560]{0:T(1024)S(1)}, s32[]{:T(128)}) %tuple.112), condition=%wide.region_6.7_spmd, body=%wide.region_5.6_spmd.sunk | while | flops 5122 | bytes 82021 | solution.py:221
  1423.0 15.0 all_to_all.114
  1453.0 23.8 %all-to-all-done.3 = bf16[128,8,960]{0,2,1:T(8,128)(2,1)S(1)} async-done(((bf16[128,8,960]{0,2,1:T(8,128)(2,1)}), bf16[128,8,960]{0,2,1:T(8,128)(2,1)S(1)}, u32[]{:S(2)}, u32[]{:S(2)}) %all-to-all-start.3) | async-done | bytes 1966112 | tf_op jit(solution)/shard_map/all_to_all | solution.py:259
  1497.9 32.4 %all_to_all.115 = bf16[128,8,960]{0,2,1:T(8,128)(2,1)S(1)} all-to-all(bf16[128,8,960]{0,2,1:T(8,128)(2,1)} %bitcast.141), channel_id=1, replica_groups=mesh['dp'=4,'context'=8] {'context'}, dimensions={1} | all-to-all | bytes 3932160 | tf_op jit(solution)/shard_map/all_to_all | solution.py:260
  1556.3 21.7 all-to-all-done.5
  1603.1 10.1 fusion.88
  1613.2 16.5 convolution_add_fusion.1
  1639.3 47.9 %all-reduce.76 = (f32[2560]{0:T(1024)S(1)}, f32[2560]{0:T(1024)S(1)}, f32[2560]{0:T(1024)S(1)}, f32[2560]{0:T(1024)S(1)}, f32[2560]{0:T(1024)S(1)}, /*index=5*/f32[2560]{0:T(1024)S(1)}) all-reduce(f32[2560]{0:T(1024)S(1)} %get-tuple-element.71, ...), channel_id=2, replica_groups=mesh['dp'=4,'context'=8] {'dp','context'}, use_global_device_ids=true, to_apply=%region_9.10.clone | all-reduce | flops 15360 | bytes 122880
  1701.6 38.5 %reduce-scatter.36.cloned.1.call-done = bf16[640,960]{1,0:T(8,128)(2,1)} async-done(((bf16[2560,960]{1,0:T(8,128)(2,1)}), bf16[640,960]{1,0:T(8,128)(2,1)}) %reduce-scatter.36.cloned.1.call-update) | async-done | bytes 1228816
  1743.8 92.8 %reduce-scatter.38.cloned.1.call-done = bf16[640,960]{1,0:T(8,128)(2,1)} async-done(((bf16[2560,960]{1,0:T(8,128)(2,1)}), bf16[640,960]{1,0:T(8,128)(2,1)}) %reduce-scatter.38.cloned.1.call-update) | async-done | bytes 1228816
  1840.4 93.0 %reduce-scatter.40.cloned.1.call-done = bf16[640,960]{1,0:T(8,128)(2,1)} async-done(((bf16[2560,960]{1,0:T(8,128)(2,1)}), bf16[640,960]{1,0:T(8,128)(2,1)}) %reduce-scatter.40.cloned.1.call-update) | async-done | bytes 1228816
  1937.1 131.9 %reduce-scatter.24.cloned.1.call-done = f32[80,256]{1,0:T(8,128)} async-done(((f32[2560,256]{1,0:T(8,128)}), f32[80,256]{1,0:T(8,128)}) %reduce-scatter.24.cloned.1.call-update) | async-done | bytes 81936 | tf_op jit(solution)/shard_map/reduce_scatter | solution.py:311
  2069.0 136.5 %reduce-scatter.26.cloned.1.call-done = f32[80,256]{1,0:T(8,128)} async-done(((f32[2560,256]{1,0:T(8,128)}), f32[80,256]{1,0:T(8,128)}) %reduce-scatter.26.cloned.1.call-update) | async-done | bytes 81936 | tf_op jit(solution)/shard_map/reduce_scatter | solution.py:313
  (697 shorter events, 590.2 us)
Async XLA Ops:
  7.2 105.6 %all-gather.16.cloned.1.call-start = ((), (), s32[]{:S(2)}) async-start(), calls=%async_computation.16 | async-start | bytes 13516800 | tf_op jit(solution)/shard_map/all_gather | solution.py:123
  7.9 160.3 %all-gather.18.cloned.1.call-start = ((), (), s32[]{:S(2)}) async-start(), calls=%async_computation.17 | async-start | bytes 1351680 | tf_op jit(solution)/shard_map/all_gather | solution.py:126
  8.7 215.6 %all-gather.20.cloned.1.call-start = ((), (), s32[]{:S(2)}) async-start(), calls=%async_computation.18 | async-start | bytes 1351680 | tf_op jit(solution)/shard_map/all_gather | solution.py:128
  9.4 361.1 %all-gather.14.cloned.1.call-start = ((), (), s32[]{:S(2)}) async-start(), calls=%async_computation.15 | async-start | bytes 13516800 | tf_op jit(solution)/shard_map/all_gather | solution.py:122
  10.0 414.5 %all-gather.22.cloned.1.call-start = ((), (), s32[]{:S(2)}) async-start(), calls=%async_computation.19 | async-start | bytes 13516800 | tf_op jit(solution)/shard_map/all_gather | solution.py:131
  10.6 637.4 %all-gather.24.cloned.1.call-start = ((), (), s32[]{:S(2)}) async-start(), calls=%async_computation.20 | async-start | bytes 40550400 | tf_op jit(solution)/shard_map/all_gather | solution.py:181
  11.2 860.3 %all-gather.26.cloned.1.call-start = ((), (), s32[]{:S(2)}) async-start(), calls=%async_computation.21 | async-start | bytes 40550400 | tf_op jit(solution)/shard_map/all_gather | solution.py:182
  12.0 1083.1 %all-gather.28.cloned.1.call-start = ((), (), s32[]{:S(2)}) async-start(), calls=%async_computation.22 | async-start | bytes 40550400 | tf_op jit(solution)/shard_map/all_gather | solution.py:183
  12.7 1368.9 %all-gather.32.cloned.1.call-start = ((), (), s32[]{:S(2)}) async-start(), calls=%async_computation.26 | async-start | bytes 5898240 | tf_op jit(solution)/shard_map/all_gather | solution.py:265
  384.4 5.2 collective-permute-start
  389.6 5.2 collective-permute-start
  394.9 5.2 collective-permute-start
  400.1 5.7 collective-permute-start
  416.7 982.1 %all-gather.30.cloned.1.call-start = ((), (), s32[]{:S(2)}) async-start(), calls=%async_computation.23 | async-start | bytes 5898240 | tf_op jit(solution)/shard_map/all_gather | solution.py:264
  417.3 1035.8 %all-gather.34.cloned.1.call-start = ((), (), s32[]{:S(2)}) async-start(), calls=%async_computation.27 | async-start | bytes 5898240 | tf_op jit(solution)/shard_map/all_gather | solution.py:266
  433.4 1123.0 %all-gather.36.cloned.1.call-start = ((), (), s32[]{:S(2)}) async-start(), calls=%async_computation.28 | async-start | bytes 5898240 | tf_op jit(solution)/shard_map/all_gather | solution.py:267
  1331.0 5.5 collective-permute-start.1
  1336.6 5.9 collective-permute-start.1
  1367.5 15.1 all-to-all-start.2
  1374.9 318.6 %reduce-scatter.32.cloned.1.call-start = ((), (), s32[]{:S(2)}) async-start(), calls=%async_computation.31 | async-start | bytes 1351680
  1381.6 313.3 %reduce-scatter.34.cloned.1.call-start = ((), (), s32[]{:S(2)}) async-start(), calls=%async_computation.32 | async-start | bytes 2457600
  1391.6 15.6 all-to-all-start
  1398.5 298.6 %reduce-scatter.28.cloned.1.call-start = ((), (), s32[]{:S(2)}) async-start(), calls=%async_computation.29 | async-start | bytes 2457600
  1414.0 285.4 %reduce-scatter.30.cloned.1.call-start = ((), (), s32[]{:S(2)}) async-start(), calls=%async_computation.30 | async-start | bytes 2457600
  1415.8 6.8 collective-permute-start.3
  1448.7 28.1 %all-to-all-start.3 = ((bf16[128,8,960]{0,2,1:T(8,128)(2,1)}), bf16[128,8,960]{0,2,1:T(8,128)(2,1)S(1)}, u32[]{:S(2)}, u32[]{:S(2)}) async-start(bf16[128,8,960]{0,2,1:T(8,128)(2,1)} %bitcast.139), calls=%async_computation.5 | async-start | bytes 3932160 | tf_op jit(solution)/shard_map/all_to_all | solution.py:259
  1453.0 287.1 %reduce-scatter.36.cloned.1.call-start = ((), (), s32[]{:S(2)}) async-start(), calls=%async_computation.33 | async-start | bytes 6553600
  1494.1 342.5 %reduce-scatter.38.cloned.1.call-start = ((), (), s32[]{:S(2)}) async-start(), calls=%async_computation.34 | async-start | bytes 6553600
  1551.5 26.6 %all-to-all-start.5 = ((bf16[128,8,960]{0,2,1:T(8,128)(2,1)}), bf16[128,8,960]{0,2,1:T(8,128)(2,1)}, u32[]{:S(2)}, u32[]{:S(2)}) async-start(bf16[128,8,960]{0,2,1:T(8,128)(2,1)} %bitcast.140), calls=%async_computation.7 | async-start | bytes 3932160 | tf_op jit(solution)/shard_map/all_to_all | solution.py:261
  1556.3 377.0 %reduce-scatter.40.cloned.1.call-start = ((), (), s32[]{:S(2)}) async-start(), calls=%async_computation.35 | async-start | bytes 6553600
  1595.7 473.3 %reduce-scatter.24.cloned.1.call-start = ((), (), s32[]{:S(2)}) async-start(), calls=%async_computation.24 | async-start | bytes 2703360 | tf_op jit(solution)/shard_map/reduce_scatter | solution.py:311
  1598.9 606.6 %reduce-scatter.26.cloned.1.call-start = ((), (), s32[]{:S(2)}) async-start(), calls=%async_computation.25 | async-start | bytes 2703360 | tf_op jit(solution)/shard_map/reduce_scatter | solution.py:313
  (140 other events, 2050.7 us)
Sparse Core Ops, SparseCore 0:
  10.9 101.8 all-gather.15
  115.6 52.4 all-gather.17
  171.1 53.2 all-gather.19
  227.0 97.4 all-gather.13
  327.2 97.2 all-gather.21
  427.2 220.6 all-gather.23
  650.8 220.6 all-gather.25
  874.4 220.6 all-gather.27
  1097.6 39.2 all-gather.31
  1138.7 41.1 all-gather.29
  1182.3 41.1 all-gather.33
  1225.8 41.1 all-gather.35
  1381.7 130.8 reduce-scatter.31
  1514.9 42.5 reduce-scatter.33
  1559.8 40.6 reduce-scatter.27
  1602.8 40.6 reduce-scatter.29
  1645.8 94.2 reduce-scatter.35
  1742.3 94.2 reduce-scatter.37
  1839.0 94.2 reduce-scatter.39
  1936.1 132.7 reduce-scatter.23
  2071.9 133.5 reduce-scatter.25
where the time goes:
time: 2240 us; the launch traced here: 2210 us
  waiting for transfers between devices  1300 us (58%)
  local copies, waits for them, and re-layouts  320 us (14%)
  matrix products  229 us (10%)
  blocking collectives  179 us (8%)
  other arithmetic  93.9 us (4%)
  starting transfers between devices  76 us (3%)
    unnamed x28, waiting for transfers between devices  230 us
    all_gather x1, waiting for transfers between devices, per_device(): lax.all_gather(mlp_up_w, ('dp', 'context'), axis=0, tiled=True)  205 us
    all_gather x1, waiting for transfers between devices, per_device(): lax.all_gather(mlp_down_w, ('dp', 'context'), axis=0, tiled=True)  205 us
    all_gather x1, waiting for transfers between devices, per_device(): lax.all_gather(mlp_gate_w, ('dp', 'context'), axis=0, tiled=True)  189 us
    reduce_scatter x1, waiting for transfers between devices, per_device(): lax.psum_scatter(grad_input_w, ('dp', 'context'), scatter_dimension=0, ti...  137 us
    reduce_scatter x1, waiting for transfers between devices, per_device(): lax.psum_scatter(grad_recur_w, ('dp', 'context'), scatter_dimension=0, ti...  132 us
    unnamed x2, blocking collectives  92 us
    slice x49, local copies, waits for them, and re-layouts, per_device(): lax.associative_scan(combine_pair, (next_decay, state_grad), reverse=True...  83.8 us
  transfers between devices with their start and end apart: 41, of which 32 were waited for; matrix products, arithmetic and copies ran while one was open for 28% of the time, Pallas kernels for 0%

commit v1 on v0

v1 whole, which is shorter than its diff:
```python
import functools

import jax
import jax.numpy as jnp
from jax import lax
from jax.experimental import pallas as pl
from jax.experimental.pallas import tpu as pltpu
from jax.sharding import Mesh
from jax.sharding import PartitionSpec as P

HEADS = 10
CONV = 4
CHUNK = 256
BF = jnp.bfloat16
F32 = jnp.float32
DP = ("hi", "lo")
CTX = ("cxy", "core")
CUBE = ("lo", "cxy", "core")
EVERY = ("hi", "lo", "cxy", "core")
SWAP = [(0, 1), (1, 0)]


def dot(a, b, ca, cb):
    return lax.dot_general(a, b, (((ca,), (cb,)), ((), ())), preferred_element_type=F32)


def rms_back(values, gain, grad):
    r = lax.rsqrt(jnp.mean(values * values, axis=-1, keepdims=True) + 1e-06)
    q = grad * gain
    gain_grad = jnp.sum(grad * values * r, axis=0)
    value_grad = r * q - r * r * r * values * jnp.mean(q * values, axis=-1, keepdims=True)
    return value_grad, gain_grad


def gelu_parts(x):
    c0 = 0.7978845608028654
    c1 = 0.044715
    x2 = x * x
    th = jnp.tanh(c0 * x * (1.0 + c1 * x2))
    half = 0.5 * (1.0 + th)
    slope = half + 0.5 * x * (1.0 - th * th) * c0 * (1.0 + 3.0 * c1 * x2)
    return x * half, slope


def minus_expm1(x):
    series = 1.0 + x * (1.0 / 8.0)
    for n in range(7, 1, -1):
        series = 1.0 + x * (1.0 / n) * series
    return jnp.where(x > -0.5, -x * series, 1.0 - jnp.exp(x))


def forward_kernel(
    lin_ref, gpre_ref, meta_ref, vec_ref, rw_ref, iw_ref,
    mixed_ref, prev_ref, conv_ref, rec_ref, inp_ref,
    xbuf, dec_s, drv_s, st_s, carry,
):
    rows = lin_ref.shape[0]
    first = pl.program_id(1) == 0

    @pl.when(first)
    def _():
        xbuf[0:8, :] = jnp.zeros((8, xbuf.shape[1]), F32)
        carry[...] = jnp.zeros_like(carry)

    x = lin_ref[...].astype(F32)
    xbuf[8 : 8 + rows, :] = x
    conv = vec_ref[4:5, :] + vec_ref[0:1, :] * x
    for k in range(1, CONV):
        conv = conv + vec_ref[k : k + 1, :] * (xbuf[8 - k : 8 - k + rows, :] * meta_ref[:, k : k + 1])
    xbuf[0:8, :] = x[rows - 8 : rows, :]
    low = conv.astype(BF)
    rec = jax.nn.sigmoid(jnp.dot(low, rw_ref[...], preferred_element_type=F32) + vec_ref[5:6, :])
    inp = jax.nn.sigmoid(jnp.dot(low, iw_ref[...], preferred_element_type=F32) + vec_ref[6:7, :])
    reset = meta_ref[:, 0:1] > 0.5
    log_decay = vec_ref[7:8, :] * rec
    scale = jnp.where(reset, 1.0, jnp.sqrt(minus_expm1(2.0 * log_decay)))
    dec_s[...] = jnp.where(reset, 0.0, jnp.exp(log_decay))
    drv_s[...] = scale * inp * conv
    conv_ref[...] = conv
    rec_ref[...] = rec
    inp_ref[...] = inp
    width = carry.shape[1]
    row = lax.broadcasted_iota(jnp.int32, (8, width), 0)

    def step(i, held):
        at = pl.multiple_of(i * 8, 8)
        a = dec_s[pl.ds(at, 8), :]
        b = drv_s[pl.ds(at, 8), :]
        for s in (1, 2, 4):
            keep = row >= s
            b = a * jnp.where(keep, pltpu.roll(b, s, 0), 0.0) + b
            a = a * jnp.where(keep, pltpu.roll(a, s, 0), 1.0)
        h = a * held + b
        st_s[pl.ds(at, 8), :] = h
        prev_ref[pl.ds(at, 8), :] = jnp.where(row == 0, held, pltpu.roll(h, 1, 0))
        return jnp.broadcast_to(h[7:8, :], (8, width))

    carry[...] = lax.fori_loop(0, rows // 8, step, carry[...], unroll=4)
    gel, _ = gelu_parts(gpre_ref[...])
    mixed_ref[...] = (gel * st_s[...] * vec_ref[8:9, :]).astype(BF)


def backward_kernel(
    mg_ref, gpre_ref, conv_ref, rec_ref, inp_ref, prev_ref, lin_ref, meta_ref, vec_ref, rw_ref, iw_ref,
    glow_ref, llow_ref, rwg_ref, iwg_ref, sum_ref,
    dec_s, sg_s, lam_s, gbuf, carry,
):
    rows = lin_ref.shape[0]
    first = pl.program_id(1) == 0

    @pl.when(first)
    def _():
        carry[...] = jnp.zeros_like(carry)
        for k in range(CONV - 1):
            gbuf[k, rows : rows + 8, :] = jnp.zeros((8, gbuf.shape[2]), F32)
        rwg_ref[...] = jnp.zeros_like(rwg_ref)
        iwg_ref[...] = jnp.zeros_like(iwg_ref)
        sum_ref[...] = jnp.zeros_like(sum_ref)

    mg = mg_ref[...]
    conv = conv_ref[...]
    rec = rec_ref[...]
    inp = inp_ref[...]
    prev = prev_ref[...]
    own = vec_ref[8:9, :]
    gel, slope = gelu_parts(gpre_ref[...])
    reset = meta_ref[:, 0:1] > 0.5
    log_decay = vec_ref[7:8, :] * rec
    scale = jnp.where(reset, 1.0, jnp.sqrt(minus_expm1(2.0 * log_decay)))
    dec = jnp.where(reset, 0.0, jnp.exp(log_decay))
    gated = scale * inp
    states = dec * prev + gated * conv
    glow_ref[...] = (mg * states * slope * own).astype(BF)
    dec_s[...] = dec
    sg_s[...] = mg * gel
    width = carry.shape[1]
    row = lax.broadcasted_iota(jnp.int32, (8, width), 0)
    blocks = rows // 8

    def step(i, held):
        at = pl.multiple_of((blocks - 1 - i) * 8, 8)
        a = dec_s[pl.ds(at, 8), :]
        g = sg_s[pl.ds(at, 8), :]
        b = a * g
        for s in (1, 2, 4):
            keep = row < 8 - s
            b = a * jnp.where(keep, pltpu.roll(b, 8 - s, 0), 0.0) + b
            a = a * jnp.where(keep, pltpu.roll(a, 8 - s, 0), 1.0)
        m = a * held + b
        lam_s[pl.ds(at, 8), :] = g + jnp.where(row == 7, held, pltpu.roll(m, 7, 0))
        return jnp.broadcast_to(m[0:1, :], (8, width))

    carry[...] = lax.fori_loop(0, blocks, step, carry[...], unroll=4)
    lam = lam_s[...]
    conv_gate = lam * gated
    dinp = lam * scale * conv
    dscale = lam * inp * conv
    dlog = jnp.where(reset, 0.0, (lam * prev - dscale * dec / scale) * dec)
    recur_grad = vec_ref[7:8, :] * dlog * rec * (1.0 - rec)
    input_grad = dinp * inp * (1.0 - inp)
    rlow = recur_grad.astype(BF)
    ilow = input_grad.astype(BF)
    low = conv.astype(BF)
    rwg_ref[...] += dot(low, rlow, 0, 0)
    iwg_ref[...] += dot(low, ilow, 0, 0)
    conv_grad = conv_gate + dot(rlow, rw_ref[...], 1, 1) + dot(ilow, iw_ref[...], 1, 1)
    lin = lin_ref[...].astype(F32)
    linear_grad = vec_ref[0:1, :] * conv_grad

    def add(at, value):
        sum_ref[at : at + 1, :] += jnp.sum(value, axis=0, keepdims=True)

    add(0, conv_grad * lin)
    for k in range(1, CONV):
        masked = conv_grad * meta_ref[:, k : k + 1]
        gbuf[k - 1, 0:rows, :] = masked
        moved = gbuf[k - 1, k : k + rows, :]
        gbuf[k - 1, rows : rows + 8, :] = masked[0:8, :]
        linear_grad = linear_grad + vec_ref[k : k + 1, :] * moved
        add(k, moved * lin)
    llow_ref[...] = (linear_grad * own).astype(BF)
    add(4, conv_grad)
    add(5, recur_grad)
    add(6, input_grad)
    add(7, vec_ref[9:10, :] * rec * dlog)


def forward_call(lin, gpre, meta, vecs, rw, iw):
    tokens, win = lin.shape
    bw = rw.shape[1]
    rows = min(CHUNK, tokens)
    grid = (win // bw, tokens // rows)
    tok = pl.BlockSpec((rows, bw), lambda h, j: (j, h))
    mspec = pl.BlockSpec((rows, meta.shape[1]), lambda h, j: (j, 0))
    vspec = pl.BlockSpec((vecs.shape[0], bw), lambda h, j: (0, h))
    wspec = pl.BlockSpec((bw, bw), lambda h, j: (h, 0))
    full = jax.ShapeDtypeStruct((tokens, win), F32)
    return pl.pallas_call(
        forward_kernel,
        grid=grid,
        in_specs=[tok, tok, mspec, vspec, wspec, wspec],
        out_specs=[tok] * 5,
        out_shape=[jax.ShapeDtypeStruct((tokens, win), BF), full, full, full, full],
        scratch_shapes=[
            pltpu.VMEM((rows + 8, bw), F32),
            pltpu.VMEM((rows, bw), F32),
            pltpu.VMEM((rows, bw), F32),
            pltpu.VMEM((rows, bw), F32),
            pltpu.VMEM((8, bw), F32),
        ],
        compiler_params=pltpu.CompilerParams(vmem_limit_bytes=40 << 20),
        cost_estimate=pl.CostEstimate(
            flops=tokens * win * (4 * bw + 100), bytes_accessed=tokens * win * 24, transcendentals=tokens * win * 6
        ),
        name="recur_forward",
    )(lin, gpre, meta, vecs, rw, iw)


def backward_call(mg, gpre, conv, rec, inp, prev, lin, meta, vecs, rw, iw):
    tokens, win = lin.shape
    bw = rw.shape[1]
    rows = min(CHUNK, tokens)
    steps = tokens // rows
    grid = (win // bw, steps)
    tok = pl.BlockSpec((rows, bw), lambda h, j: (steps - 1 - j, h))
    mspec = pl.BlockSpec((rows, meta.shape[1]), lambda h, j: (steps - 1 - j, 0))
    vspec = pl.BlockSpec((vecs.shape[0], bw), lambda h, j: (0, h))
    wspec = pl.BlockSpec((bw, bw), lambda h, j: (h, 0))
    sspec = pl.BlockSpec((8, bw), lambda h, j: (0, h))
    lows = jax.ShapeDtypeStruct((tokens, win), BF)
    wgrad = jax.ShapeDtypeStruct((win, bw), F32)
    return pl.pallas_call(
        backward_kernel,
        grid=grid,
        in_specs=[tok] * 7 + [mspec, vspec, wspec, wspec],
        out_specs=[tok, tok, wspec, wspec, sspec],
        out_shape=[lows, lows, wgrad, wgrad, jax.ShapeDtypeStruct((8, win), F32)],
        scratch_shapes=[
            pltpu.VMEM((rows, bw), F32),
            pltpu.VMEM((rows, bw), F32),
            pltpu.VMEM((rows, bw), F32),
            pltpu.VMEM((CONV - 1, rows + 8, bw), F32),
            pltpu.VMEM((8, bw), F32),
        ],
        compiler_params=pltpu.CompilerParams(vmem_limit_bytes=40 << 20),
        cost_estimate=pl.CostEstimate(
            flops=tokens * win * (8 * bw + 150), bytes_accessed=tokens * win * 30, transcendentals=tokens * win * 6
        ),
        name="recur_backward",
    )(mg, gpre, conv, rec, inp, prev, lin, meta, vecs, rw, iw)


def exchange(value, axes):
    return lax.all_to_all(value, axes, split_axis=0, concat_axis=0, tiled=True)


def in_order(flag, mine, other, axis):
    return jnp.where(
        flag == 0, jnp.concatenate([mine, other], axis=axis), jnp.concatenate([other, mine], axis=axis)
    )


def gather_rows(rows, axes):
    count = lax.axis_size(axes)
    mine = exchange(jnp.broadcast_to(rows[None], (count,) + rows.shape), axes)
    other = lax.ppermute(mine, "core", SWAP)
    both = in_order(lax.axis_index("core"), mine[:, None], other[:, None], 1)
    return both.reshape((-1,) + rows.shape[1:])


def scatter_sum(partial, axes, tok):
    core = lax.axis_index("core")
    blocks = partial.reshape((-1, 2, tok) + partial.shape[1:])
    mine = lax.dynamic_index_in_dim(blocks, core, 1, keepdims=False)
    away = lax.dynamic_index_in_dim(blocks, 1 - core, 1, keepdims=False)
    got = lax.ppermute(away, "core", SWAP)
    pair = (mine.astype(F32) + got.astype(F32)).astype(BF)
    return jnp.sum(exchange(pair, axes).astype(F32), axis=0)


def pad_last(value, width):
    extra = width - value.shape[-1]
    return value if extra == 0 else jnp.pad(value, [(0, 0)] * (value.ndim - 1) + [(0, extra)])


def per_device(
    inputs, segment_ids, first_gain, gelu_in_w, linear_in_w, conv_weight, conv_bias, recur_gate_w, recur_gate_b,
    input_gate_w, input_gate_b, decay_param, out_proj_w, second_gain, mlp_gate_w, mlp_up_w, mlp_down_w, out_grad,
):
    n_hi, n_lo, n_cx, n_core = (lax.axis_size(a) for a in EVERY)
    hi, lo, cx, core = (lax.axis_index(a) for a in EVERY)
    n_ctx = n_cx * n_core
    n_dp = n_hi * n_lo
    n_dev = n_dp * n_ctx
    ctx = cx * n_core + core
    tok, width = inputs.shape
    tokens = segment_ids.shape[1]
    chans = linear_in_w.shape[1]
    bw = recur_gate_w.shape[1]
    hidden_units = mlp_gate_w.shape[1]
    own_ch = chans // n_ctx
    starts = [own_ch * c // bw for c in range(n_ctx)]
    span = max((own_ch * (c + 1) - 1) // bw - starts[c] + 1 for c in range(n_ctx))
    starts = [min(s, HEADS - span) for s in starts]
    win = span * bw
    head0 = jnp.array(starts, jnp.int32)[ctx]
    ch0 = head0 * bw
    own_off = own_ch * ctx - ch0
    ff_own = hidden_units // (n_lo * n_ctx)
    ff_pad = -(-ff_own // 128) * 128

    piece = width // n_dev
    small = jnp.concatenate(
        [v[None] for v in (first_gain, second_gain)]
        + [conv_weight]
        + [v[None] for v in (conv_bias, recur_gate_b, input_gate_b, decay_param)],
        axis=0,
    )
    small_all = exchange(jnp.broadcast_to(small[None], (n_dev,) + small.shape), EVERY)
    small_all = small_all.transpose(1, 0, 2).reshape(small.shape[0], width).astype(F32)
    gain_first = small_all[0]
    gain_second = small_all[1]

    windows = [
        jnp.concatenate(
            [gelu_in_w[:, s * bw : s * bw + win], linear_in_w[:, s * bw : s * bw + win]], axis=1
        )
        for s in starts
    ]
    gl_part = exchange(jnp.stack(windows), CTX).reshape(-1, 2 * win)
    gl_w = lax.all_gather(gl_part, DP, axis=0, tiled=True)
    gates_all = lax.all_gather(jnp.concatenate([recur_gate_w, input_gate_w], axis=1), EVERY, axis=0, tiled=True)
    gates_win = lax.dynamic_slice_in_dim(gates_all, ch0, win)
    recur_w = gates_win[:, :bw]
    input_w = gates_win[:, bw:]
    proj_all = lax.all_gather(out_proj_w, EVERY, axis=0, tiled=True)
    proj_w = lax.dynamic_slice_in_dim(proj_all, ch0, win)

    r_first = lax.rsqrt(jnp.mean(inputs * inputs, axis=-1, keepdims=True) + 1e-06)
    normed = (inputs * r_first * gain_first).astype(BF)
    normed_all = gather_rows(normed, "cxy")

    down_grad = lax.all_gather(out_grad.astype(BF), CUBE, axis=0, tiled=True)

    def columns(weight):
        parts = weight.reshape(weight.shape[0], n_ctx, n_lo, ff_own).transpose(2, 1, 0, 3)
        return pad_last(parts.reshape(n_lo * n_ctx, weight.shape[0], ff_own), ff_pad)

    gu_send = jnp.concatenate([columns(mlp_gate_w), columns(mlp_up_w)], axis=2)
    gu_mine = exchange(gu_send, CUBE).reshape(-1, 2 * ff_pad)
    gu_other = lax.ppermute(gu_mine, "hi", SWAP)
    gu_w = in_order(hi, gu_mine, gu_other, 0)
    down_other = lax.ppermute(mlp_down_w, "hi", SWAP)
    n_cube = n_lo * n_ctx
    half = n_cube // 2
    to_a, to_b = [], []
    for q in range(n_cube):
        lower, upper = q // 2, q // 2 + half
        near, far = (lower, upper) if q % 2 == 0 else (upper, lower)
        place = lambda t: (t % n_lo) * n_ctx + t // n_lo
        to_a.append((q, place(near)))
        to_b.append((q, place(far)))
    odd = core
    same = hi == odd
    down_a = lax.ppermute(jnp.where(same, mlp_down_w, down_other), CUBE, to_a)
    down_b = lax.ppermute(jnp.where(same, down_other, mlp_down_w), CUBE, to_b)
    slot = ctx * n_lo + lo
    down_w = in_order((slot >= half).astype(jnp.int32), down_a, down_b, 0)
    down_w = jnp.pad(down_w, ((0, ff_pad - ff_own), (0, 0)))

    ids = segment_ids[0]
    metas = [jnp.concatenate([jnp.ones((1,), F32), (ids[1:] != ids[:-1]).astype(F32)])]
    for k in range(1, CONV):
        metas.append(jnp.concatenate([jnp.zeros((k,), F32), (ids[k:] == ids[:-k]).astype(F32)]))
    meta = jnp.stack(metas, axis=1)
    vec_win = lax.dynamic_slice_in_dim(small_all[2:], ch0, win, axis=1)
    decay_win = vec_win[7:8]
    place_in = jnp.arange(win) - own_off
    own_mask = ((place_in >= 0) & (place_in < own_ch)).astype(F32)[None]
    vecs = jnp.concatenate(
        [
            vec_win[:7],
            -8.0 * jax.nn.softplus(decay_win),
            own_mask,
            -8.0 * jax.nn.sigmoid(decay_win),
            jnp.zeros((6, win), F32),
        ],
        axis=0,
    )
    gelu_pre = dot(normed_all, gl_w[:, :win], 1, 0)
    linear_out = dot(normed_all, gl_w[:, win:], 1, 0).astype(BF)
    mixed, prev, conv_out, rec, inp = forward_call(linear_out, gelu_pre, meta, vecs, recur_w, input_w)
    proj_part = dot(mixed, proj_w, 1, 0).astype(BF)
    hidden = inputs + scatter_sum(proj_part, "cxy", tok)
    mixed_own = lax.dynamic_slice_in_dim(mixed, own_off, own_ch, axis=1)
    mixed_all = lax.all_gather(mixed_own, CTX, axis=0, tiled=False)

    r_second = lax.rsqrt(jnp.mean(hidden * hidden, axis=-1, keepdims=True) + 1e-06)
    second = (hidden * r_second * gain_second).astype(BF)
    second_all = gather_rows(second, ("lo", "cxy"))
    pre = dot(second_all, gu_w, 1, 0)
    gate_pre, up_pre = pre[:, :ff_pad], pre[:, ff_pad:]
    act_grad = dot(down_grad, down_w, 1, 1)
    gel, slope = gelu_parts(gate_pre)
    activation = (gel * up_pre).astype(BF)
    gu_low = jnp.concatenate([(act_grad * up_pre * slope).astype(BF), (act_grad * gel).astype(BF)], axis=1)
    second_part = dot(gu_low, gu_w, 1, 1).astype(BF)
    second_grad = scatter_sum(second_part, ("lo", "cxy"), tok)
    out_part = dot(activation, down_w, 1, 0).astype(BF)
    output = hidden + lax.psum_scatter(out_part, CUBE, scatter_dimension=0, tiled=True).astype(F32)

    grad_gu = dot(second_all, gu_low, 0, 0).astype(BF)
    grad_down = dot(activation, down_grad, 0, 0).astype(BF)

    def settle(partial, axis):
        size = partial.shape[axis] // n_hi
        mine = lax.dynamic_slice_in_dim(partial, hi * size, size, axis)
        away = lax.dynamic_slice_in_dim(partial, (1 - hi) * size, size, axis)
        both = (mine.astype(F32) + lax.ppermute(away, "hi", SWAP).astype(F32)).astype(BF)
        if n_lo == 1:
            return both, None
        size = size // n_lo
        mine = lax.dynamic_slice_in_dim(both, lo * size, size, axis)
        away = lax.dynamic_slice_in_dim(both, (1 - lo) * size, size, axis)
        return mine, lax.ppermute(away, "lo", SWAP)

    gu_a, gu_b = settle(grad_gu, 0)
    dn_a, dn_b = settle(grad_down, 1)
    grad_gate = in_order(lo, gu_a[:, :ff_own], gu_b[:, :ff_own], 1).astype(F32)
    grad_up = in_order(
        lo, gu_a[:, ff_pad : ff_pad + ff_own], gu_b[:, ff_pad : ff_pad + ff_own], 1
    ).astype(F32)
    grad_dn = in_order(lo, dn_a[:ff_own], dn_b[:ff_own], 0).astype(F32)

    hidden_part, grad_gain_two = rms_back(hidden, gain_second, second_grad)
    hidden_grad = out_grad + hidden_part
    branch = hidden_grad.astype(BF)
    branch_all = gather_rows(branch, "cxy")

    mixed_grad = dot(branch_all, proj_w, 1, 1)
    gelu_low, linear_low, recur_wg, input_wg, sums = backward_call(
        mixed_grad, gelu_pre, conv_out, rec, inp, prev, linear_out, meta, vecs, recur_w, input_w
    )
    branch_cols = lax.dynamic_slice_in_dim(branch_all, ctx * (width // n_ctx), width // n_ctx, axis=1)
    grad_proj = jnp.einsum("ctr,td->crd", mixed_all, branch_cols, preferred_element_type=F32)
    grad_proj = grad_proj.reshape(chans, width // n_ctx).astype(BF)
    grad_proj = lax.psum_scatter(grad_proj, DP, scatter_dimension=0, tiled=True).astype(F32)
    lows = jnp.concatenate([gelu_low, linear_low], axis=1)
    own_lows = jnp.concatenate(
        [
            lax.dynamic_slice_in_dim(gelu_low, own_off, own_ch, axis=1),
            lax.dynamic_slice_in_dim(linear_low, own_off, own_ch, axis=1),
        ],
        axis=1,
    )
    grad_gl = dot(normed_all, own_lows, 0, 0).astype(BF)
    grad_gl = lax.psum_scatter(grad_gl, DP, scatter_dimension=0, tiled=True).astype(F32)
    first_part = dot(lows, gl_w, 1, 1).astype(BF)
    first_grad = scatter_sum(first_part, "cxy", tok)
    input_part, grad_gain_one = rms_back(inputs, gain_first, first_grad)
    input_grad = hidden_grad + input_part

    packed = jnp.concatenate([recur_wg, input_wg, pad_last(sums.T, 128)], axis=1)
    packed = lax.dynamic_slice_in_dim(packed, own_off, own_ch, axis=0)
    packed = jnp.sum(exchange(packed.reshape(n_dp, own_ch // n_dp, packed.shape[1]), DP), axis=0)
    routes = [(d * n_ctx + c, c * n_dp + d) for d in range(n_dp) for c in range(n_ctx)]
    packed = lax.ppermute(packed, EVERY, routes)
    grad_recur_w = packed[:, :bw]
    grad_input_w = packed[:, bw : 2 * bw]
    rest = packed[:, 2 * bw : 2 * bw + 8].T
    gains = jnp.stack([grad_gain_one, grad_gain_two]).reshape(2, n_dev, piece).transpose(1, 0, 2)
    gains = jnp.sum(exchange(gains, EVERY), axis=0)

    return (
        output,
        input_grad,
        gains[0],
        grad_gl[:, :own_ch],
        grad_gl[:, own_ch:],
        rest[:CONV],
        rest[4],
        grad_recur_w,
        rest[5],
        grad_input_w,
        rest[6],
        rest[7],
        grad_proj,
        gains[1],
        grad_gate,
        grad_up,
        grad_dn,
    )


def solution(mesh):
    n_dp = mesh.shape["dp"]
    n_ctx = mesh.shape["context"]
    inner = Mesh(mesh.devices.reshape(2, n_dp // 2, n_ctx // 2, 2), EVERY)
    rows = P(EVERY, None)
    vec = P(EVERY)
    return jax.shard_map(
        per_device,
        mesh=inner,
        in_specs=(
            rows, P(DP, None), vec, rows, rows, P(None, EVERY), vec, rows, vec, rows, vec, vec, rows, vec,
            rows, rows, rows, rows,
        ),
        out_specs=(
            rows, rows, vec, P(DP, CTX), P(DP, CTX), P(None, EVERY), vec, rows, vec, rows, vec, vec,
            P(DP, CTX), vec, P(DP, CTX), P(DP, CTX), P(CTX, DP),
        ),
        check_vma=False,
    )
```

time: 2240 us -> 1280 us (0.57); the launches traced: 2210 us -> 1280 us
  waiting for transfers between devices: 1300 us -> 803 us
  local copies, waits for them, and re-layouts: 320 us -> 89.6 us
  blocking collectives: 179 us -> 61.7 us
  matrix products: 229 us -> 136 us
  Pallas kernels: 0 us -> 29.9 us
    all_gather x12 -> x5, waiting for transfers between devices: 714 us -> 149 us  [the longest x1 74.5 us: per_device(): gl_w = lax.all_gather(gl_part, DP, axis=0, tiled=True)]
    ppermute x16 -> x15, waiting for transfers between devices: 30.1 us -> 349 us  [the longest x2 126 us: settle(): lax.ppermute(away, 'hi', SWAP).astype(F32)]
    unnamed x28 -> x9, waiting for transfers between devices: 230 us -> 0.8 us
    reduce_scatter x2, waiting for transfers between devices: 268 us -> 65.2 us  [the longest x1 65.2 us: per_device(): lax.psum_scatter(out_part, CUBE, scatter_dimension=0, tiled=True)]
    all_to_all x4 -> x9, waiting for transfers between devices: 54.9 us -> 239 us  [exchange(): return lax.all_to_all(value, axes, split_axis=0, concat_axis=0, tiled=True)]
    slice x96 -> x14, local copies, waits for them, and re-layouts: 153 us -> 10.4 us  [the longest x2 2.26 us: per_device(): grad_dn = in_order(lo, dn_a[:ff_own], dn_b[:ff_own], 0).astype(F32)]
    dot_general x24 -> x13, matrix products: 229 us -> 136 us  [the longest x12 128 us: dot(): lax.dot_general(a, b, (((ca,), (cb,)), ((), ())), preferred_element_type=...]
    unnamed x2 -> x0, blocking collectives: 92 us -> none
  transfers between devices with their start and end apart: 41 -> 32, of which waited for: 32 -> 21; matrix products, arithmetic and copies ran while one was open for 28% -> 18% of each run, Pallas kernels for 0% -> 2%
where the time goes in v1:
time: 1280 us
  waiting for transfers between devices  803 us (63%)
  matrix products  136 us (11%)
  local copies, waits for them, and re-layouts  89.6 us (7%)
  other arithmetic  78.3 us (6%)
  blocking collectives  61.7 us (5%)
  starting transfers between devices  59.5 us (5%)
  Pallas kernels  29.9 us (2%)
  between operations  17.6 us (1%)
    all_to_all x9, waiting for transfers between devices, exchange(): return lax.all_to_all(value, axes, split_axis=0, concat_axis=0, tiled=True)  239 us
    dot_general x12, matrix products, dot(): lax.dot_general(a, b, (((ca,), (cb,)), ((), ())), preferred_element_type=...  128 us
    ppermute x2, waiting for transfers between devices, settle(): lax.ppermute(away, 'hi', SWAP).astype(F32)  126 us
    all_gather x1, waiting for transfers between devices, per_device(): gl_w = lax.all_gather(gl_part, DP, axis=0, tiled=True)  74.5 us
    all_gather x1, waiting for transfers between devices, per_device(): proj_all = lax.all_gather(out_proj_w, EVERY, axis=0, tiled=True)  74.2 us
    ppermute x1, waiting for transfers between devices, per_device(): gu_other = lax.ppermute(gu_mine, 'hi', SWAP)  72.3 us
    ppermute x1, waiting for transfers between devices, per_device(): down_other = lax.ppermute(mlp_down_w, 'hi', SWAP)  71.3 us
    reduce_scatter x1, waiting for transfers between devices, per_device(): lax.psum_scatter(out_part, CUBE, scatter_dimension=0, tiled=True)  65.2 us
  transfers between devices with their start and end apart: 32, of which 21 were waited for; matrix products, arithmetic and copies ran while one was open for 18% of the time, Pallas kernels for 2%

profile of v1, /device:TPU:1, one launch (start us, length us, event | category | flops | bytes accessed | tf_op | source)
XLA Modules:
  0.0 1275.8 jit_solution(17144779911034086736)
XLA Ops:
  11.4 22.7 %all_to_all.55 = bf16[8,80,1024]{2,1,0:T(8,128)(2,1)} all-to-all(bf16[8,80,1024]{2,1,0:T(8,128)(2,1)S(1)} %fusion.45), channel_id=1, replica_groups=mesh['hi'=2,'lo'=2,'cxy'=4,'core'=2] {'cxy','core'}, dimensions={0} | all-to-all | bytes 2621440 | tf_op jit(solution)/shard_map/all_to_all | solution.py:254
  49.7 39.0 %all_to_all.56 = bf16[4,128,2560]{2,1,0:T(8,128)(2,1)} all-to-all(bf16[4,128,2560]{2,1,0:T(8,128)(2,1)S(1)} %broadcast_in_dim.77), channel_id=1, replica_groups=mesh['hi'=2,'lo'=2,'cxy'=4,'core'=2] {'cxy'}, dimensions={0} | all-to-all | bytes 5242880 | tf_op jit(solution)/shard_map/all_to_all | solution.py:254
  104.1 74.5 %all-gather.7.cloned.1.call-done = bf16[2560,1024]{1,0:T(8,128)(2,1)} async-done(((bf16[640,1024]{1,0:T(8,128)(2,1)}), bf16[2560,1024]{1,0:T(8,128)(2,1)}) %all-gather.7.cloned.1.call-update) | async-done | bytes 5242896 | tf_op jit(solution)/shard_map/all_gather | solution.py:331
  187.9 10.3 recur_forward.1
  204.5 74.2 %all-gather.11.cloned.1.call-done = bf16[2560,2560]{1,0:T(8,128)(2,1)} async-done(((bf16[80,2560]{1,0:T(8,128)(2,1)}), bf16[2560,2560]{1,0:T(8,128)(2,1)}) %all-gather.11.cloned.1.call-update) | async-done | bytes 13107216 | tf_op jit(solution)/shard_map/all_gather | solution.py:336
  301.1 30.4 %all-to-all-done.3 = bf16[4,128,2560]{2,1,0:T(8,128)(2,1)} async-done(((bf16[4,128,2560]{2,1,0:T(8,128)(2,1)}), bf16[4,128,2560]{2,1,0:T(8,128)(2,1)}, u32[]{:S(2)}, u32[]{:S(2)}) %all-to-all-start.3) | async-done | bytes 2621472 | tf_op jit(solution)/shard_map/all_to_all | solution.py:254
  358.1 68.6 %all-to-all-done.4 = bf16[8,128,2560]{2,1,0:T(8,128)(2,1)} async-done(((bf16[8,128,2560]{2,1,0:T(8,128)(2,1)}), bf16[8,128,2560]{2,1,0:T(8,128)(2,1)}, u32[]{:S(2)}, u32[]{:S(2)}) %all-to-all-start.4) | async-done | bytes 5242912 | tf_op jit(solution)/shard_map/all_to_all | solution.py:254
  426.7 8.3 all-to-all-start.5
  435.5 71.3 %collective-permute-done.4 = bf16[240,2560]{1,0:T(8,128)(2,1)} collective-permute-done((bf16[240,2560]{1,0:T(8,128)(2,1)S(1)}, bf16[240,2560]{1,0:T(8,128)(2,1)}, u32[]{:S(2)}, u32[]{:S(2)}) %collective-permute-start.4) | collective-permute-done | bytes 1228832 | tf_op jit(solution)/shard_map/ppermute | solution.py:353
  516.3 24.2 %collective-permute-done.5 = bf16[240,2560]{1,0:T(8,128)(2,1)S(1)} collective-permute-done((bf16[240,2560]{1,0:T(8,128)(2,1)}, bf16[240,2560]{1,0:T(8,128)(2,1)S(1)}, u32[]{:S(2)}, u32[]{:S(2)}) %collective-permute-start.5) | collective-permute-done | bytes 1228832 | tf_op jit(solution)/shard_map/ppermute | solution.py:365
  544.5 12.8 %maximum_select_fusion = bf16[8,2,128,2560]{3,2,1,0:T(8,128)(2,1)} fusion(bf16[8,1,128,2560]{3,2,1,0:T(8,128)(2,1)} %bitcast.24, bf16[8,1,128,2560]{3,2,1,0:T(8,128)(2,1)} %bitcast.23, pred[]{:T(512)S(6)} %eq.31), kind=kLoop, calls=%fused_computation.2 | loop fusion | flops 15728640 | bytes 20971520 | tf_op jit(solution)/shard_map/jit(_where)/select_n | solution.py:258
  557.2 72.3 %collective-permute-done.3 = bf16[1280,1024]{1,0:T(8,128)(2,1)} collective-permute-done((bf16[1280,1024]{1,0:T(8,128)(2,1)}, bf16[1280,1024]{1,0:T(8,128)(2,1)}, u32[]{:S(2)}, u32[]{:S(2)}) %collective-permute-start.3) | collective-permute-done | bytes 2621472 | tf_op jit(solution)/shard_map/ppermute | solution.py:351
  629.5 19.1 %fusion.32 = f32[2048,1024]{0,1:T(8,128)} fusion(bf16[2048,2560]{1,0:T(8,128)(2,1)} %bitcast.115, bf16[1280,1024]{1,0:T(8,128)(2,1)} %collective-permute-done.3, bf16[1280,1024]{1,0:T(8,128)(2,1)} %bitcast.30, pred[]{:T(512)S(6)} %eq.35), kind=kOutput, calls=%fused_computation.81 | convolution fusion | flops 10761011200 | bytes 24117248 | tf_op jit(solution)/shard_map/dot_general | solution.py:24
  648.6 14.6 %fusion.6 = (bf16[2048,512]{0,1:T(8,128)(2,1)}, bf16[2048,512]{0,1:T(8,128)(2,1)}, bf16[2048,512]{0,1:T(8,128)(2,1)S(1)}) fusion(f32[2048,1024]{0,1:T(8,128)} %fusion.32, bf16[2048,2560]{1,0:T(8,128)(2,1)} %all-gather.13.cloned.1.call-done, bf16[480,2560]{1,0:T(8,128)(2,1)} %maximum_select_fusion.4), kind=kOutput, calls=%fused_computation.30 | convolution fusion | flops 5393874944 | bytes 27623424 | tf_op jit(solution)/shard_map/dot_general | solution.py:24
  664.5 17.7 %convolution_convert_fusion.1 = bf16[2048,2560]{1,0:T(8,128)(2,1)} fusion(bf16[2048,512]{0,1:T(8,128)(2,1)S(1)} %get-tuple-element.123, bf16[480,2560]{1,0:T(8,128)(2,1)S(1)} %copy-done.34), kind=kOutput, calls=%fused_computation.1 | convolution fusion | flops 5373952000 | bytes 15040512 | tf_op jit(solution)/shard_map/dot_general | solution.py:24
  682.2 18.9 %convolution_convert_fusion = bf16[2048,2560]{1,0:T(8,128)(2,1)} fusion(bf16[2048,512]{0,1:T(8,128)(2,1)} %get-tuple-element.122, bf16[2048,512]{0,1:T(8,128)(2,1)} %get-tuple-element.121, bf16[1280,1024]{1,0:T(8,128)(2,1)} %collective-permute-done.3, bf16[1280,1024]{1,0:T(8,128)(2,1)} %bitcast.30, pred[]{:T(512)S(6)} %eq.35), kind=kOutput, calls=%fused_computation | convolution fusion | flops 10774642688 | bytes 19922944 | tf_op jit(solution)/shard_map/dot_general | solution.py:24
  705.7 8.4 collective-permute-done.7
  728.4 97.6 %all-to-all-done.6 = bf16[8,128,2560]{2,1,0:T(8,128)(2,1)} async-done(((bf16[8,128,2560]{2,1,0:T(8,128)(2,1)}), bf16[8,128,2560]{2,1,0:T(8,128)(2,1)}, u32[]{:S(2)}, u32[]{:S(2)}) %all-to-all-start.6) | async-done | bytes 5242912 | tf_op jit(solution)/shard_map/all_to_all | solution.py:254
  829.9 65.2 %reduce-scatter.6.cloned.1.call-done = bf16[128,2560]{1,0:T(8,128)(2,1)} async-done(((bf16[2048,2560]{1,0:T(8,128)(2,1)}), bf16[128,2560]{1,0:T(8,128)(2,1)}) %reduce-scatter.6.cloned.1.call-update) | async-done | bytes 655376 | tf_op jit(solution)/shard_map/reduce_scatter | solution.py:410
  904.4 9.0 convolution_convert_fusion.6
  915.3 18.5 %all-to-all-done.7 = bf16[4,128,2560]{2,1,0:T(8,128)(2,1)S(1)} async-done(((bf16[4,128,2560]{2,1,0:T(8,128)(2,1)}), bf16[4,128,2560]{2,1,0:T(8,128)(2,1)S(1)}, u32[]{:S(2)}, u32[]{:S(2)}) %all-to-all-start.7) | async-done | bytes 2621472 | tf_op jit(solution)/shard_map/all_to_all | solution.py:254
  933.8 14.9 %convolution_convert_fusion.3 = bf16[2560,1024]{0,1:T(8,128)(2,1)S(1)} fusion(bf16[2048,2560]{1,0:T(8,128)(2,1)} %bitcast.116, bf16[2048,512]{0,1:T(8,128)(2,1)} %get-tuple-element.122, bf16[2048,512]{0,1:T(8,128)(2,1)} %get-tuple-element.121), kind=kOutput, calls=%fused_computation.7 | convolution fusion | flops 10748428288 | bytes 19922944 | tf_op jit(solution)/shard_map/dot_general | solution.py:24
  955.3 13.6 %copy.74 = bf16[4,2,128,2560]{2,1,0,3:T(2,128)(2,1)} copy(bf16[4,2,128,2560]{3,2,0,1:T(8,128)(2,1)} %maximum_select_fusion.3) | data formatting | bytes 10485760 | tf_op jit(solution)/shard_map/jit(_where)/select_n | solution.py:258
  968.9 9.4 select_n.148
  978.3 7.7 convolution_convert_fusion.7
  992.2 19.6 %recur_backward.1 = (bf16[1024,512]{1,0:T(8,128)(2,1)S(1)}, bf16[1024,512]{1,0:T(8,128)(2,1)S(1)}, f32[512,256]{1,0:T(8,128)S(1)}, f32[512,256]{1,0:T(8,128)S(1)}, f32[8,512]{1,0:T(8,128)S(1)}) custom-call(f32[1024,512]{1,0:T(8,128)S(1)} %fusion.17.mg_ref, f32[1024,512]{1,0:T(8,128)S(1)} %copy-done.1, f32[1024,512]{1,0:T(8,128)S(1)} %copy-done.4, ...), custom_call_target="tpu_custom_call" | custom-call | flops 1152385024 | bytes 15728640 | tf_op jit(solution)/shard_map/recur_backward/pallas_call | solution.py:232
  1011.9 8.7 convolution_convert_fusion.4
  1031.1 30.5 %collective-permute-done.13 = bf16[512,1280]{1,0:T(8,128)(2,1)} collective-permute-done((bf16[512,1280]{1,0:T(8,128)(2,1)}, bf16[512,1280]{1,0:T(8,128)(2,1)}, u32[]{:S(2)}, u32[]{:S(2)}) %collective-permute-start.13) | collective-permute-done | bytes 1310752 | tf_op jit(solution)/shard_map/ppermute | solution.py:419
  1070.2 95.7 %collective-permute-done.11 = bf16[1280,1024]{0,1:T(8,128)(2,1)} collective-permute-done((bf16[1280,1024]{0,1:T(8,128)(2,1)}, bf16[1280,1024]{0,1:T(8,128)(2,1)}, u32[]{:S(2)}, u32[]{:S(2)}) %collective-permute-start.11) | collective-permute-done | bytes 2621472 | tf_op jit(solution)/shard_map/ppermute | solution.py:419
  1174.8 12.7 all-to-all-done.10
  1197.5 28.1 %collective-permute-done.12 = bf16[640,1024]{0,1:T(8,128)(2,1)} collective-permute-done((bf16[640,1024]{0,1:T(8,128)(2,1)}, bf16[640,1024]{0,1:T(8,128)(2,1)}, u32[]{:S(2)}, u32[]{:S(2)}) %collective-permute-start.12) | collective-permute-done | bytes 1310752 | tf_op jit(solution)/shard_map/ppermute | solution.py:425
  1234.9 10.5 collective-permute-done.10
  (282 shorter events, 229.2 us)
Async XLA Ops:
  8.0 94.9 %all-gather.9.cloned.1.call-start = ((), (), s32[]{:S(2)}) async-start(), calls=%async_computation.15 | async-start | bytes 2703360 | tf_op jit(solution)/shard_map/all_gather | solution.py:332
  9.5 169.1 %all-gather.7.cloned.1.call-start = ((), (), s32[]{:S(2)}) async-start(), calls=%async_computation.14 | async-start | bytes 6553600 | tf_op jit(solution)/shard_map/all_gather | solution.py:331
  34.1 244.5 %all-gather.11.cloned.1.call-start = ((), (), s32[]{:S(2)}) async-start(), calls=%async_computation.16 | async-start | bytes 13516800 | tf_op jit(solution)/shard_map/all_gather | solution.py:336
  35.8 13.0 %all-to-all-start = ((bf16[32,2,400]{2,1,0:T(2,128)(2,1)}), bf16[32,2,400]{2,1,0:T(2,128)(2,1)S(1)}, u32[]{:S(2)}, u32[]{:S(2)}) async-start(bf16[32,2,400]{2,1,0:T(2,128)(2,1)} %reshape.215), calls=%async_computation | async-start | bytes 131072 | tf_op jit(solution)/shard_map/all_to_all | solution.py:254
  88.8 5.9 collective-permute-start
  286.5 5.3 collective-permute-start.1
  296.5 35.0 %all-to-all-start.3 = ((bf16[4,128,2560]{2,1,0:T(8,128)(2,1)}), bf16[4,128,2560]{2,1,0:T(8,128)(2,1)}, u32[]{:S(2)}, u32[]{:S(2)}) async-start(bf16[4,128,2560]{2,1,0:T(8,128)(2,1)} %fusion.2), calls=%async_computation.3 | async-start | bytes 5242880 | tf_op jit(solution)/shard_map/all_to_all | solution.py:254
  338.1 88.6 %all-to-all-start.4 = ((bf16[8,128,2560]{2,1,0:T(8,128)(2,1)}), bf16[8,128,2560]{2,1,0:T(8,128)(2,1)}, u32[]{:S(2)}, u32[]{:S(2)}) async-start(bf16[8,128,2560]{2,1,0:T(8,128)(2,1)} %broadcast_in_dim.81), calls=%async_computation.4 | async-start | bytes 10485760 | tf_op jit(solution)/shard_map/all_to_all | solution.py:254
  342.9 305.7 %all-gather.13.cloned.1.call-start = ((), (), s32[]{:S(2)}) async-start(), calls=%async_computation.18 | async-start | bytes 11141120 | tf_op jit(solution)/shard_map/all_gather | solution.py:343
  426.7 86.3 %all-to-all-start.5 = ((bf16[16,80,1024]{2,1,0:T(8,128)(2,1)}), bf16[16,80,1024]{2,1,0:T(8,128)(2,1)}, u32[]{:S(2)}, u32[]{:S(2)}) async-start(bf16[16,80,1024]{2,1,0:T(8,128)(2,1)} %fusion.9), calls=%async_computation.5 | async-start | bytes 5242880 | tf_op jit(solution)/shard_map/all_to_all | solution.py:254
  435.1 460.1 %reduce-scatter.6.cloned.1.call-start = ((), (), s32[]{:S(2)}) async-start(), calls=%async_computation.17 | async-start | bytes 11141120 | tf_op jit(solution)/shard_map/reduce_scatter | solution.py:410
  435.1 109.4 %collective-permute-start.2 = (bf16[8,128,2560]{2,1,0:T(8,128)(2,1)}, bf16[8,128,2560]{2,1,0:T(8,128)(2,1)}, u32[]{:S(2)}, u32[]{:S(2)}) collective-permute-start(bf16[8,128,2560]{2,1,0:T(8,128)(2,1)} %all-to-all-done.4), channel_id=1, source_target_pairs={{0,1},{1,0},{2,3},{3,2},{4,5},{5,4},{6,7},{7,6},{8,9},{9,8},{10,11... | collective-permute-start | bytes 15728648 | tf_op jit(solution)/shard_map/ppermute | solution.py:266
  435.5 71.3 %collective-permute-start.4 = (bf16[240,2560]{1,0:T(8,128)(2,1)S(1)}, bf16[240,2560]{1,0:T(8,128)(2,1)}, u32[]{:S(2)}, u32[]{:S(2)}) collective-permute-start(bf16[240,2560]{1,0:T(8,128)(2,1)S(1)} %copy-done.37), channel_id=1, source_target_pairs={{0,16},{16,0},{1,17},{17,1},{2,18},{18,2},{3,19},{19,3},{4,20},{20... | collective-permute-start | bytes 3686408 | tf_op jit(solution)/shard_map/ppermute | solution.py:353
  509.6 30.9 %collective-permute-start.5 = (bf16[240,2560]{1,0:T(8,128)(2,1)}, bf16[240,2560]{1,0:T(8,128)(2,1)S(1)}, u32[]{:S(2)}, u32[]{:S(2)}) collective-permute-start(bf16[240,2560]{1,0:T(8,128)(2,1)} %get-tuple-element.128), channel_id=1, source_target_pairs={{0,0},{1,4},{2,8},{3,12},{4,1},{5,5},{6,9},{7,13},{8,2},{9,6},{10,... | collective-permute-start | bytes 3686408 | tf_op jit(solution)/shard_map/ppermute | solution.py:365
  513.0 28.5 %collective-permute-start.6 = (bf16[240,2560]{1,0:T(8,128)(2,1)}, bf16[240,2560]{1,0:T(8,128)(2,1)}, u32[]{:S(2)}, u32[]{:S(2)}) collective-permute-start(bf16[240,2560]{1,0:T(8,128)(2,1)} %get-tuple-element.129), channel_id=1, source_target_pairs={{0,4},{1,0},{2,12},{3,8},{4,5},{5,1},{6,13},{7,9},{8,6},{9,2},{10,... | collective-permute-start | bytes 3686408 | tf_op jit(solution)/shard_map/ppermute | solution.py:366
  513.1 116.5 %collective-permute-start.3 = (bf16[1280,1024]{1,0:T(8,128)(2,1)}, bf16[1280,1024]{1,0:T(8,128)(2,1)}, u32[]{:S(2)}, u32[]{:S(2)}) collective-permute-start(bf16[1280,1024]{1,0:T(8,128)(2,1)} %bitcast.30), channel_id=1, source_target_pairs={{0,16},{16,0},{1,17},{17,1},{2,18},{18,2},{3,19},{19,3},{4,20},{20... | collective-permute-start | bytes 7864328 | tf_op jit(solution)/shard_map/ppermute | solution.py:351
  704.4 9.7 collective-permute-start.7
  720.7 105.4 %all-to-all-start.6 = ((bf16[8,128,2560]{2,1,0:T(8,128)(2,1)}), bf16[8,128,2560]{2,1,0:T(8,128)(2,1)}, u32[]{:S(2)}, u32[]{:S(2)}) async-start(bf16[8,128,2560]{2,1,0:T(8,128)(2,1)} %fusion), calls=%async_computation.7 | async-start | bytes 10485760 | tf_op jit(solution)/shard_map/all_to_all | solution.py:254
  727.1 251.2 %all-gather.15.cloned.1.call-start = ((), (), s32[]{:S(2)}) async-start(), calls=%async_computation.20 | async-start | bytes 7077888 | tf_op jit(solution)/shard_map/all_gather | solution.py:396
  900.3 33.5 %all-to-all-start.7 = ((bf16[4,128,2560]{2,1,0:T(8,128)(2,1)}), bf16[4,128,2560]{2,1,0:T(8,128)(2,1)S(1)}, u32[]{:S(2)}, u32[]{:S(2)}) async-start(bf16[4,128,2560]{2,1,0:T(8,128)(2,1)} %broadcast_in_dim.84), calls=%async_computation.8 | async-start | bytes 5242880 | tf_op jit(solution)/shard_map/all_to_all | solution.py:254
  903.9 343.5 %reduce-scatter.10.cloned.1.call-start = ((), (), s32[]{:S(2)}) async-start(), calls=%async_computation.21 | async-start | bytes 2457600
  915.3 146.3 %collective-permute-start.13 = (bf16[512,1280]{1,0:T(8,128)(2,1)}, bf16[512,1280]{1,0:T(8,128)(2,1)}, u32[]{:S(2)}, u32[]{:S(2)}) collective-permute-start(bf16[512,1280]{1,0:T(8,128)(2,1)} %constant_dynamic-slice_fusion.4), channel_id=1, source_target_pairs={{0,16},{16,0},{1,17},{17,1},{2,18},{18,2},{3,19},{19,3},{4,20},{20... | collective-permute-start | bytes 3932168 | tf_op jit(solution)/shard_map/ppermute | solution.py:419
  933.8 18.1 %collective-permute-start.8 = (bf16[4,128,2560]{2,1,0:T(8,128)(2,1)S(1)}, bf16[4,128,2560]{2,1,0:T(8,128)(2,1)S(1)}, u32[]{:S(2)}, u32[]{:S(2)}) collective-permute-start(bf16[4,128,2560]{2,1,0:T(8,128)(2,1)S(1)} %all-to-all-done.7), channel_id=1, source_target_pairs={{0,1},{1,0},{2,3},{3,2},{4,5},{5,4},{6,7},{7,6},{8,9},{9,8},{10,11... | collective-permute-start | bytes 7864328 | tf_op jit(solution)/shard_map/ppermute | solution.py:266
  951.8 214.0 %collective-permute-start.11 = (bf16[1280,1024]{0,1:T(8,128)(2,1)}, bf16[1280,1024]{0,1:T(8,128)(2,1)}, u32[]{:S(2)}, u32[]{:S(2)}) collective-permute-start(bf16[1280,1024]{0,1:T(8,128)(2,1)} %constant_dynamic-slice_fusion.6), channel_id=1, source_target_pairs={{0,16},{16,0},{1,17},{17,1},{2,18},{18,2},{3,19},{19,3},{4,20},{20... | collective-permute-start | bytes 7864328 | tf_op jit(solution)/shard_map/ppermute | solution.py:419
  986.0 278.3 %reduce-scatter.8.cloned.1.call-start = ((), (), s32[]{:S(2)}) async-start(), calls=%async_computation.19 | async-start | bytes 4096000 | tf_op jit(solution)/shard_map/reduce_scatter | solution.py:457
  1023.7 146.4 %collective-permute-start.9 = (bf16[4,128,2560]{2,1,0:T(8,128)(2,1)}, bf16[4,128,2560]{2,1,0:T(8,128)(2,1)}, u32[]{:S(2)}, u32[]{:S(2)}) collective-permute-start(bf16[4,128,2560]{2,1,0:T(8,128)(2,1)} %dynamic-slice_bitcast_fusion.1), channel_id=1, source_target_pairs={{0,1},{1,0},{2,3},{3,2},{4,5},{5,4},{6,7},{7,6},{8,9},{9,8},{10,11... | collective-permute-start | bytes 7864328 | tf_op jit(solution)/shard_map/ppermute | solution.py:276
  1065.6 127.9 %collective-permute-start.14 = (bf16[512,640]{1,0:T(8,128)(2,1)}, bf16[512,640]{1,0:T(8,128)(2,1)}, u32[]{:S(2)}, u32[]{:S(2)}) collective-permute-start(bf16[512,640]{1,0:T(8,128)(2,1)} %constant_dynamic-slice_fusion.2), channel_id=1, source_target_pairs={{0,8},{8,0},{1,9},{9,1},{2,10},{10,2},{3,11},{11,3},{4,12},{12,4},... | collective-permute-start | bytes 1966088 | tf_op jit(solution)/shard_map/ppermute | solution.py:425
  1066.7 120.9 %all-to-all-start.10 = ((f32[4,80,640]{2,1,0:T(8,128)}), f32[4,80,640]{2,1,0:T(8,128)S(1)}, u32[]{:S(2)}, u32[]{:S(2)}) async-start(f32[4,80,640]{2,1,0:T(8,128)} %bitcast.43), calls=%async_computation.12 | async-start | bytes 1638400 | tf_op jit(solution)/shard_map/all_to_all | solution.py:254
  1170.2 55.4 %collective-permute-start.12 = (bf16[640,1024]{0,1:T(8,128)(2,1)}, bf16[640,1024]{0,1:T(8,128)(2,1)}, u32[]{:S(2)}, u32[]{:S(2)}) collective-permute-start(bf16[640,1024]{0,1:T(8,128)(2,1)} %constant_dynamic-slice_fusion.5), channel_id=1, source_target_pairs={{0,8},{8,0},{1,9},{9,1},{2,10},{10,2},{3,11},{11,3},{4,12},{12,4},... | collective-permute-start | bytes 3932168 | tf_op jit(solution)/shard_map/ppermute | solution.py:425
  1187.5 62.1 %all-to-all-start.8 = ((bf16[4,128,2560]{2,1,0:T(8,128)(2,1)}), bf16[4,128,2560]{2,1,0:T(8,128)(2,1)}, u32[]{:S(2)}, u32[]{:S(2)}) async-start(bf16[4,128,2560]{2,1,0:T(8,128)(2,1)} %fusion.1), calls=%async_computation.9 | async-start | bytes 5242880 | tf_op jit(solution)/shard_map/all_to_all | solution.py:254
  1227.7 17.7 %collective-permute-start.10 = (f32[80,640]{1,0:T(8,128)}, f32[80,640]{1,0:T(8,128)S(1)}, u32[]{:S(2)}, u32[]{:S(2)}) collective-permute-start(f32[80,640]{1,0:T(8,128)} %reduce_sum.117), channel_id=1, source_target_pairs={{0,0},{1,4},{2,8},{3,12},{4,16},{5,20},{6,24},{7,28},{8,1},{9,5},{... | collective-permute-start | bytes 614408 | tf_op jit(solution)/shard_map/ppermute | solution.py:467
  1253.1 10.6 all-to-all-start.9
  (56 other events, 1129.9 us)
Sparse Core Ops, SparseCore 0:
  12.3 68.0 all-gather.8
  82.0 96.5 all-gather.6
  181.5 97.1 all-gather.10
  730.1 105.5 all-gather.14
  986.1 68.6 reduce-scatter.9
  1056.9 149.6 reduce-scatter.7
Sparse Core Ops, SparseCore 1:
  345.6 152.9 all-gather.12
  682.3 212.8 reduce-scatter.5

commit v2 on v1

--- a/solution.py
+++ b/solution.py
@@ -22,14 +22,6 @@
 
 def dot(a, b, ca, cb):
     return lax.dot_general(a, b, (((ca,), (cb,)), ((), ())), preferred_element_type=F32)
-
-
-def rms_back(values, gain, grad):
-    r = lax.rsqrt(jnp.mean(values * values, axis=-1, keepdims=True) + 1e-06)
-    q = grad * gain
-    gain_grad = jnp.sum(grad * values * r, axis=0)
-    value_grad = r * q - r * r * r * values * jnp.mean(q * values, axis=-1, keepdims=True)
-    return value_grad, gain_grad
 
 
 def gelu_parts(x):
@@ -260,22 +252,492 @@
     )
 
 
-def gather_rows(rows, axes):
-    count = lax.axis_size(axes)
-    mine = exchange(jnp.broadcast_to(rows[None], (count,) + rows.shape), axes)
-    other = lax.ppermute(mine, "core", SWAP)
-    both = in_order(lax.axis_index("core"), mine[:, None], other[:, None], 1)
-    return both.reshape((-1,) + rows.shape[1:])
-
-
-def scatter_sum(partial, axes, tok):
+def chain_sum(partial, count):
+    here = lax.axis_index("hi") * (count // 2) + lax.axis_index("lo")
+    size = partial.shape[0] // count
+    block = lambda d: lax.dynamic_slice_in_dim(partial, jnp.clip(d, 0, count - 1) * size, size).astype(F32)
+    total = block(here)
+    for way in (1, -1):
+        held = None
+        for k in range(count - 1):
+            value = block(here + way * (count - 1 - k))
+            value = value if held is None else value + held
+            pairs = [(z, z + 1) for z in range(k + 1)]
+            if way < 0:
+                pairs = [(count - 1 - a, count - 1 - b) for a, b in pairs]
+            held = lax.ppermute(value.astype(BF), DP, pairs).astype(F32)
+        total = total + held
+    return total
+
+
+def device(lo, cx, core):
+    return {"lo": lo, "cxy": cx, "core": core}
+
+
+class Group:
+    def __init__(self, n_lo, n_cx, cube):
+        self.n_cx = n_cx
+        self.count = n_lo * n_cx if cube else n_cx
+        self.cube = cube
+        self.lo = lax.axis_index("lo")
+        self.cx = lax.axis_index("cxy")
+        self.core = lax.axis_index("core")
+        self.place = self.lo * n_cx + self.cx if cube else self.cx
+
+    def at(self, step):
+        return lax.rem(self.place + step + self.count, self.count)
+
+    def peer(self, step):
+        spot = self.at(step)
+        lo = spot // self.n_cx if self.cube else self.lo
+        return device(lo, lax.rem(spot, self.n_cx), self.core)
+
+    def sibling(self):
+        return device(self.lo, self.cx, 1 - self.core)
+
+
+def across():
+    return {"hi": 1 - lax.axis_index("hi")}
+
+
+def meet(group, both=False):
+    barrier = pltpu.get_barrier_semaphore()
+    if both:
+        pl.semaphore_signal(barrier, inc=1, device_id=across(), device_id_type=pl.DeviceIdType.MESH)
+    for step in range(1, group.count):
+        pl.semaphore_signal(barrier, inc=1, device_id=group.peer(step), device_id_type=pl.DeviceIdType.MESH)
+    pl.semaphore_signal(barrier, inc=1, device_id=group.sibling(), device_id_type=pl.DeviceIdType.MESH)
+    pl.semaphore_wait(barrier, group.count + int(both))
+
+
+def send(src, dst, out_sem, in_sem, target):
+    return pltpu.make_async_remote_copy(
+        src_ref=src, dst_ref=dst, send_sem=out_sem, recv_sem=in_sem,
+        device_id=target, device_id_type=pl.DeviceIdType.MESH,
+    )
+
+
+def spread_begin(group, src, out, sems):
+    keep, out_sems, in_sems, pass_sems, mate_sems = sems
+    mine = out.at[group.place * 2 + group.core]
+    local = pltpu.make_async_copy(src, mine, keep)
+    local.start()
+    direct = [send(src, mine, out_sems.at[s], in_sems.at[s], group.peer(s)) for s in range(1, group.count)]
+    for copy in direct:
+        copy.start()
+    mate = send(src, mine, pass_sems.at[0], mate_sems.at[0], group.sibling())
+    mate.start()
+    return local, direct, mate
+
+
+def spread_end(group, src, out, sems, begun):
+    keep, out_sems, in_sems, pass_sems, mate_sems = sems
+    slot = lambda place, core: out.at[place * 2 + core]
+    local, direct, first = begun
+    mate = [first]
+    for s in range(1, group.count):
+        came = slot(group.at(-s), group.core)
+        send(came, came, out_sems.at[s], in_sems.at[s], group.peer(s)).wait_recv()
+        mate.append(send(came, came, pass_sems.at[s], mate_sems.at[s], group.sibling()))
+        mate[s].start()
+    local.wait()
+    for copy in direct:
+        copy.wait_send()
+    for s in range(group.count):
+        mate[s].wait_send()
+        there = slot(group.at(-s), 1 - group.core)
+        send(there, there, pass_sems.at[s], mate_sems.at[s], group.sibling()).wait_recv()
+
+
+def spread(group, src, out, sems):
+    spread_end(group, src, out, sems, spread_begin(group, src, out, sems))
+
+
+def spread_sems(count):
+    return [pltpu.SemaphoreType.DMA(())] + [pltpu.SemaphoreType.DMA((count,)) for _ in range(4)]
+
+
+def fold(group, part, mate_buf, far_buf, mine, stage, total, sems):
+    load_sems, pass_sems, mate_sems, out_sems, in_sems, stage_sems = sems
+    order = list(range(1, group.count)) + [0]
+    rows = total.shape[0]
+    mates, loads, fars = {}, {}, {}
+    for s in order:
+        spot = group.at(s)
+        mates[s] = send(
+            part.at[spot, 1 - group.core], mate_buf.at[spot], pass_sems.at[s], mate_sems.at[s], group.sibling()
+        )
+        mates[s].start()
+        loads[s] = pltpu.make_async_copy(part.at[spot, group.core], mine.at[s], load_sems.at[s])
+        loads[s].start()
+    for turn, s in enumerate(order):
+        mates[s].wait_recv()
+        slot = turn % 2
+        fetch = pltpu.make_async_copy(mate_buf.at[group.at(s)], stage.at[slot], stage_sems.at[slot])
+        fetch.start()
+        loads[s].wait()
+        fetch.wait()
+
+        def add(r, held):
+            at = pl.ds(pl.multiple_of(r * 16, 16), 16)
+            value = mine[s, at, :].astype(F32) + stage[slot, at, :].astype(F32)
+            if s:
+                mine[s, at, :] = value.astype(BF)
+            else:
+                total[at, :] = value
+            return held
+
+        lax.fori_loop(0, rows // 16, add, 0)
+        if s:
+            fars[s] = send(mine.at[s], far_buf.at[s - 1], out_sems.at[s], in_sems.at[s], group.peer(s))
+            fars[s].start()
+    for turn, s in enumerate(order[:-1]):
+        fars[s].wait_recv()
+        slot = turn % 2
+        fetch = pltpu.make_async_copy(far_buf.at[s - 1], stage.at[slot], stage_sems.at[slot])
+        fetch.start()
+        fetch.wait()
+
+        def take(r, held):
+            at = pl.ds(pl.multiple_of(r * 16, 16), 16)
+            total[at, :] += stage[slot, at, :].astype(F32)
+            return held
+
+        lax.fori_loop(0, rows // 16, take, 0)
+    for s in order:
+        mates[s].wait_send()
+        if s:
+            fars[s].wait_send()
+
+
+def fold_scratch(count, tok, width):
+    return [
+        pltpu.VMEM((count, tok, width), BF),
+        pltpu.VMEM((2, tok, width), BF),
+        pltpu.VMEM((tok, width), F32),
+    ] + [pltpu.SemaphoreType.DMA((count,)) for _ in range(5)] + [pltpu.SemaphoreType.DMA((2,))]
+
+
+def each_rows(rows, body):
+    def run(r, held):
+        body(pl.ds(pl.multiple_of(r * 16, 16), 16))
+        return held
+
+    lax.fori_loop(0, rows // 16, run, 0)
+
+
+def middle_forward(n_lo, n_cx, part, away, inputs, gain, hidden, second_all, got, mate_buf, far_buf,
+                   mine, stage, total, f0, f1, f2, f3, f4, f5, second, k, s0, s1, s2, s3, h0, h1):
+    cube = Group(n_lo, n_cx, True)
+    plane = Group(n_lo, n_cx, False)
+    meet(cube, True)
+    half = send(away, got, h0, h1, across())
+    half.start()
+    fold(plane, part, mate_buf, far_buf, mine, stage, total, (f0, f1, f2, f3, f4, f5))
+
+    def norm(at):
+        h = inputs[at, :] + total[at, :]
+        hidden[at, :] = h
+        r = lax.rsqrt(jnp.mean(h * h, axis=-1, keepdims=True) + 1e-06)
+        second[at, :] = (h * r * gain[...]).astype(BF)
+
+    each_rows(total.shape[0], norm)
+    spread(cube, second, second_all, (k, s0, s1, s2, s3))
+    half.wait()
+
+
+def norm_back(values, gain, grad, base, out, gain_grad, at):
+    v = values[at, :]
+    g = grad[at, :]
+    r = lax.rsqrt(jnp.mean(v * v, axis=-1, keepdims=True) + 1e-06)
+    q = g * gain[...]
+    back = base[at, :] + r * q - r * r * r * v * jnp.mean(q * v, axis=-1, keepdims=True)
+    out[at, :] = back
+    term = g * v * r
+    gain_grad[...] += term[0:8, :] + term[8:16, :]
+    return back
+
+
+def middle_backward(n_lo, n_cx, part, away_a, away_b, hidden, out_grad, gain, hidden_grad, gain_grad, branch_all,
+                    got_a, got_b, mate_buf, far_buf,
+                    mine, stage, total, f0, f1, f2, f3, f4, f5, branch, k, s0, s1, s2, s3, h0, h1, h2, h3):
+    cube = Group(n_lo, n_cx, True)
+    plane = Group(n_lo, n_cx, False)
+    meet(cube, True)
+    halves = [send(away_a, got_a, h0, h1, across()), send(away_b, got_b, h2, h3, across())]
+    for half in halves:
+        half.start()
+    fold(cube, part, mate_buf, far_buf, mine, stage, total, (f0, f1, f2, f3, f4, f5))
+    gain_grad[...] = jnp.zeros_like(gain_grad)
+
+    def norm(at):
+        branch[at, :] = norm_back(hidden, gain, total, out_grad, hidden_grad, gain_grad, at).astype(BF)
+
+    each_rows(total.shape[0], norm)
+    spread(plane, branch, branch_all, (k, s0, s1, s2, s3))
+    for half in halves:
+        half.wait()
+
+
+def last_backward(n_lo, n_cx, part, inputs, hidden_grad, gain, input_grad, gain_grad, mate_buf, far_buf,
+                  mine, stage, total, f0, f1, f2, f3, f4, f5):
+    plane = Group(n_lo, n_cx, False)
+    meet(plane)
+    fold(plane, part, mate_buf, far_buf, mine, stage, total, (f0, f1, f2, f3, f4, f5))
+    gain_grad[...] = jnp.zeros_like(gain_grad)
+
+    def norm(at):
+        norm_back(inputs, gain, total, hidden_grad, input_grad, gain_grad, at)
+
+    each_rows(total.shape[0], norm)
+
+
+def comm_call(kernel, name, number, raw, args, outs, scratch, micros):
+    any_spec = pl.BlockSpec(memory_space=pl.ANY)
+    vmem = pl.BlockSpec(memory_space=pltpu.VMEM)
+    return pl.pallas_call(
+        kernel,
+        in_specs=[any_spec] * len(raw) + [vmem] * len(args),
+        out_specs=[vmem if inside else any_spec for _, inside in outs],
+        out_shape=[shape for shape, _ in outs],
+        scratch_shapes=scratch,
+        compiler_params=pltpu.CompilerParams(
+            collective_id=number, has_side_effects=True, vmem_limit_bytes=48 << 20
+        ),
+        cost_estimate=pl.CostEstimate(flops=micros * 10**9, bytes_accessed=micros * 10**6, transcendentals=0),
+        name=name,
+    )(*raw, *args)
+
+
+def middle_forward_call(n_lo, n_cx, part, away, inputs, gain):
+    tok, width = inputs.shape
+    near = n_cx
+    far = n_lo * n_cx
+    rows = jax.ShapeDtypeStruct((tok, width), F32)
+    bf = lambda n: jax.ShapeDtypeStruct((n, tok, width), BF)
+    hidden, second_all, got, _, _ = comm_call(
+        functools.partial(middle_forward, n_lo, n_cx), "sum_norm_gather_forward", 1,
+        (part.reshape(near, 2, tok, width), away), (inputs, gain),
+        [(rows, True), (bf(far * 2), False), (jax.ShapeDtypeStruct(away.shape, BF), False), (bf(near), False),
+         (bf(near - 1), False)],
+        fold_scratch(near, tok, width) + [pltpu.VMEM((tok, width), BF)] + spread_sems(far)
+        + [pltpu.SemaphoreType.DMA(()) for _ in range(2)], 120,
+    )
+    return hidden, second_all.reshape(-1, width), got
+
+
+def middle_backward_call(n_lo, n_cx, part, away_a, away_b, hidden, out_grad, gain):
+    tok, width = hidden.shape
+    near = n_cx
+    far = n_lo * n_cx
+    rows = jax.ShapeDtypeStruct((tok, width), F32)
+    bf = lambda n: jax.ShapeDtypeStruct((n, tok, width), BF)
+    hidden_grad, gain_grad, branch_all, got_a, got_b, _, _ = comm_call(
+        functools.partial(middle_backward, n_lo, n_cx), "sum_norm_gather_backward", 2,
+        (part.reshape(far, 2, tok, width), away_a, away_b), (hidden, out_grad, gain),
+        [(rows, True), (jax.ShapeDtypeStruct((8, width), F32), True), (bf(near * 2), False),
+         (jax.ShapeDtypeStruct(away_a.shape, BF), False), (jax.ShapeDtypeStruct(away_b.shape, BF), False),
+         (bf(far), False), (bf(far - 1), False)],
+        fold_scratch(far, tok, width) + [pltpu.VMEM((tok, width), BF)] + spread_sems(near)
+        + [pltpu.SemaphoreType.DMA(()) for _ in range(4)], 120,
+    )
+    return hidden_grad, gain_grad, branch_all.reshape(-1, width), got_a, got_b
+
+
+def last_backward_call(n_lo, n_cx, part, inputs, hidden_grad, gain):
+    tok, width = inputs.shape
+    near = n_cx
+    rows = jax.ShapeDtypeStruct((tok, width), F32)
+    bf = lambda n: jax.ShapeDtypeStruct((n, tok, width), BF)
+    input_grad, gain_grad, _, _ = comm_call(
+        functools.partial(last_backward, n_lo, n_cx), "sum_norm_backward", 3,
+        (part.reshape(near, 2, tok, width),), (inputs, hidden_grad, gain),
+        [(rows, True), (jax.ShapeDtypeStruct((8, width), F32), True), (bf(near), False), (bf(near - 1), False)],
+        fold_scratch(near, tok, width), 50,
+    )
+    return input_grad, gain_grad
+
+
+class Line:
+    def __init__(self, n_hi, n_lo):
+        self.n_lo = n_lo
+        self.count = n_hi * n_lo
+        self.z = lax.axis_index("hi") * n_lo + lax.axis_index("lo")
+
+    def device(self, z):
+        return {"hi": z // self.n_lo, "lo": lax.rem(z, self.n_lo)}
+
+    def run(self, buf, sems, k, action):
+        out_sems, in_sems = sems
+        last = self.count - 1
+        z = self.z
+        for side, way in ((0, 1), (1, -1)):
+            if way == 1:
+                sends = jnp.logical_and(z >= k, z < last)
+                comes = z >= k + 1
+            else:
+                sends = jnp.logical_and(z <= last - k, z > 0)
+                comes = z <= last - 1 - k
+            at = side * last + k
+            if action == "recv":
+                @pl.when(comes)
+                def _():
+                    plane = buf.at[z - way * (k + 1)]
+                    send(plane, plane, out_sems.at[at], in_sems.at[at], self.device(z - way)).wait_recv()
+            else:
+                @pl.when(sends)
+                def _():
+                    plane = buf.at[z - way * k]
+                    copy = send(plane, plane, out_sems.at[at], in_sems.at[at], self.device(z + way))
+                    if action == "start":
+                        copy.start()
+                    else:
+                        copy.wait_send()
+
+
+def window_head(c, own_ch, bw, span):
+    head = own_ch * c // bw
+    top = HEADS - span
+    return head - head // (top + 1) * (head - top)
+
+
+def window_shard(head, n_dev, n_ctx, span):
+    return head * ((n_dev - n_ctx) // (HEADS - span))
+
+
+def gather_start(sizes, gl_send, gu_send, pg, normed, down,
+                 gl_out, gu_out, pg_z, pg_win, normed_all, down_other,
+                 local_sems, gl_s, gl_r, gu_s, gu_r, win_s, win_r, zp_s, zp_r, zg_s, zg_r, dn_s, dn_r,
+                 k0, k1, k2, k3, k4):
+    n_hi, n_lo, n_cx, n_core, own_ch, bw, span = sizes
+    n_ctx = n_cx * n_core
+    n_cube = n_lo * n_ctx
+    n_dev = n_hi * n_cube
+    hi = lax.axis_index("hi")
+    lo = lax.axis_index("lo")
+    cx = lax.axis_index("cxy")
     core = lax.axis_index("core")
-    blocks = partial.reshape((-1, 2, tok) + partial.shape[1:])
-    mine = lax.dynamic_index_in_dim(blocks, core, 1, keepdims=False)
-    away = lax.dynamic_index_in_dim(blocks, 1 - core, 1, keepdims=False)
-    got = lax.ppermute(away, "core", SWAP)
-    pair = (mine.astype(F32) + got.astype(F32)).astype(BF)
-    return jnp.sum(exchange(pair, axes).astype(F32), axis=0)
+    ctx = cx * n_core + core
+    spot = lo * n_ctx + ctx
+    number = hi * n_cube + spot
+    line = Line(n_hi, n_lo)
+    z = line.z
+    plane = Group(n_lo, n_cx, False)
+    in_plane = lambda c: {"cxy": c // n_core, "core": lax.rem(c, n_core)}
+    in_cube = lambda u: {"lo": u // n_ctx, **in_plane(lax.rem(u, n_ctx))}
+
+    barrier = pltpu.get_barrier_semaphore()
+
+    def greet(i, held):
+        other = lax.rem(number + i, n_dev)
+        pl.semaphore_signal(
+            barrier, inc=1, device_id={"hi": other // n_cube, **in_cube(lax.rem(other, n_cube))},
+            device_id_type=pl.DeviceIdType.MESH,
+        )
+        return held
+
+    lax.fori_loop(1, n_dev, greet, 0)
+    pl.semaphore_wait(barrier, n_dev - 1)
+
+    locals_ = [
+        pltpu.make_async_copy(pg, pg_z.at[z], local_sems.at[0]),
+        pltpu.make_async_copy(gl_send.at[ctx], gl_out.at[z, ctx], local_sems.at[1]),
+        pltpu.make_async_copy(gu_send.at[spot], gu_out.at[spot], local_sems.at[2]),
+    ]
+    for copy in locals_:
+        copy.start()
+    locals_[0].wait()
+    pg_sems, gl_sems = (zp_s, zp_r), (zg_s, zg_r)
+    steps = line.count - 1
+    line.run(pg_z, pg_sems, 0, "start")
+    gl_copies = []
+    for s in range(1, n_ctx):
+        to = lax.rem(ctx + s, n_ctx)
+        gl_copies.append(send(gl_send.at[to], gl_out.at[z, ctx], gl_s.at[s], gl_r.at[s], in_plane(to)))
+        gl_copies[-1].start()
+    spread_sems_ = (k0, k1, k2, k3, k4)
+    mates = spread_begin(plane, normed, normed_all, spread_sems_)
+    locals_[1].wait()
+    for s in range(1, n_ctx):
+        came = gl_out.at[z, lax.rem(ctx - s + n_ctx, n_ctx)]
+        send(came, came, gl_s.at[s], gl_r.at[s], in_plane(lax.rem(ctx + s, n_ctx))).wait_recv()
+    line.run(gl_out, gl_sems, 0, "start")
+    for k in range(1, steps):
+        line.run(pg_z, pg_sems, k - 1, "recv")
+        line.run(pg_z, pg_sems, k, "start")
+    line.run(pg_z, pg_sems, steps - 1, "recv")
+
+    def window(src, dst):
+        first = window_shard(window_head(dst, own_ch, bw, span), n_dev, n_ctx, span)
+        turn = lax.rem(src - first + n_dev, n_ctx)
+        return (first + turn) // n_ctx, turn
+
+    shard, turn = window(ctx, ctx)
+    own_window = pltpu.make_async_copy(pg_z.at[shard], pg_win.at[turn], local_sems.at[3])
+    own_window.start()
+    win_copies = []
+    for s in range(1, n_ctx):
+        to = lax.rem(ctx + s, n_ctx)
+        shard, turn = window(ctx, to)
+        win_copies.append(send(pg_z.at[shard], pg_win.at[turn], win_s.at[s], win_r.at[s], in_plane(to)))
+        win_copies[-1].start()
+    gu_copies = []
+    for s in range(1, n_cube):
+        to = lax.rem(spot + s, n_cube)
+        gu_copies.append(send(gu_send.at[to], gu_out.at[spot], gu_s.at[s], gu_r.at[s], in_cube(to)))
+        gu_copies[-1].start()
+    for k in range(1, steps):
+        line.run(gl_out, gl_sems, k - 1, "recv")
+        line.run(gl_out, gl_sems, k, "start")
+    down_copy = send(down, down_other, dn_s, dn_r, {"hi": 1 - hi})
+    down_copy.start()
+    spread_end(plane, normed, normed_all, spread_sems_, mates)
+    for s in range(1, n_ctx):
+        _, turn = window(lax.rem(ctx - s + n_ctx, n_ctx), ctx)
+        came = pg_win.at[turn]
+        send(came, came, win_s.at[s], win_r.at[s], in_plane(lax.rem(ctx + s, n_ctx))).wait_recv()
+    for s in range(1, n_cube):
+        came = gu_out.at[lax.rem(spot - s + n_cube, n_cube)]
+        send(came, came, gu_s.at[s], gu_r.at[s], in_cube(lax.rem(spot + s, n_cube))).wait_recv()
+    line.run(gl_out, gl_sems, steps - 1, "recv")
+    own_window.wait()
+    locals_[2].wait()
+    for copy in gl_copies + win_copies + gu_copies:
+        copy.wait_send()
+    for k in range(steps):
+        line.run(pg_z, pg_sems, k, "sent")
+        line.run(gl_out, gl_sems, k, "sent")
+    down_copy.wait()
+
+
+def gather_start_call(sizes, gl_send, gu_send, pg, normed, down):
+    n_hi, n_lo, n_cx, n_core = sizes[:4]
+    n_ctx = n_cx * n_core
+    n_cube = n_lo * n_ctx
+    n_dp = n_hi * n_lo
+    sds = lambda *shape: jax.ShapeDtypeStruct(shape, BF)
+    any_spec = pl.BlockSpec(memory_space=pl.ANY)
+    dma = lambda *n: pltpu.SemaphoreType.DMA(n)
+    outs = [
+        sds(n_dp, n_ctx, *gl_send.shape[1:]), sds(*gu_send.shape), sds(n_dp, *pg.shape), sds(n_ctx, *pg.shape),
+        sds(n_ctx, *normed.shape), sds(*down.shape),
+    ]
+    hops = 2 * (n_dp - 1)
+    got = pl.pallas_call(
+        functools.partial(gather_start, sizes),
+        in_specs=[any_spec] * 5,
+        out_specs=[any_spec] * 6,
+        out_shape=outs,
+        scratch_shapes=[
+            dma(4), dma(n_ctx), dma(n_ctx), dma(n_cube), dma(n_cube), dma(n_ctx), dma(n_ctx),
+            dma(hops), dma(hops), dma(hops), dma(hops), dma(), dma(),
+        ] + spread_sems(n_cx),
+        compiler_params=pltpu.CompilerParams(collective_id=4, has_side_effects=True),
+        cost_estimate=pl.CostEstimate(flops=10**11, bytes_accessed=10**8, transcendentals=0),
+        name="gather_start",
+    )(gl_send, gu_send, pg, normed, down)
+    gl_out, gu_out, _, pg_win, normed_all, down_other = got
+    return gl_out, gu_out, pg_win, normed_all, down_other
 
 
 def pad_last(value, width):
@@ -299,11 +761,10 @@
     bw = recur_gate_w.shape[1]
     hidden_units = mlp_gate_w.shape[1]
     own_ch = chans // n_ctx
-    starts = [own_ch * c // bw for c in range(n_ctx)]
-    span = max((own_ch * (c + 1) - 1) // bw - starts[c] + 1 for c in range(n_ctx))
-    starts = [min(s, HEADS - span) for s in starts]
+    span = max((own_ch * (c + 1) - 1) // bw - own_ch * c // bw + 1 for c in range(n_ctx))
+    starts = [window_head(c, own_ch, bw, span) for c in range(n_ctx)]
     win = span * bw
-    head0 = jnp.array(starts, jnp.int32)[ctx]
+    head0 = window_head(ctx, own_ch, bw, span)
     ch0 = head0 * bw
     own_off = own_ch * ctx - ch0
     ff_own = hidden_units // (n_lo * n_ctx)
@@ -327,30 +788,29 @@
         )
         for s in starts
     ]
-    gl_part = exchange(jnp.stack(windows), CTX).reshape(-1, 2 * win)
-    gl_w = lax.all_gather(gl_part, DP, axis=0, tiled=True)
-    gates_all = lax.all_gather(jnp.concatenate([recur_gate_w, input_gate_w], axis=1), EVERY, axis=0, tiled=True)
-    gates_win = lax.dynamic_slice_in_dim(gates_all, ch0, win)
-    recur_w = gates_win[:, :bw]
-    input_w = gates_win[:, bw:]
-    proj_all = lax.all_gather(out_proj_w, EVERY, axis=0, tiled=True)
-    proj_w = lax.dynamic_slice_in_dim(proj_all, ch0, win)
+    pg = jnp.concatenate([out_proj_w, recur_gate_w, input_gate_w], axis=1)
 
     r_first = lax.rsqrt(jnp.mean(inputs * inputs, axis=-1, keepdims=True) + 1e-06)
     normed = (inputs * r_first * gain_first).astype(BF)
-    normed_all = gather_rows(normed, "cxy")
-
-    down_grad = lax.all_gather(out_grad.astype(BF), CUBE, axis=0, tiled=True)
 
     def columns(weight):
         parts = weight.reshape(weight.shape[0], n_ctx, n_lo, ff_own).transpose(2, 1, 0, 3)
         return pad_last(parts.reshape(n_lo * n_ctx, weight.shape[0], ff_own), ff_pad)
 
     gu_send = jnp.concatenate([columns(mlp_gate_w), columns(mlp_up_w)], axis=2)
-    gu_mine = exchange(gu_send, CUBE).reshape(-1, 2 * ff_pad)
-    gu_other = lax.ppermute(gu_mine, "hi", SWAP)
-    gu_w = in_order(hi, gu_mine, gu_other, 0)
-    down_other = lax.ppermute(mlp_down_w, "hi", SWAP)
+    sizes = (n_hi, n_lo, n_cx, n_core, own_ch, bw, span)
+    gl_w, gu_mine, pg_win, normed_all, down_other = gather_start_call(
+        sizes, jnp.stack(windows), gu_send, pg, normed, mlp_down_w
+    )
+    gl_w = gl_w.reshape(width, 2 * win)
+    gu_mine = gu_mine.reshape(-1, 2 * ff_pad)
+    normed_all = normed_all.reshape(tokens, width)
+    pg_win = lax.dynamic_slice_in_dim(
+        pg_win.reshape(-1, pg.shape[1]), ch0 - window_shard(head0, n_dev, n_ctx, span) * piece, win
+    )
+    proj_w = pg_win[:, :width]
+    recur_w = pg_win[:, width : width + bw]
+    input_w = pg_win[:, width + bw :]
     n_cube = n_lo * n_ctx
     half = n_cube // 2
     to_a, to_b = [], []
@@ -391,13 +851,11 @@
     linear_out = dot(normed_all, gl_w[:, win:], 1, 0).astype(BF)
     mixed, prev, conv_out, rec, inp = forward_call(linear_out, gelu_pre, meta, vecs, recur_w, input_w)
     proj_part = dot(mixed, proj_w, 1, 0).astype(BF)
-    hidden = inputs + scatter_sum(proj_part, "cxy", tok)
-    mixed_own = lax.dynamic_slice_in_dim(mixed, own_off, own_ch, axis=1)
-    mixed_all = lax.all_gather(mixed_own, CTX, axis=0, tiled=False)
-
-    r_second = lax.rsqrt(jnp.mean(hidden * hidden, axis=-1, keepdims=True) + 1e-06)
-    second = (hidden * r_second * gain_second).astype(BF)
-    second_all = gather_rows(second, ("lo", "cxy"))
+    out_grad_low = lax.optimization_barrier((out_grad.astype(BF), proj_w))[0]
+    down_grad = lax.all_gather(out_grad_low, CUBE, axis=0, tiled=True)
+    hidden, second_all, gu_other = middle_forward_call(n_lo, n_cx, proj_part, gu_mine, inputs, gain_second[None])
+    gu_w = in_order(hi, gu_mine, gu_other, 0)
+
     pre = dot(second_all, gu_w, 1, 0)
     gate_pre, up_pre = pre[:, :ff_pad], pre[:, ff_pad:]
     act_grad = dot(down_grad, down_w, 1, 1)
@@ -405,46 +863,44 @@
     activation = (gel * up_pre).astype(BF)
     gu_low = jnp.concatenate([(act_grad * up_pre * slope).astype(BF), (act_grad * gel).astype(BF)], axis=1)
     second_part = dot(gu_low, gu_w, 1, 1).astype(BF)
-    second_grad = scatter_sum(second_part, ("lo", "cxy"), tok)
-    out_part = dot(activation, down_w, 1, 0).astype(BF)
-    output = hidden + lax.psum_scatter(out_part, CUBE, scatter_dimension=0, tiled=True).astype(F32)
-
     grad_gu = dot(second_all, gu_low, 0, 0).astype(BF)
     grad_down = dot(activation, down_grad, 0, 0).astype(BF)
 
-    def settle(partial, axis):
-        size = partial.shape[axis] // n_hi
-        mine = lax.dynamic_slice_in_dim(partial, hi * size, size, axis)
-        away = lax.dynamic_slice_in_dim(partial, (1 - hi) * size, size, axis)
-        both = (mine.astype(F32) + lax.ppermute(away, "hi", SWAP).astype(F32)).astype(BF)
-        if n_lo == 1:
-            return both, None
-        size = size // n_lo
-        mine = lax.dynamic_slice_in_dim(both, lo * size, size, axis)
-        away = lax.dynamic_slice_in_dim(both, (1 - lo) * size, size, axis)
-        return mine, lax.ppermute(away, "lo", SWAP)
-
-    gu_a, gu_b = settle(grad_gu, 0)
-    dn_a, dn_b = settle(grad_down, 1)
+    def half_of(partial, which, axis, parts):
+        size = partial.shape[axis] // parts
+        return lax.dynamic_slice_in_dim(partial, which * size, size, axis)
+
+    away_gu = half_of(grad_gu, 1 - hi, 0, n_hi)
+    away_dn = half_of(grad_down, 1 - hi, 1, n_hi)
+    early = away_gu.shape[0] // 2
+    hidden_grad, gain_two_rows, branch_all, got_gu, got_dn = middle_backward_call(
+        n_lo, n_cx, second_part, away_gu[:early], away_dn, hidden, out_grad, gain_second[None]
+    )
+    rest_gu = lax.ppermute(lax.optimization_barrier((away_gu[early:], gain_two_rows))[0], "hi", SWAP)
+
+    def settle(partial, got, axis):
+        both = (half_of(partial, hi, axis, n_hi).astype(F32) + got.astype(F32)).astype(BF)
+        return half_of(both, lo, axis, n_lo), lax.ppermute(half_of(both, 1 - lo, axis, n_lo), "lo", SWAP)
+
+    dn_a, dn_b = settle(grad_down, got_dn, 1)
+    gu_a, gu_b = settle(grad_gu, jnp.concatenate([got_gu, rest_gu], axis=0), 0)
     grad_gate = in_order(lo, gu_a[:, :ff_own], gu_b[:, :ff_own], 1).astype(F32)
     grad_up = in_order(
         lo, gu_a[:, ff_pad : ff_pad + ff_own], gu_b[:, ff_pad : ff_pad + ff_own], 1
     ).astype(F32)
     grad_dn = in_order(lo, dn_a[:ff_own], dn_b[:ff_own], 0).astype(F32)
 
-    hidden_part, grad_gain_two = rms_back(hidden, gain_second, second_grad)
-    hidden_grad = out_grad + hidden_part
-    branch = hidden_grad.astype(BF)
-    branch_all = gather_rows(branch, "cxy")
+    out_part = dot(activation, lax.optimization_barrier((down_w, gain_two_rows))[0], 1, 0).astype(BF)
+    output = hidden + lax.psum_scatter(out_part, CUBE, scatter_dimension=0, tiled=True).astype(F32)
 
     mixed_grad = dot(branch_all, proj_w, 1, 1)
     gelu_low, linear_low, recur_wg, input_wg, sums = backward_call(
         mixed_grad, gelu_pre, conv_out, rec, inp, prev, linear_out, meta, vecs, recur_w, input_w
     )
-    branch_cols = lax.dynamic_slice_in_dim(branch_all, ctx * (width // n_ctx), width // n_ctx, axis=1)
-    grad_proj = jnp.einsum("ctr,td->crd", mixed_all, branch_cols, preferred_element_type=F32)
-    grad_proj = grad_proj.reshape(chans, width // n_ctx).astype(BF)
-    grad_proj = lax.psum_scatter(grad_proj, DP, scatter_dimension=0, tiled=True).astype(F32)
+    own_mixed = lax.dynamic_slice_in_dim(mixed, own_off, own_ch, axis=1)
+    grad_proj = dot(own_mixed, branch_all, 0, 0).astype(BF).reshape(own_ch, n_ctx, width // n_ctx)
+    grad_proj = exchange(grad_proj.transpose(1, 0, 2), CTX).reshape(chans, width // n_ctx)
+    grad_proj = chain_sum(grad_proj, n_dp).astype(F32)
     lows = jnp.concatenate([gelu_low, linear_low], axis=1)
     own_lows = jnp.concatenate(
         [
@@ -454,11 +910,9 @@
         axis=1,
     )
     grad_gl = dot(normed_all, own_lows, 0, 0).astype(BF)
-    grad_gl = lax.psum_scatter(grad_gl, DP, scatter_dimension=0, tiled=True).astype(F32)
+    grad_gl = chain_sum(grad_gl, n_dp).astype(F32)
     first_part = dot(lows, gl_w, 1, 1).astype(BF)
-    first_grad = scatter_sum(first_part, "cxy", tok)
-    input_part, grad_gain_one = rms_back(inputs, gain_first, first_grad)
-    input_grad = hidden_grad + input_part
+    input_grad, gain_one_rows = last_backward_call(n_lo, n_cx, first_part, inputs, hidden_grad, gain_first[None])
 
     packed = jnp.concatenate([recur_wg, input_wg, pad_last(sums.T, 128)], axis=1)
     packed = lax.dynamic_slice_in_dim(packed, own_off, own_ch, axis=0)
@@ -468,7 +922,7 @@
     grad_recur_w = packed[:, :bw]
     grad_input_w = packed[:, bw : 2 * bw]
     rest = packed[:, 2 * bw : 2 * bw + 8].T
-    gains = jnp.stack([grad_gain_one, grad_gain_two]).reshape(2, n_dev, piece).transpose(1, 0, 2)
+    gains = jnp.stack([jnp.sum(gain_one_rows, axis=0), jnp.sum(gain_two_rows, axis=0)]).reshape(2, n_dev, piece).transpose(1, 0, 2)
     gains = jnp.sum(exchange(gains, EVERY), axis=0)
 
     return (

time: 1280 us -> 1100 us (0.86)
  waiting for transfers between devices: 803 us -> 36.9 us
  Pallas kernels: 29.9 us -> 683 us
  blocking collectives: 61.7 us -> 0 us
  other arithmetic: 78.3 us -> 62.4 us
  starting transfers between devices: 59.5 us -> 75.2 us
    pallas_call x0 -> x4, Pallas kernels: none -> 653 us  [the longest x3 454 us: comm_call(): pl.pallas_call(kernel, in_specs=[any_spec] * len(raw) + [vmem] * len(args...]
    ppermute x12 -> x15, waiting for transfers between devices: 314 us -> 29.3 us  [the longest x12 29.2 us: chain_sum(): held = lax.ppermute(value.astype(BF), DP, pairs).astype(F32)]
    all_to_all x9 -> x4, waiting for transfers between devices: 239 us -> 7.65 us  [exchange(): return lax.all_to_all(value, axes, split_axis=0, concat_axis=0, tiled=True)]
    all_gather x5 -> x1, waiting for transfers between devices: 149 us -> 0.01 us  [per_device(): down_grad = lax.all_gather(out_grad_low, CUBE, axis=0, tiled=True)]
    reduce_scatter x1, waiting for transfers between devices: 65.2 us -> 0.01 us  [per_device(): lax.psum_scatter(out_part, CUBE, scatter_dimension=0, tiled=True)]
    all_to_all x2 -> x0, blocking collectives: 61.7 us -> none  [exchange(): return lax.all_to_all(value, axes, split_axis=0, concat_axis=0, tiled=True)]
    ppermute x12 -> x15, starting transfers between devices: 6.71 us -> 37.1 us  [the longest x12 30.7 us: chain_sum(): held = lax.ppermute(value.astype(BF), DP, pairs).astype(F32)]
    select_n x3 -> x0, local copies, waits for them, and re-layouts: 26 us -> none  [in_order(): jnp.where(flag == 0, jnp.concatenate([mine, other], axis=axis), jnp.conca...]
  transfers between devices with their start and end apart: 32 -> 24, of which waited for: 21 -> 5; matrix products, arithmetic and copies ran while one was open for 18% -> 17% of each run, Pallas kernels for 2% -> 24%
where the time goes in v2:
time: 1100 us; the launch traced here: 1090 us
  Pallas kernels  683 us (62%)
  matrix products  128 us (12%)
  local copies, waits for them, and re-layouts  84.9 us (8%)
  starting transfers between devices  75.2 us (7%)
  other arithmetic  62.4 us (6%)
  waiting for transfers between devices  36.9 us (3%)
  between operations  15.2 us (1%)
    pallas_call x3, Pallas kernels, comm_call(): pl.pallas_call(kernel, in_specs=[any_spec] * len(raw) + [vmem] * len(args...  454 us
    pallas_call x1, Pallas kernels, gather_start_call(): pl.pallas_call(functools.partial(gather_start, sizes), in_specs=[any_spec...  200 us
    dot_general x13, matrix products, dot(): lax.dot_general(a, b, (((ca,), (cb,)), ((), ())), preferred_element_type=...  128 us
    unnamed x138, local copies, waits for them, and re-layouts  37.1 us
    ppermute x12, starting transfers between devices, chain_sum(): held = lax.ppermute(value.astype(BF), DP, pairs).astype(F32)  30.7 us
    ppermute x12, waiting for transfers between devices, chain_sum(): held = lax.ppermute(value.astype(BF), DP, pairs).astype(F32)  29.2 us
    all_to_all x4, starting transfers between devices, exchange(): return lax.all_to_all(value, axes, split_axis=0, concat_axis=0, tiled=True)  26.3 us
  transfers between devices with their start and end apart: 24, of which 5 were waited for; matrix products, arithmetic and copies ran while one was open for 17% of the time, Pallas kernels for 24%

profile of v2, /device:TPU:1, one launch (start us, length us, event | category | flops | bytes accessed | tf_op | source)
XLA Modules:
  0.0 1085.4 jit_solution(1803962634422890129)
XLA Ops:
  9.5 7.2 all-to-all-start
  21.2 4.0 reshape.139
  46.1 199.9 %gather_start.1 = (bf16[4,8,80,1024]{3,2,1,0:T(8,128)(2,1)}, bf16[16,80,1024]{2,1,0:T(8,128)(2,1)}, bf16[4,80,3072]{2,1,0:T(8,128)(2,1)}, bf16[8,80,3072]{2,1,0:...) custom-call(bf16[8,80,1024]{2,1,0:T(8,128)(2,1)} %fusion.32.gl_send, ...), custom_call_target="tpu_custom_call" | custom-call | flops 99999997952 | bytes 100000000 | tf_op jit(solution)/shard_map/gather_start/pallas_call | solution.py:726
  256.2 7.8 collective-permute-start.1
  265.7 6.5 fusion.4.gpre_ref
  275.2 10.3 recur_forward.1
  285.6 4.7 convolution_convert_fusion.2
  290.3 157.9 %sum_norm_gather_forward.1 = (f32[128,2560]{1,0:T(8,128)S(1)}, bf16[16,128,2560]{2,1,0:T(8,128)(2,1)}, bf16[1280,1024]{1,0:T(8,128)(2,1)}, bf16[4,128,2560]{2,1,0:T(8,128)(2,1)}, bf16[3,128,2560]{2,1,0:T(8,128)(2,1)}) custom-call(bf16[4,2,128,2560]{3,2,1,0:T(8,128)(2,1)} %bitcast.118, bf16[1280,1024]{1,0:T(8,128)(2,1)} %bitcast.119, ...), custom_call_target="tpu_custom_call" | custom-call | flops 120000004096 | bytes 120000000 | tf_op jit(solution)/shard_map/sum_norm_gather_forward/pallas_call | solution.py:498
  449.3 19.2 %fusion.20 = f32[2048,1024]{0,1:T(8,128)} fusion(bf16[2048,2560]{1,0:T(8,128)(2,1)} %bitcast.102, bf16[1280,1024]{1,0:T(8,128)(2,1)} %get-tuple-element.52, bf16[1280,1024]{1,0:T(8,128)(2,1)} %bitcast.120, pred[]{:T(512)S(6)} %eq.29), kind=kOutput, calls=%fused_computation.55 | convolution fusion | flops 10761011200 | bytes 24117248 | tf_op jit(solution)/shard_map/dot_general | solution.py:24
  474.3 14.6 %multiply_convert_fusion.1 = (bf16[2048,512]{0,1:T(8,128)(2,1)S(1)}, bf16[2048,512]{0,1:T(8,128)(2,1)S(1)}, bf16[2048,512]{0,1:T(8,128)(2,1)}) fusion(f32[2048,1024]{0,1:T(8,128)} %fusion.20, bf16[2048,2560]{1,0:T(8,128)(2,1)} %all-gather.2.cloned.1.call-done, bf16[480,2560]{1,0:T(8,128)(2,1)} %copy-done.31), kind=kOutput, calls=%fused_computation.15 | convolution fusion | flops 5393874944 | bytes 27623424 | tf_op jit(solution)/shard_map/dot_general | solution.py:24
  490.9 15.5 %convolution_convert_fusion.4 = bf16[2560,1024]{1,0:T(8,128)(2,1)} fusion(bf16[2048,2560]{1,0:T(8,128)(2,1)} %bitcast.103, bf16[2048,512]{0,1:T(8,128)(2,1)S(1)} %get-tuple-element.133, bf16[2048,512]{0,1:T(8,128)(2,1)S(1)} %get-tuple-element.132), kind=kOutput, calls=%fused_computation.4 | convolution fusion | flops 10748428288 | bytes 19922944 | tf_op jit(solution)/shard_map/dot_general | solution.py:24
  506.4 19.0 %convolution_convert_fusion.1 = bf16[2048,2560]{1,0:T(8,128)(2,1)} fusion(bf16[2048,512]{0,1:T(8,128)(2,1)} %copy-done.57, bf16[2048,512]{0,1:T(8,128)(2,1)} %copy-done.56, bf16[1280,1024]{1,0:T(8,128)(2,1)} %get-tuple-element.52, bf16[1280,1024]{1,0:T(8,128)(2,1)} %bitcast.121, pred[]{:T(512)S(6)} %eq.29), kind=kOutput, calls=%fused_computation.1 | convolution fusion | flops 10774642688 | bytes 19922944 | tf_op jit(solution)/shard_map/dot_general | solution.py:24
  525.5 9.1 convolution_convert_fusion.6
  537.1 218.7 %sum_norm_gather_backward.1 = (f32[128,2560]{1,0:T(8,128)S(1)}, f32[8,2560]{1,0:T(8,128)S(1)}, bf16[8,128,2560]{2,1,0:T(8,128)(2,1)}, bf16[640,1024]{1,0:T(8,128...) custom-call(bf16[8,2,128,2560]{3,2,1,0:T(8,128)(2,1)} %bitcast.104, ...), custom_call_target="tpu_custom_call" | custom-call | flops 120000004096 | bytes 120000000 | tf_op jit(solution)/shard_map/sum_norm_gather_backward/pallas_call | solution.py:498
  759.1 8.5 convolution_convert_fusion
  772.4 5.6 collective-permute-start.15
  778.0 5.0 fusion.50.mg_ref
  783.1 19.5 %recur_backward.1 = (bf16[1024,512]{1,0:T(8,128)(2,1)S(1)}, bf16[1024,512]{1,0:T(8,128)(2,1)S(1)}, f32[512,256]{1,0:T(8,128)S(1)}, f32[512,256]{1,0:T(8,128)S(1)}, f32[8,512]{1,0:T(8,128)S(1)}) custom-call(f32[1024,512]{1,0:T(8,128)S(1)} %fusion.50.mg_ref, f32[1024,512]{1,0:T(8,128)S(1)} %copy-done.2, f32[1024,512]{1,0:T(8,128)S(1)} %get-tuple-element.58.conv_ref, ...), custom_call_target="tpu_custom_call" | custom-call | flops 1152385024 | bytes 15728640 | tf_op jit(solution)/shard_map/recur_backward/pallas_call | solution.py:224
  807.0 10.3 convolution_convert_fusion.3
  817.3 77.0 %sum_norm_backward.1 = (f32[128,2560]{1,0:T(8,128)S(1)}, f32[8,2560]{1,0:T(8,128)S(1)}, bf16[4,128,2560]{2,1,0:T(8,128)(2,1)}, bf16[3,128,2560]{2,1,0:T(8,128)(2,1)}) custom-call(bf16[4,2,128,2560]{3,2,1,0:T(8,128)(2,1)} %bitcast.117, f32[128,2560]{1,0:T(8,128)S(1)} %copy-done, f32[128,2560]{1,0:T(8,128)S(1)} %copy-done.29, f32[1,2560]{1,0:T(1,128)S(1)} %slice.216.gain), custom_call_target="tpu_custom_call" | custom-call | flops 49999998976 | bytes 50000000 | tf_op jit(solution)/shard_map/sum_norm_backward/pallas_call | solution.py:498
  895.1 10.1 all-to-all-start.1
  912.3 3.9 all-to-all-start.2
  916.2 6.6 convolution_convert_fusion.5
  925.9 4.3 collective-permute-start.2
  930.2 5.7 convolution_convert_fusion.7
  935.9 4.1 reshape.153
  943.1 5.2 all-to-all-start.3
  959.5 5.0 collective-permute-start.3
  972.7 6.2 all-to-all-done.3
  999.5 18.1 %collective-permute-done.9 = bf16[640,320]{0,1:T(8,128)(2,1)} collective-permute-done((bf16[640,320]{0,1:T(8,128)(2,1)}, bf16[640,320]{0,1:T(8,128)(2,1)}, u32[]{:S(2)}, u32[]{:S(2)}) %collective-permute-start.9) | collective-permute-done | bytes 409632 | tf_op jit(solution)/shard_map/ppermute | solution.py:268
  1019.5 4.9 collective-permute-start.10
  1062.7 8.6 collective-permute-done.7
  (271 shorter events, 167.5 us)
Async XLA Ops:
  9.5 33.8 %all-to-all-start = ((bf16[32,2,400]{2,1,0:T(2,128)(2,1)}), bf16[32,2,400]{2,1,0:T(2,128)(2,1)}, u32[]{:S(2)}, u32[]{:S(2)}) async-start(bf16[32,2,400]{2,1,0:T(2,128)(2,1)} %reshape.178), calls=%async_computation | async-start | bytes 131072 | tf_op jit(solution)/shard_map/all_to_all | solution.py:246
  16.7 457.6 %all-gather.2.cloned.1.call-start = ((), (), s32[]{:S(2)}) async-start(), calls=%async_computation.5 | async-start | bytes 11141120 | tf_op jit(solution)/shard_map/all_gather | solution.py:855
  33.1 11.9 %copy-start = (f32[128,2560]{1,0:T(8,128)S(1)}, f32[128,2560]{1,0:T(8,128)}, u32[]{:S(2)}) copy-start(f32[128,2560]{1,0:T(8,128)} %inputs.3) | copy-start | bytes 3932164
  249.5 824.9 %reduce-scatter.2.cloned.1.call-start = ((), (), s32[]{:S(2)}) async-start(), calls=%async_computation.6 | async-start | bytes 11141120 | tf_op jit(solution)/shard_map/reduce_scatter | solution.py:894
  254.3 214.2 %collective-permute-start = (bf16[240,2560]{1,0:T(8,128)(2,1)}, bf16[240,2560]{1,0:T(8,128)(2,1)}, u32[]{:S(2)}, u32[]{:S(2)}) collective-permute-start(bf16[240,2560]{1,0:T(8,128)(2,1)} %get-tuple-element.145), channel_id=1, source_target_pairs={{0,0},{1,4},{2,8},{3,12},{4,1},{5,5},{6,9},{7,13},{8,2},{9,6},{10,... | collective-permute-start | bytes 3686408 | tf_op jit(solution)/shard_map/ppermute | solution.py:825
  256.2 212.3 %collective-permute-start.1 = (bf16[240,2560]{1,0:T(8,128)(2,1)}, bf16[240,2560]{1,0:T(8,128)(2,1)}, u32[]{:S(2)}, u32[]{:S(2)}) collective-permute-start(bf16[240,2560]{1,0:T(8,128)(2,1)} %get-tuple-element.146), channel_id=1, source_target_pairs={{0,4},{1,0},{2,12},{3,8},{4,5},{5,1},{6,13},{7,9},{8,6},{9,2},{10,... | collective-permute-start | bytes 3686408 | tf_op jit(solution)/shard_map/ppermute | solution.py:826
  537.1 221.9 %copy-start.37 = (bf16[512,2560]{1,0:T(8,128)(2,1)S(1)}, bf16[512,2560]{1,0:T(8,128)(2,1)}, u32[]{:S(2)}) copy-start(bf16[512,2560]{1,0:T(8,128)(2,1)} %pad.21) | copy-start | bytes 7864324
  537.1 221.9 %copy-start.55 = (bf16[2048,512]{0,1:T(8,128)(2,1)S(1)}, bf16[2048,512]{0,1:T(8,128)(2,1)}, u32[]{:S(2)}) copy-start(bf16[2048,512]{0,1:T(8,128)(2,1)} %get-tuple-element.134) | copy-start | bytes 6291460
  771.6 180.0 %collective-permute-start.17 = (bf16[512,640]{1,0:T(8,128)(2,1)}, bf16[512,640]{1,0:T(8,128)(2,1)}, u32[]{:S(2)}, u32[]{:S(2)}) collective-permute-start(bf16[512,640]{1,0:T(8,128)(2,1)} %constant_dynamic-slice_fusion.2), channel_id=1, source_target_pairs={{0,8},{8,0},{1,9},{9,1},{2,10},{10,2},{3,11},{11,3},{4,12},{12,4},... | collective-permute-start | bytes 1966088 | tf_op jit(solution)/shard_map/ppermute | solution.py:883
  772.4 194.7 %collective-permute-start.15 = (bf16[640,1024]{1,0:T(8,128)(2,1)}, bf16[640,1024]{1,0:T(8,128)(2,1)}, u32[]{:S(2)}, u32[]{:S(2)}) collective-permute-start(bf16[640,1024]{1,0:T(8,128)(2,1)} %get-tuple-element.71), channel_id=1, source_target_pairs={{0,16},{16,0},{1,17},{17,1},{2,18},{18,2},{3,19},{19,3},{4,20},{20... | collective-permute-start | bytes 3932168 | tf_op jit(solution)/shard_map/ppermute | solution.py:879
  817.3 90.4 %copy-start.24 = (f32[512,256]{1,0:T(8,128)S(1)}, f32[512,256]{1,0:T(8,128)}, u32[]{:S(2)}) copy-start(f32[512,256]{1,0:T(8,128)} %copy-done.23) | copy-start | bytes 1572868
  894.3 15.4 %copy-start.21 = (bf16[1024,512]{1,0:T(8,128)(2,1)S(1)}, bf16[1024,512]{1,0:T(8,128)(2,1)}, u32[]{:S(2)}) copy-start(bf16[1024,512]{1,0:T(8,128)(2,1)} %copy-done.20) | copy-start | bytes 3145732
  895.1 17.2 %all-to-all-start.1 = ((f32[32,2,80]{2,1,0:T(2,128)}), f32[32,2,80]{2,1,0:T(2,128)S(1)}, u32[]{:S(2)}, u32[]{:S(2)}) async-start(f32[32,2,80]{2,1,0:T(2,128)} %maximum_bitcast_fusion.8), calls=%async_computation.2 | async-start | bytes 65536 | tf_op jit(solution)/shard_map/all_to_all | solution.py:246
  912.3 30.8 %all-to-all-start.2 = ((f32[4,80,640]{2,1,0:T(8,128)}), f32[4,80,640]{2,1,0:T(8,128)S(1)}, u32[]{:S(2)}, u32[]{:S(2)}) async-start(f32[4,80,640]{2,1,0:T(8,128)} %bitcast.91), calls=%async_computation.3 | async-start | bytes 1638400 | tf_op jit(solution)/shard_map/all_to_all | solution.py:246
  925.9 31.1 %collective-permute-start.2 = (bf16[640,640]{0,1:T(8,128)(2,1)}, bf16[640,640]{0,1:T(8,128)(2,1)}, u32[]{:S(2)}, u32[]{:S(2)}) collective-permute-start(bf16[640,640]{0,1:T(8,128)(2,1)} %get-tuple-element.141), channel_id=1, source_target_pairs={{0,8},{1,9},{2,10},{3,11},{4,12},{5,13},{6,14},{7,15}} | collective-permute-start | bytes 2457608 | tf_op jit(solution)/shard_map/ppermute | solution.py:268
  943.1 35.7 %all-to-all-start.3 = ((bf16[8,320,320]{2,1,0:T(8,128)(2,1)}), bf16[8,320,320]{2,1,0:T(8,128)(2,1)}, u32[]{:S(2)}, u32[]{:S(2)}) async-start(bf16[8,320,320]{2,1,0:T(8,128)(2,1)} %bitcast.88), calls=%async_computation.4 | async-start | bytes 3932160 | tf_op jit(solution)/shard_map/all_to_all | solution.py:246
  948.4 46.1 %collective-permute-start.5 = (bf16[640,640]{0,1:T(8,128)(2,1)}, bf16[640,640]{0,1:T(8,128)(2,1)}, u32[]{:S(2)}, u32[]{:S(2)}) collective-permute-start(bf16[640,640]{0,1:T(8,128)(2,1)} %get-tuple-element.142), channel_id=1, source_target_pairs={{24,16},{25,17},{26,18},{27,19},{28,20},{29,21},{30,22},{31,23}} | collective-permute-start | bytes 2457608 | tf_op jit(solution)/shard_map/ppermute | solution.py:268
  954.5 12.7 %copy-start.13 = (bf16[640,1024]{1,0:T(8,128)(2,1)S(1)}, bf16[640,1024]{1,0:T(8,128)(2,1)}, u32[]{:S(2)}) copy-start(bf16[640,1024]{1,0:T(8,128)(2,1)} %copy-done.12) | copy-start | bytes 3932164
  959.5 35.0 %collective-permute-start.3 = (bf16[640,640]{0,1:T(8,128)(2,1)}, bf16[640,640]{0,1:T(8,128)(2,1)}, u32[]{:S(2)}, u32[]{:S(2)}) collective-permute-start(bf16[640,640]{0,1:T(8,128)(2,1)} %add_convert_fusion.5), channel_id=1, source_target_pairs={{0,8},{8,16},{1,9},{9,17},{2,10},{10,18},{3,11},{11,19},{4,12},{12... | collective-permute-start | bytes 2457608 | tf_op jit(solution)/shard_map/ppermute | solution.py:268
  965.2 23.2 %collective-permute-start.8 = (f32[80,640]{1,0:T(8,128)}, f32[80,640]{1,0:T(8,128)S(1)}, u32[]{:S(2)}, u32[]{:S(2)}) collective-permute-start(f32[80,640]{1,0:T(8,128)} %reduce_sum.49), channel_id=1, source_target_pairs={{0,0},{1,4},{2,8},{3,12},{4,16},{5,20},{6,24},{7,28},{8,1},{9,5},{... | collective-permute-start | bytes 614408 | tf_op jit(solution)/shard_map/ppermute | solution.py:921
  971.7 76.3 %collective-permute-start.16 = (bf16[640,1024]{1,0:T(8,128)(2,1)}, bf16[640,1024]{1,0:T(8,128)(2,1)}, u32[]{:S(2)}, u32[]{:S(2)}) collective-permute-start(bf16[640,1024]{1,0:T(8,128)(2,1)} %constant_dynamic-slice_fusion.4), channel_id=1, source_target_pairs={{0,8},{8,0},{1,9},{9,1},{2,10},{10,2},{3,11},{11,3},{4,12},{12,4},... | collective-permute-start | bytes 3932168 | tf_op jit(solution)/shard_map/ppermute | solution.py:883
  984.4 33.2 %collective-permute-start.9 = (bf16[640,320]{0,1:T(8,128)(2,1)}, bf16[640,320]{0,1:T(8,128)(2,1)}, u32[]{:S(2)}, u32[]{:S(2)}) collective-permute-start(bf16[640,320]{0,1:T(8,128)(2,1)} %copy.76), channel_id=1, source_target_pairs={{0,8},{1,9},{2,10},{3,11},{4,12},{5,13},{6,14},{7,15}} | collective-permute-start | bytes 1228808 | tf_op jit(solution)/shard_map/ppermute | solution.py:268
  988.4 36.0 %collective-permute-start.12 = (bf16[640,320]{0,1:T(8,128)(2,1)}, bf16[640,320]{0,1:T(8,128)(2,1)}, u32[]{:S(2)}, u32[]{:S(2)}) collective-permute-start(bf16[640,320]{0,1:T(8,128)(2,1)} %copy.79), channel_id=1, source_target_pairs={{24,16},{25,17},{26,18},{27,19},{28,20},{29,21},{30,22},{31,23}} | collective-permute-start | bytes 1228808 | tf_op jit(solution)/shard_map/ppermute | solution.py:268
  994.4 23.2 %copy-start.41 = (bf16[640,320]{0,1:T(8,128)(2,1)S(1)}, bf16[640,320]{0,1:T(8,128)(2,1)}, u32[]{:S(2)}) copy-start(bf16[640,320]{0,1:T(8,128)(2,1)} %copy.75) | copy-start | bytes 1228804
  994.4 29.9 %copy-start.39 = (bf16[640,320]{0,1:T(8,128)(2,1)S(1)}, bf16[640,320]{0,1:T(8,128)(2,1)}, u32[]{:S(2)}) copy-start(bf16[640,320]{0,1:T(8,128)(2,1)} %copy.78) | copy-start | bytes 1228804
  998.0 46.3 %collective-permute-start.6 = (bf16[640,640]{0,1:T(8,128)(2,1)}, bf16[640,640]{0,1:T(8,128)(2,1)}, u32[]{:S(2)}, u32[]{:S(2)}) collective-permute-start(bf16[640,640]{0,1:T(8,128)(2,1)} %get-tuple-element.140), channel_id=1, source_target_pairs={{24,16},{16,8},{25,17},{17,9},{26,18},{18,10},{27,19},{19,11},{28,... | collective-permute-start | bytes 2457608 | tf_op jit(solution)/shard_map/ppermute | solution.py:268
  1019.5 15.9 %collective-permute-start.10 = (bf16[640,320]{0,1:T(8,128)(2,1)}, bf16[640,320]{0,1:T(8,128)(2,1)}, u32[]{:S(2)}, u32[]{:S(2)}) collective-permute-start(bf16[640,320]{0,1:T(8,128)(2,1)} %add_convert_fusion.9), channel_id=1, source_target_pairs={{0,8},{8,16},{1,9},{9,17},{2,10},{10,18},{3,11},{11,19},{4,12},{12... | collective-permute-start | bytes 1228808 | tf_op jit(solution)/shard_map/ppermute | solution.py:268
  1026.2 14.7 %collective-permute-start.13 = (bf16[640,320]{0,1:T(8,128)(2,1)}, bf16[640,320]{0,1:T(8,128)(2,1)}, u32[]{:S(2)}, u32[]{:S(2)}) collective-permute-start(bf16[640,320]{0,1:T(8,128)(2,1)} %add_convert_fusion.7), channel_id=1, source_target_pairs={{24,16},{16,8},{25,17},{17,9},{26,18},{18,10},{27,19},{19,11},{28,... | collective-permute-start | bytes 1228808 | tf_op jit(solution)/shard_map/ppermute | solution.py:268
  1033.2 29.5 %collective-permute-start.4 = (bf16[640,640]{0,1:T(8,128)(2,1)}, bf16[640,640]{0,1:T(8,128)(2,1)}, u32[]{:S(2)}, u32[]{:S(2)}) collective-permute-start(bf16[640,640]{0,1:T(8,128)(2,1)} %get-tuple-element.139), channel_id=1, source_target_pairs={{0,8},{8,16},{16,24},{1,9},{9,17},{17,25},{2,10},{10,18},{18,26},{... | collective-permute-start | bytes 2457608 | tf_op jit(solution)/shard_map/ppermute | solution.py:268
  1037.3 23.1 %collective-permute-start.11 = (bf16[640,320]{0,1:T(8,128)(2,1)}, bf16[640,320]{0,1:T(8,128)(2,1)}, u32[]{:S(2)}, u32[]{:S(2)}) collective-permute-start(bf16[640,320]{0,1:T(8,128)(2,1)} %add_convert_fusion.8), channel_id=1, source_target_pairs={{0,8},{8,16},{16,24},{1,9},{9,17},{17,25},{2,10},{10,18},{18,26},{... | collective-permute-start | bytes 1228808 | tf_op jit(solution)/shard_map/ppermute | solution.py:268
  1042.8 17.7 %collective-permute-start.14 = (bf16[640,320]{0,1:T(8,128)(2,1)}, bf16[640,320]{0,1:T(8,128)(2,1)}, u32[]{:S(2)}, u32[]{:S(2)}) collective-permute-start(bf16[640,320]{0,1:T(8,128)(2,1)} %add_convert_fusion.6), channel_id=1, source_target_pairs={{24,16},{16,8},{8,0},{25,17},{17,9},{9,1},{26,18},{18,10},{10,2},{... | collective-permute-start | bytes 1228808 | tf_op jit(solution)/shard_map/ppermute | solution.py:268
  1046.7 24.5 %collective-permute-start.7 = (bf16[640,640]{0,1:T(8,128)(2,1)}, bf16[640,640]{0,1:T(8,128)(2,1)}, u32[]{:S(2)}, u32[]{:S(2)}) collective-permute-start(bf16[640,640]{0,1:T(8,128)(2,1)} %add_convert_fusion.2), channel_id=1, source_target_pairs={{24,16},{16,8},{8,0},{25,17},{17,9},{9,1},{26,18},{18,10},{10,2},{... | collective-permute-start | bytes 2457608 | tf_op jit(solution)/shard_map/ppermute | solution.py:268
  (54 other events, 290.3 us)
Sparse Core Ops, SparseCore 0:
  249.7 190.6 all-gather.1
  767.7 174.5 reduce-scatter.1

commit v3 on v1

--- a/solution.py
+++ b/solution.py
@@ -22,14 +22,6 @@
 
 def dot(a, b, ca, cb):
     return lax.dot_general(a, b, (((ca,), (cb,)), ((), ())), preferred_element_type=F32)
-
-
-def rms_back(values, gain, grad):
-    r = lax.rsqrt(jnp.mean(values * values, axis=-1, keepdims=True) + 1e-06)
-    q = grad * gain
-    gain_grad = jnp.sum(grad * values * r, axis=0)
-    value_grad = r * q - r * r * r * values * jnp.mean(q * values, axis=-1, keepdims=True)
-    return value_grad, gain_grad
 
 
 def gelu_parts(x):
@@ -260,22 +252,815 @@
     )
 
 
-def gather_rows(rows, axes):
-    count = lax.axis_size(axes)
-    mine = exchange(jnp.broadcast_to(rows[None], (count,) + rows.shape), axes)
-    other = lax.ppermute(mine, "core", SWAP)
-    both = in_order(lax.axis_index("core"), mine[:, None], other[:, None], 1)
-    return both.reshape((-1,) + rows.shape[1:])
-
-
-def scatter_sum(partial, axes, tok):
+def send(src, dst, out_sem, in_sem, target):
+    return pltpu.make_async_remote_copy(
+        src_ref=src, dst_ref=dst, send_sem=out_sem, recv_sem=in_sem,
+        device_id=target, device_id_type=pl.DeviceIdType.MESH,
+    )
+
+
+def across():
+    return {"hi": 1 - lax.axis_index("hi")}
+
+
+def sibling():
+    return {"core": 1 - lax.axis_index("core")}
+
+
+def meet(targets):
+    barrier = pltpu.get_barrier_semaphore()
+    for target in targets:
+        pl.semaphore_signal(barrier, inc=1, device_id=target, device_id_type=pl.DeviceIdType.MESH)
+    pl.semaphore_wait(barrier, len(targets))
+
+
+def subsets(bits):
+    out = [()]
+    for b in bits:
+        out += [m + (b,) for m in out]
+    return out
+
+
+def lane_slices(width, parts):
+    tiles = width // 128
+    cuts = [tiles * i // parts * 128 for i in range(parts + 1)]
+    return [pl.ds(a, b - a) for a, b in zip(cuts[:-1], cuts[1:])]
+
+
+class Group:
+    def __init__(self, n_lo, n_cx, cube):
+        self.n_cx = n_cx
+        self.near = list(range(n_cx.bit_length() - 1))
+        self.far = len(self.near)
+        self.cube = cube and n_lo == 2
+        self.bits = self.near + ([self.far] if self.cube else [])
+        self.count = n_cx * (2 if self.cube else 1)
+        self.lo = lax.axis_index("lo")
+        self.cx = lax.axis_index("cxy")
+        self.core = lax.axis_index("core")
+        self.place = self.lo * n_cx + self.cx if self.cube else self.cx
+
+    def delta(self, bit):
+        stride = 1 << bit
+        return stride * (1 - 2 * lax.rem(self.place // stride, 2))
+
+    def at(self, mask):
+        spot = self.place
+        for bit in mask:
+            spot = spot + self.delta(bit)
+        return spot
+
+    def partner(self, bit):
+        if bit == self.far:
+            return {"lo": 1 - self.lo}
+        return {"cxy": self.cx + self.delta(bit)}
+
+    def partners(self):
+        return [self.partner(bit) for bit in self.bits]
+
+    def orders(self):
+        return [self.bits[i:] + self.bits[:i] for i in range(len(self.bits))]
+
+
+class Spread:
+    def __init__(self, group, src, out, sems):
+        self.group, self.src, self.out = group, src, out
+        self.keep, self.out_sems, self.in_sems, self.pass_sems, self.mate_sems = sems
+        self.orders = group.orders()
+        self.lanes = lane_slices(src.shape[-1], len(self.orders))
+        self.moves = []
+        index = 0
+        for s in range(len(group.bits)):
+            row = []
+            for order, lanes in zip(self.orders, self.lanes):
+                for mask in subsets(order[:s]):
+                    row.append((index, lanes, mask, order[s]))
+                    index += 1
+            self.moves.append(row)
+
+    @staticmethod
+    def sems(group_bits, parts):
+        moves = parts * ((1 << group_bits) - 1)
+        return [
+            pltpu.SemaphoreType.DMA(()), pltpu.SemaphoreType.DMA((moves,)), pltpu.SemaphoreType.DMA((moves,)),
+            pltpu.SemaphoreType.DMA((moves + 1,)), pltpu.SemaphoreType.DMA((moves + 1,)),
+        ]
+
+    def block(self, mask, core):
+        return self.group.at(mask) * 2 + core
+
+    def copy(self, move):
+        index, lanes, mask, bit = move
+        dst = self.out.at[self.block(mask, self.group.core), :, lanes]
+        src = dst if mask else self.src.at[:, lanes]
+        return send(src, dst, self.out_sems.at[index], self.in_sems.at[index], self.group.partner(bit))
+
+    def relay(self, move, core):
+        index, lanes, mask, bit = move
+        ref = self.out.at[self.block(mask + (bit,), core), :, lanes]
+        return send(ref, ref, self.pass_sems.at[index + 1], self.mate_sems.at[index + 1], sibling())
+
+    def own(self):
+        mine = self.out.at[self.block((), self.group.core)]
+        local = pltpu.make_async_copy(self.src, mine, self.keep)
+        return local, send(self.src, mine, self.pass_sems.at[0], self.mate_sems.at[0], sibling())
+
+    def begin(self):
+        self.start(0)
+        for copy in self.own():
+            copy.start()
+
+    def start(self, s):
+        for move in self.moves[s]:
+            self.copy(move).start()
+
+    def finish(self, s):
+        for move in self.moves[s]:
+            index, lanes, mask, bit = move
+            came = self.out.at[self.block(mask + (bit,), self.group.core), :, lanes]
+            send(came, came, self.out_sems.at[index], self.in_sems.at[index], self.group.partner(bit)).wait_recv()
+
+    def pass_on(self, s):
+        for move in self.moves[s]:
+            self.relay(move, self.group.core).start()
+
+    def step(self, s):
+        self.finish(s)
+        if s + 1 < len(self.moves):
+            self.start(s + 1)
+        self.pass_on(s)
+
+    def end(self):
+        local, mate = self.own()
+        local.wait()
+        mate.wait_send()
+        other = self.out.at[self.block((), 1 - self.group.core)]
+        send(other, other, self.pass_sems.at[0], self.mate_sems.at[0], sibling()).wait_recv()
+        for row in self.moves:
+            for move in row:
+                self.copy(move).wait_send()
+                self.relay(move, self.group.core).wait_send()
+                self.relay(move, 1 - self.group.core).wait_recv()
+
+
+class Fold:
+    def __init__(self, group, part, mate_buf, scratch):
+        self.group, self.part, self.mate_buf = group, part, mate_buf
+        (self.mine, self.far, self.stage, self.total,
+         self.load_sems, self.pass_sems, self.mate_sems, self.out_sems, self.in_sems, self.stage_sems) = scratch
+        self.orders = group.orders()
+        self.lanes = lane_slices(part.shape[-1], len(self.orders))
+        self.rows = self.total.shape[0]
+        self.moves = []
+        index = slot0 = 0
+        levels = len(group.bits)
+        for s in range(levels):
+            row = []
+            for order, lanes in zip(self.orders, self.lanes):
+                for n, mask in enumerate(subsets(order[s + 1 :])):
+                    row.append((index, lanes, mask, order[s], slot0 + n))
+                    index += 1
+            self.moves.append(row)
+            slot0 += 1 << (levels - s - 1)
+        masks = []
+        for order in self.orders:
+            masks += [m for m in subsets(group.bits) if order[0] in m and m not in masks]
+        masks += [m for m in subsets(group.bits) if m and m not in masks] + [()]
+        self.masks = masks
+
+    @staticmethod
+    def scratch(bits, parts, tok, width):
+        count = 1 << bits
+        moves = parts * (count - 1)
+        dma = lambda n: pltpu.SemaphoreType.DMA((n,))
+        return [
+            pltpu.VMEM((count, tok, width), BF), pltpu.VMEM((count - 1, tok, width), BF),
+            pltpu.VMEM((2, tok, width), BF), pltpu.VMEM((tok, width), F32),
+            dma(count), dma(count), dma(count), dma(moves), dma(moves), dma(2),
+        ]
+
+    def mate(self, n):
+        spot = self.group.at(self.masks[n])
+        return send(
+            self.part.at[spot, 1 - self.group.core], self.mate_buf.at[spot],
+            self.pass_sems.at[n], self.mate_sems.at[n], sibling(),
+        )
+
+    def load(self, n):
+        spot = self.group.at(self.masks[n])
+        return pltpu.make_async_copy(self.part.at[spot, self.group.core], self.mine.at[spot], self.load_sems.at[n])
+
+    def fetch(self, n):
+        return pltpu.make_async_copy(
+            self.mate_buf.at[self.group.at(self.masks[n])], self.stage.at[n % 2], self.stage_sems.at[n % 2]
+        )
+
+    def begin(self):
+        for n in range(len(self.masks)):
+            self.mate(n).start()
+            self.load(n).start()
+
+    def pairs(self):
+        started = [False] * len(self.orders)
+        count = len(self.masks)
+        self.mate(0).wait_recv()
+        self.fetch(0).start()
+        for n, mask in enumerate(self.masks):
+            if n + 1 < count:
+                self.mate(n + 1).wait_recv()
+                self.fetch(n + 1).start()
+            self.load(n).wait()
+            self.fetch(n).wait()
+            spot = self.group.at(mask)
+
+            def add(at, spot=spot, mask=mask, n=n):
+                value = self.mine[spot, at, :].astype(F32) + self.stage[n % 2, at, :].astype(F32)
+                if mask:
+                    self.mine[spot, at, :] = value.astype(BF)
+                else:
+                    self.total[at, :] = value
+
+            each_rows(self.rows, add)
+            for j, order in enumerate(self.orders):
+                need = [m for m in self.masks if order[0] in m]
+                if not started[j] and all(m in self.masks[: n + 1] for m in need):
+                    started[j] = True
+                    self.start(0, j)
+
+    def copy(self, move):
+        index, lanes, mask, bit, slot = move
+        return send(
+            self.mine.at[self.group.at(mask + (bit,)), :, lanes], self.far.at[slot, :, lanes],
+            self.out_sems.at[index], self.in_sems.at[index], self.group.partner(bit),
+        )
+
+    def start(self, s, part=None):
+        per = len(self.moves[s]) // len(self.orders)
+        for n, move in enumerate(self.moves[s]):
+            if part is None or n // per == part:
+                self.copy(move).start()
+
+    def take(self, s):
+        per = len(self.moves[s]) // len(self.orders)
+        for n, move in enumerate(self.moves[s]):
+            self.copy(move).wait_recv()
+            index, lanes, mask, bit, slot = move
+            spot = self.group.at(mask)
+
+            def add(at):
+                value = self.far[slot, at, lanes].astype(F32)
+                if mask:
+                    self.mine[spot, at, lanes] = (self.mine[spot, at, lanes].astype(F32) + value).astype(BF)
+                else:
+                    self.total[at, lanes] += value
+
+            each_rows(self.rows, add)
+            if (n + 1) % per == 0 and s + 1 < len(self.moves):
+                self.start(s + 1, n // per)
+
+    def end(self):
+        for n in range(len(self.masks)):
+            self.mate(n).wait_send()
+        for row in self.moves:
+            for move in row:
+                self.copy(move).wait_send()
+
+
+def each_rows(rows, body):
+    def run(r, held):
+        body(pl.ds(pl.multiple_of(r * 16, 16), 16))
+        return held
+
+    lax.fori_loop(0, rows // 16, run, 0)
+
+
+N_FOLD = 10
+N_SPREAD = 5
+
+
+def middle_forward(n_lo, n_cx, part, inputs, gain, hidden, second_all, mate_buf, *scratch):
+    fold_s, rest = scratch[:N_FOLD], scratch[N_FOLD:]
+    spread_s, (second,) = rest[:N_SPREAD], rest[N_SPREAD:]
+    cube = Group(n_lo, n_cx, True)
+    plane = Group(n_lo, n_cx, False)
+    meet(cube.partners() + [sibling()])
+    fold = Fold(plane, part, mate_buf, fold_s)
+    fold.begin()
+    fold.pairs()
+    for s in range(len(plane.bits)):
+        fold.take(s)
+
+    def norm(at):
+        h = inputs[at, :] + fold.total[at, :]
+        hidden[at, :] = h
+        r = lax.rsqrt(jnp.mean(h * h, axis=-1, keepdims=True) + 1e-06)
+        second[at, :] = (h * r * gain[...]).astype(BF)
+
+    each_rows(fold.rows, norm)
+    rows = Spread(cube, second, second_all, spread_s)
+    rows.begin()
+    for s in range(len(cube.bits)):
+        rows.step(s)
+    fold.end()
+    rows.end()
+
+
+def norm_back(values, gain, grad, base, out, gain_grad, at):
+    v = values[at, :]
+    g = grad[at, :]
+    r = lax.rsqrt(jnp.mean(v * v, axis=-1, keepdims=True) + 1e-06)
+    q = g * gain[...]
+    back = base[at, :] + r * q - r * r * r * v * jnp.mean(q * v, axis=-1, keepdims=True)
+    out[at, :] = back
+    term = g * v * r
+    gain_grad[...] += term[0:8, :] + term[8:16, :]
+    return back
+
+
+def middle_backward(n_lo, n_cx, part, hidden, out_grad, gain, hidden_grad, gain_grad, branch_all, mate_buf, *scratch):
+    fold_s, rest = scratch[:N_FOLD], scratch[N_FOLD:]
+    spread_s, (branch,) = rest[:N_SPREAD], rest[N_SPREAD:]
+    cube = Group(n_lo, n_cx, True)
+    plane = Group(n_lo, n_cx, False)
+    meet(cube.partners() + [sibling()])
+    fold = Fold(cube, part, mate_buf, fold_s)
+    fold.begin()
+    fold.pairs()
+    for s in range(len(cube.bits)):
+        fold.take(s)
+    gain_grad[...] = jnp.zeros_like(gain_grad)
+
+    def norm(at):
+        branch[at, :] = norm_back(hidden, gain, fold.total, out_grad, hidden_grad, gain_grad, at).astype(BF)
+
+    each_rows(fold.rows, norm)
+    rows = Spread(plane, branch, branch_all, spread_s)
+    rows.begin()
+    for s in range(len(plane.bits)):
+        rows.step(s)
+    fold.end()
+    rows.end()
+
+
+class Chain:
+    def __init__(self, z, count, part, blocks, came, sems, along):
+        self.z, self.count, self.part, self.blocks, self.came, self.along = z, count, part, blocks, came, along
+        self.load_sems, self.out_sems, self.in_sems = sems
+
+    @staticmethod
+    def scratch(count, rows, cols):
+        hops = 2 * (count - 1)
+        return [pltpu.VMEM((count, rows, cols), BF), pltpu.VMEM((hops, rows, cols), BF)] + dma_sems(count, hops, hops)
+
+    def load(self, d):
+        return pltpu.make_async_copy(self.part.at[d], self.blocks.at[d], self.load_sems.at[d])
+
+    def begin(self):
+        for d in range(self.count):
+            self.load(d).start()
+
+    def ready(self):
+        for d in range(self.count):
+            self.load(d).wait()
+
+    def sides(self, k):
+        last = self.count - 1
+        z = self.z
+        yield 0, 1, jnp.logical_and(z <= k, z < last), jnp.logical_and(z >= 1, z <= k + 1)
+        yield 1, -1, jnp.logical_and(z >= last - k, z > 0), jnp.logical_and(z <= last - 1, z >= last - 1 - k)
+
+    def copy(self, side, way, k):
+        at = side * (self.count - 1) + k
+        block = self.blocks.at[self.z + way * (self.count - 1 - k)]
+        return send(block, self.came.at[at], self.out_sems.at[at], self.in_sems.at[at], self.along(self.z + way))
+
+    def start(self, k):
+        for side, way, sends, _ in self.sides(k):
+            @pl.when(sends)
+            def _():
+                self.copy(side, way, k).start()
+
+    def take(self, k, total):
+        final = k == self.count - 2
+        for side, way, _, comes in self.sides(k):
+            at = side * (self.count - 1) + k
+
+            @pl.when(comes)
+            def _():
+                land = self.came.at[at]
+                send(land, land, self.out_sems.at[at], self.in_sems.at[at], self.along(self.z - way)).wait_recv()
+
+                def add(rows):
+                    value = self.came[at, rows, :].astype(F32)
+                    if final:
+                        total[rows, :] += value
+                    else:
+                        spot = self.z + way * (self.count - 2 - k)
+                        self.blocks[spot, rows, :] = (self.blocks[spot, rows, :].astype(F32) + value).astype(BF)
+
+                each_rows(total.shape[0], add)
+
+    def own(self, total):
+        def put(rows):
+            total[rows, :] = self.blocks[self.z, rows, :].astype(F32)
+
+        each_rows(total.shape[0], put)
+
+    def end(self):
+        for k in range(self.count - 1):
+            for side, way, sends, _ in self.sides(k):
+                @pl.when(sends)
+                def _():
+                    self.copy(side, way, k).wait_send()
+
+
+N_CHAIN = 5
+
+
+def last_backward(n_lo, n_cx, n_hi, with_out, part, sums, *refs):
+    if with_out:
+        out_part, inputs, hidden_grad, gain, hidden, input_grad, gain_grad, summed, mate_a, output, mate_b, *scratch = refs
+    else:
+        inputs, hidden_grad, gain, hidden, input_grad, gain_grad, summed, mate_a, *scratch = refs
+    fold_a, rest = scratch[:N_FOLD], scratch[N_FOLD:]
+    chain_s, fold_b = rest[:N_CHAIN], rest[N_CHAIN:]
+    cube = Group(n_lo, n_cx, True)
+    plane = Group(n_lo, n_cx, False)
+    n_dp = n_hi * n_lo
+    z = lax.axis_index("hi") * n_lo + lax.axis_index("lo")
+    along = lambda d: {"hi": d // n_lo, "lo": lax.rem(d, n_lo)}
+    meet([cube.partner(b) for b in cube.near] + [sibling()] + [along(lax.rem(z + i, n_dp)) for i in range(1, n_dp)])
+    first = Fold(plane, part, mate_a, fold_a)
+    chain = Chain(z, n_dp, sums, chain_s[0], chain_s[1], chain_s[2:], along)
+    chain.begin()
+    first.begin()
+    if with_out:
+        outs = Fold(cube, out_part, mate_b, fold_b)
+        outs.begin()
+    hops = n_dp - 1
+    chain.ready()
+    chain.start(0)
+    chain.own(summed)
+    first.pairs()
+    if with_out:
+        outs.pairs()
+    first.take(0)
+    for k in range(hops - 1):
+        chain.take(k, summed)
+        chain.start(k + 1)
+        if with_out and k + 1 < len(cube.bits):
+            outs.take(k)
+        if k + 1 < len(plane.bits):
+            first.take(k + 1)
+    for s in range(hops, len(plane.bits)):
+        first.take(s)
+    gain_grad[...] = jnp.zeros_like(gain_grad)
+
+    def norm(at):
+        norm_back(inputs, gain, first.total, hidden_grad, input_grad, gain_grad, at)
+
+    each_rows(first.rows, norm)
+    if with_out:
+        for s in range(min(hops - 1, len(cube.bits) - 1), len(cube.bits)):
+            outs.take(s)
+
+        def finish(at):
+            output[at, :] = hidden[at, :] + outs.total[at, :]
+
+        each_rows(outs.rows, finish)
+    chain.take(hops - 1, summed)
+    first.end()
+    if with_out:
+        outs.end()
+    chain.end()
+
+
+def comm_call(kernel, name, number, raw, args, outs, scratch, micros):
+    any_spec = pl.BlockSpec(memory_space=pl.ANY)
+    vmem = pl.BlockSpec(memory_space=pltpu.VMEM)
+    return pl.pallas_call(
+        kernel,
+        in_specs=[any_spec] * len(raw) + [vmem] * len(args),
+        out_specs=[vmem if inside else any_spec for _, inside in outs],
+        out_shape=[shape for shape, _ in outs],
+        scratch_shapes=scratch,
+        compiler_params=pltpu.CompilerParams(
+            collective_id=number, has_side_effects=True, vmem_limit_bytes=56 << 20
+        ),
+        cost_estimate=pl.CostEstimate(flops=micros * 10**9, bytes_accessed=micros * 10**6, transcendentals=0),
+        name=name,
+    )(*raw, *args)
+
+
+def dma_sems(*counts):
+    return [pltpu.SemaphoreType.DMA((n,) if n else ()) for n in counts]
+
+
+def middle_forward_call(n_lo, n_cx, part, inputs, gain):
+    tok, width = inputs.shape
+    near = n_cx.bit_length() - 1
+    far = near + n_lo - 1
+    rows = jax.ShapeDtypeStruct((tok, width), F32)
+    sds = lambda *shape: jax.ShapeDtypeStruct(shape, BF)
+    hidden, second_all, _ = comm_call(
+        functools.partial(middle_forward, n_lo, n_cx), "sum_norm_gather_forward", 1,
+        (part.reshape(n_cx, 2, tok, width),), (inputs, gain),
+        [(rows, True), (sds(n_lo * n_cx * 2, tok, width), False), (sds(n_cx, tok, width), False)],
+        Fold.scratch(near, near, tok, width) + Spread.sems(far, far) + [pltpu.VMEM((tok, width), BF)], 1,
+    )
+    return hidden, second_all.reshape(-1, width)
+
+
+def middle_backward_call(n_lo, n_cx, part, hidden, out_grad, gain):
+    tok, width = hidden.shape
+    near = n_cx.bit_length() - 1
+    far = near + n_lo - 1
+    rows = jax.ShapeDtypeStruct((tok, width), F32)
+    sds = lambda *shape: jax.ShapeDtypeStruct(shape, BF)
+    hidden_grad, gain_grad, branch_all, _ = comm_call(
+        functools.partial(middle_backward, n_lo, n_cx), "sum_norm_gather_backward", 2,
+        (part.reshape(n_lo * n_cx, 2, tok, width),), (hidden, out_grad, gain),
+        [(rows, True), (jax.ShapeDtypeStruct((8, width), F32), True), (sds(n_cx * 2, tok, width), False),
+         (sds(n_lo * n_cx, tok, width), False)],
+        Fold.scratch(far, far, tok, width) + Spread.sems(near, near) + [pltpu.VMEM((tok, width), BF)], 100,
+    )
+    return hidden_grad, gain_grad, branch_all.reshape(-1, width)
+
+
+def last_backward_call(n_hi, n_lo, n_cx, part, out_part, sums, inputs, hidden_grad, gain, hidden):
+    tok, width = inputs.shape
+    near = n_cx.bit_length() - 1
+    far = near + n_lo - 1
+    n_dp = n_hi * n_lo
+    with_out = n_lo * n_cx <= 8
+    rows = jax.ShapeDtypeStruct((tok, width), F32)
+    sds = lambda *shape: jax.ShapeDtypeStruct(shape, BF)
+    sums = sums.reshape(n_dp, -1, sums.shape[1])
+    raw = (part.reshape(n_cx, 2, tok, width), sums)
+    outs = [(rows, True), (jax.ShapeDtypeStruct((8, width), F32), True),
+            (jax.ShapeDtypeStruct(sums.shape[1:], F32), True), (sds(n_cx, tok, width), False)]
+    scratch = Fold.scratch(near, near, tok, width) + Chain.scratch(*sums.shape)
+    if with_out:
+        raw += (out_part.reshape(n_lo * n_cx, 2, tok, width),)
+        outs += [(rows, True), (sds(n_lo * n_cx, tok, width), False)]
+        scratch += Fold.scratch(far, far, tok, width)
+    got = comm_call(
+        functools.partial(last_backward, n_lo, n_cx, n_hi, with_out), "sum_norm_backward", 3,
+        raw, (inputs, hidden_grad, gain, hidden), outs, scratch, 1,
+    )
+    input_grad, gain_grad, summed = got[:3]
+    if with_out:
+        output = got[4]
+    else:
+        output = hidden + lax.psum_scatter(out_part, CUBE, scatter_dimension=0, tiled=True).astype(F32)
+    return input_grad, gain_grad, output, summed
+
+
+class Line:
+    def __init__(self, n_hi, n_lo):
+        self.n_lo = n_lo
+        self.count = n_hi * n_lo
+        self.z = lax.axis_index("hi") * n_lo + lax.axis_index("lo")
+
+    def device(self, z):
+        return {"hi": z // self.n_lo, "lo": lax.rem(z, self.n_lo)}
+
+    def run(self, part, sems, k, action):
+        out_sems, in_sems, pass_sems, mate_sems = sems
+        last = self.count - 1
+        z = self.z
+        for side, way in ((0, 1), (1, -1)):
+            if way == 1:
+                sends = jnp.logical_and(z >= k, z < last)
+                comes = z >= k + 1
+            else:
+                sends = jnp.logical_and(z <= last - k, z > 0)
+                comes = z <= last - 1 - k
+            at = side * last + k
+            if action in ("recv", "mate_recv"):
+                @pl.when(comes)
+                def _():
+                    if action == "recv":
+                        plane = part(z - way * (k + 1), False)
+                        send(plane, plane, out_sems.at[at], in_sems.at[at], self.device(z - way)).wait_recv()
+                        if pass_sems is not None:
+                            send(plane, plane, pass_sems.at[at], mate_sems.at[at], sibling()).start()
+                    else:
+                        plane = part(z - way * (k + 1), False)
+                        send(plane, plane, pass_sems.at[at], mate_sems.at[at], sibling()).wait_send()
+                        plane = part(z - way * (k + 1), True)
+                        send(plane, plane, pass_sems.at[at], mate_sems.at[at], sibling()).wait_recv()
+            else:
+                @pl.when(sends)
+                def _():
+                    plane = part(z - way * k, False)
+                    copy = send(plane, plane, out_sems.at[at], in_sems.at[at], self.device(z + way))
+                    if action == "start":
+                        copy.start()
+                    else:
+                        copy.wait_send()
+
+
+def clamp_head(head, top):
+    return head - head // (top + 1) * (head - top)
+
+
+def window_head(c, own_ch, bw, span):
+    return clamp_head(own_ch * c // bw, HEADS - span)
+
+
+def chip_head(chip, own_ch, bw, span):
+    return clamp_head(window_head(2 * chip, own_ch, bw, span), HEADS - span - 1)
+
+
+def window_shard(head, n_dev, n_ctx, span):
+    return head * ((n_dev - n_ctx) // (HEADS - span))
+
+
+def gather_start(sizes, gelu_w, lin_w, proj, rgate, igate, normed, down, gate_w, up_w,
+                 gl_out, gu_out, pg_z, pg_win, normed_all, down_other,
+                 gu_send, own_pg, own_gl, own_rest, gl_s, gl_r, mate_s, mate_r, gu_s, gu_r, win_s, win_r,
+                 zp_s, zp_r, zg_s, zg_r, zm_s, zm_r, dn_s, dn_r, *spread_s):
+    n_hi, n_lo, n_cx, n_core, own_ch, bw, span = sizes
+    n_ctx = n_cx * n_core
+    n_cube = n_lo * n_ctx
+    n_dev = n_hi * n_cube
+    hi = lax.axis_index("hi")
+    lo = lax.axis_index("lo")
+    cx = lax.axis_index("cxy")
     core = lax.axis_index("core")
-    blocks = partial.reshape((-1, 2, tok) + partial.shape[1:])
-    mine = lax.dynamic_index_in_dim(blocks, core, 1, keepdims=False)
-    away = lax.dynamic_index_in_dim(blocks, 1 - core, 1, keepdims=False)
-    got = lax.ppermute(away, "core", SWAP)
-    pair = (mine.astype(F32) + got.astype(F32)).astype(BF)
-    return jnp.sum(exchange(pair, axes).astype(F32), axis=0)
+    ctx = cx * n_core + core
+    spot = lo * n_ctx + ctx
+    number = hi * n_cube + spot
+    line = Line(n_hi, n_lo)
+    z = line.z
+    wide = (span + 1) * bw
+    width = proj.shape[1]
+    in_plane = lambda c: {"cxy": c // n_core, "core": lax.rem(c, n_core)}
+    in_cube = lambda u: {"lo": u // n_ctx, **in_plane(lax.rem(u, n_ctx))}
+
+    barrier = pltpu.get_barrier_semaphore()
+
+    def greet(i, held):
+        other = lax.rem(number + i, n_dev)
+        pl.semaphore_signal(
+            barrier, inc=1, device_id={"hi": other // n_cube, **in_cube(lax.rem(other, n_cube))},
+            device_id_type=pl.DeviceIdType.MESH,
+        )
+        return held
+
+    lax.fori_loop(1, n_dev, greet, 0)
+    pl.semaphore_wait(barrier, n_dev - 1)
+
+    pg_parts = [(proj, 0, width), (rgate, width, bw), (igate, width + bw, bw)]
+    pg_own = [
+        pltpu.make_async_copy(ref, pg_z.at[z, :, pl.ds(a, n)], own_pg.at[i]) for i, (ref, a, n) in enumerate(pg_parts)
+    ]
+    for copy in pg_own:
+        copy.start()
+
+    def columns(ref, chip):
+        at = pl.multiple_of(chip_head(chip, own_ch, bw, span) * bw, bw)
+        return ref.at[:, pl.ds(at, wide)]
+
+    mine = lambda i: gl_out.at[z, cx, core, :, pl.ds(i * wide, wide)]
+    gl_own = [pltpu.make_async_copy(columns(ref, cx), mine(i), own_gl.at[i]) for i, ref in enumerate((gelu_w, lin_w))]
+    gl_copies = []
+    for s in range(1, n_cx):
+        to = lax.rem(cx + s, n_cx)
+        for i, ref in enumerate((gelu_w, lin_w)):
+            gl_copies.append(
+                send(columns(ref, to), mine(i), gl_s.at[2 * s + i], gl_r.at[2 * s + i], {"cxy": to})
+            )
+            gl_copies[-1].start()
+    for copy in gl_own:
+        copy.start()
+    pg_part = lambda plane, other: pg_z.at[plane]
+    gl_part = lambda plane, other: gl_out.at[plane, :, 1 - core if other else core]
+    pg_sems, gl_sems = (zp_s, zp_r, None, None), (zg_s, zg_r, zm_s, zm_r)
+    steps = line.count - 1
+    for copy in pg_own:
+        copy.wait()
+    line.run(pg_part, pg_sems, 0, "start")
+    rows = Spread(Group(n_lo, n_cx, False), normed, normed_all, spread_s)
+    rows.begin()
+    for copy in gl_own:
+        copy.wait()
+    for s in range(1, n_cx):
+        for i in range(2):
+            came = gl_out.at[z, lax.rem(cx - s + n_cx, n_cx), core, :, pl.ds(i * wide, wide)]
+            send(came, came, gl_s.at[2 * s + i], gl_r.at[2 * s + i], {"cxy": lax.rem(cx + s, n_cx)}).wait_recv()
+    line.run(gl_part, gl_sems, 0, "start")
+    own_plane = gl_part(z, False)
+    own_mate = send(own_plane, own_plane, mate_s, mate_r, sibling())
+    own_mate.start()
+
+    ff_own = gate_w.shape[1] // n_cube
+    ff_pad = gu_send.shape[2] // 2
+    shard_rows = gate_w.shape[0]
+    for u in range(n_cube):
+        first = (u % n_ctx) * (n_lo * ff_own) + (u // n_ctx) * ff_own
+        for i, ref in enumerate((gate_w, up_w)):
+            gu_send[u, :, i * ff_pad : i * ff_pad + ff_own] = ref[:, first : first + ff_own]
+            if ff_pad > ff_own:
+                gu_send[u, :, i * ff_pad + ff_own : (i + 1) * ff_pad] = jnp.zeros((shard_rows, ff_pad - ff_own), BF)
+
+    for k in range(1, steps):
+        line.run(pg_part, pg_sems, k - 1, "recv")
+        line.run(pg_part, pg_sems, k, "start")
+    for s in range(len(rows.moves)):
+        rows.step(s)
+    line.run(pg_part, pg_sems, steps - 1, "recv")
+
+    def window(src, dst):
+        first = window_shard(window_head(dst, own_ch, bw, span), n_dev, n_ctx, span)
+        turn = lax.rem(src - first + n_dev, n_ctx)
+        return (first + turn) // n_ctx, turn
+
+    shard, turn = window(ctx, ctx)
+    own_window = pltpu.make_async_copy(pg_z.at[shard], pg_win.at[turn], own_rest.at[0])
+    own_window.start()
+    win_copies = []
+    for s in range(1, n_ctx):
+        to = lax.rem(ctx + s, n_ctx)
+        shard, turn = window(ctx, to)
+        win_copies.append(send(pg_z.at[shard], pg_win.at[turn], win_s.at[s], win_r.at[s], in_plane(to)))
+        win_copies[-1].start()
+    line.run(gl_part, gl_sems, 0, "recv")
+    if steps > 1:
+        line.run(gl_part, gl_sems, 1, "start")
+    own_gu = pltpu.make_async_copy(gu_send.at[spot], gu_out.at[spot], own_rest.at[1])
+    own_gu.start()
+    gu_copies = []
+    for s in range(1, n_cube):
+        to = lax.rem(spot + s, n_cube)
+        gu_copies.append(send(gu_send.at[to], gu_out.at[spot], gu_s.at[s], gu_r.at[s], in_cube(to)))
+        gu_copies[-1].start()
+    down_copy = send(down, down_other, dn_s, dn_r, across())
+    for k in range(2, steps):
+        line.run(gl_part, gl_sems, k - 1, "recv")
+        line.run(gl_part, gl_sems, k, "start")
+    down_copy.start()
+    line.run(gl_part, gl_sems, steps - 1, "recv")
+    rows.end()
+    for s in range(1, n_ctx):
+        _, turn = window(lax.rem(ctx - s + n_ctx, n_ctx), ctx)
+        came = pg_win.at[turn]
+        send(came, came, win_s.at[s], win_r.at[s], in_plane(lax.rem(ctx + s, n_ctx))).wait_recv()
+    for s in range(1, n_cube):
+        came = gu_out.at[lax.rem(spot - s + n_cube, n_cube)]
+        send(came, came, gu_s.at[s], gu_r.at[s], in_cube(lax.rem(spot + s, n_cube))).wait_recv()
+    own_window.wait()
+    own_gu.wait()
+    for copy in gl_copies + win_copies + gu_copies:
+        copy.wait_send()
+    own_mate.wait_send()
+    other_plane = gl_part(z, True)
+    send(other_plane, other_plane, mate_s, mate_r, sibling()).wait_recv()
+    for k in range(steps):
+        line.run(pg_part, pg_sems, k, "sent")
+        line.run(gl_part, gl_sems, k, "sent")
+        line.run(gl_part, gl_sems, k, "mate_recv")
+    down_copy.wait()
+
+
+def gather_start_call(sizes, gelu_w, lin_w, proj, rgate, igate, normed, down, gate_w, up_w, ff_pad):
+    n_hi, n_lo, n_cx, n_core, own_ch, bw, span = sizes
+    n_ctx = n_cx * n_core
+    n_cube = n_lo * n_ctx
+    n_dp = n_hi * n_lo
+    shard, width = proj.shape
+    near = n_cx.bit_length() - 1
+    wide = (span + 1) * bw
+    sds = lambda *shape: jax.ShapeDtypeStruct(shape, BF)
+    any_spec = pl.BlockSpec(memory_space=pl.ANY)
+    vmem = pl.BlockSpec(memory_space=pltpu.VMEM)
+    pg_width = width + 2 * bw
+    hops = 2 * (n_dp - 1)
+    gl_out, gu_out, _, pg_win, normed_all, down_other = pl.pallas_call(
+        functools.partial(gather_start, sizes),
+        in_specs=[any_spec] * 7 + [vmem] * 2,
+        out_specs=[any_spec] * 6,
+        out_shape=[
+            sds(n_dp, n_cx, n_core, shard, 2 * wide), sds(n_cube, shard, 2 * ff_pad), sds(n_dp, shard, pg_width),
+            sds(n_ctx, shard, pg_width), sds(n_ctx, *normed.shape), sds(*down.shape),
+        ],
+        scratch_shapes=[pltpu.VMEM((n_cube, shard, 2 * ff_pad), BF)]
+        + dma_sems(3, 2, 2, 2 * n_cx, 2 * n_cx, 0, 0, n_cube, n_cube, n_ctx, n_ctx, hops, hops, hops, hops, hops, hops, 0, 0)
+        + Spread.sems(near, near),
+        compiler_params=pltpu.CompilerParams(collective_id=4, has_side_effects=True, vmem_limit_bytes=40 << 20),
+        cost_estimate=pl.CostEstimate(flops=10**11, bytes_accessed=10**8, transcendentals=0),
+        name="gather_start",
+    )(gelu_w, lin_w, proj, rgate, igate, normed, down, gate_w, up_w)
+    return gl_out.reshape(width, 2 * wide), gu_out.reshape(-1, 2 * ff_pad), pg_win.reshape(-1, pg_width), normed_all.reshape(-1, width), down_other
+
+
+def swap_first(value):
+    return lax.ppermute(value, DP, [(0, 1), (3, 2)]), lax.ppermute(value, DP, [(1, 2), (2, 1)])
+
+
+def swap_second(to_inner, crossed):
+    return lax.ppermute(to_inner, DP, [(1, 2), (2, 1)]), lax.ppermute(crossed, DP, [(1, 0), (2, 3)])
 
 
 def pad_last(value, width):
@@ -299,11 +1084,9 @@
     bw = recur_gate_w.shape[1]
     hidden_units = mlp_gate_w.shape[1]
     own_ch = chans // n_ctx
-    starts = [own_ch * c // bw for c in range(n_ctx)]
-    span = max((own_ch * (c + 1) - 1) // bw - starts[c] + 1 for c in range(n_ctx))
-    starts = [min(s, HEADS - span) for s in starts]
+    span = max((own_ch * (c + 1) - 1) // bw - own_ch * c // bw + 1 for c in range(n_ctx))
     win = span * bw
-    head0 = jnp.array(starts, jnp.int32)[ctx]
+    head0 = window_head(ctx, own_ch, bw, span)
     ch0 = head0 * bw
     own_off = own_ch * ctx - ch0
     ff_own = hidden_units // (n_lo * n_ctx)
@@ -321,52 +1104,41 @@
     gain_first = small_all[0]
     gain_second = small_all[1]
 
-    windows = [
-        jnp.concatenate(
-            [gelu_in_w[:, s * bw : s * bw + win], linear_in_w[:, s * bw : s * bw + win]], axis=1
-        )
-        for s in starts
-    ]
-    gl_part = exchange(jnp.stack(windows), CTX).reshape(-1, 2 * win)
-    gl_w = lax.all_gather(gl_part, DP, axis=0, tiled=True)
-    gates_all = lax.all_gather(jnp.concatenate([recur_gate_w, input_gate_w], axis=1), EVERY, axis=0, tiled=True)
-    gates_win = lax.dynamic_slice_in_dim(gates_all, ch0, win)
-    recur_w = gates_win[:, :bw]
-    input_w = gates_win[:, bw:]
-    proj_all = lax.all_gather(out_proj_w, EVERY, axis=0, tiled=True)
-    proj_w = lax.dynamic_slice_in_dim(proj_all, ch0, win)
-
     r_first = lax.rsqrt(jnp.mean(inputs * inputs, axis=-1, keepdims=True) + 1e-06)
     normed = (inputs * r_first * gain_first).astype(BF)
-    normed_all = gather_rows(normed, "cxy")
-
-    down_grad = lax.all_gather(out_grad.astype(BF), CUBE, axis=0, tiled=True)
-
-    def columns(weight):
-        parts = weight.reshape(weight.shape[0], n_ctx, n_lo, ff_own).transpose(2, 1, 0, 3)
-        return pad_last(parts.reshape(n_lo * n_ctx, weight.shape[0], ff_own), ff_pad)
-
-    gu_send = jnp.concatenate([columns(mlp_gate_w), columns(mlp_up_w)], axis=2)
-    gu_mine = exchange(gu_send, CUBE).reshape(-1, 2 * ff_pad)
+
+    sizes = (n_hi, n_lo, n_cx, n_core, own_ch, bw, span)
+    gl_w, gu_mine, pg_win, normed_all, down_other = gather_start_call(
+        sizes, gelu_in_w, linear_in_w, out_proj_w, recur_gate_w, input_gate_w, normed, mlp_down_w,
+        mlp_gate_w, mlp_up_w, ff_pad,
+    )
+    wide = win + bw
+    chip_off = (head0 - chip_head(cx, own_ch, bw, span)) * bw
+    gelu_w = lax.dynamic_slice_in_dim(gl_w[:, :wide], chip_off, win, axis=1)
+    lin_w = lax.dynamic_slice_in_dim(gl_w[:, wide:], chip_off, win, axis=1)
+    pg_win = lax.dynamic_slice_in_dim(pg_win, ch0 - window_shard(head0, n_dev, n_ctx, span) * piece, win)
+    proj_w = pg_win[:, :width]
+    recur_w = pg_win[:, width : width + bw]
+    input_w = pg_win[:, width + bw :]
+
     gu_other = lax.ppermute(gu_mine, "hi", SWAP)
-    gu_w = in_order(hi, gu_mine, gu_other, 0)
-    down_other = lax.ppermute(mlp_down_w, "hi", SWAP)
     n_cube = n_lo * n_ctx
     half = n_cube // 2
     to_a, to_b = [], []
+    place = lambda t: (t % n_lo) * n_ctx + t // n_lo
     for q in range(n_cube):
         lower, upper = q // 2, q // 2 + half
         near, far = (lower, upper) if q % 2 == 0 else (upper, lower)
-        place = lambda t: (t % n_lo) * n_ctx + t // n_lo
         to_a.append((q, place(near)))
         to_b.append((q, place(far)))
-    odd = core
-    same = hi == odd
+    same = hi == core
     down_a = lax.ppermute(jnp.where(same, mlp_down_w, down_other), CUBE, to_a)
     down_b = lax.ppermute(jnp.where(same, down_other, mlp_down_w), CUBE, to_b)
     slot = ctx * n_lo + lo
     down_w = in_order((slot >= half).astype(jnp.int32), down_a, down_b, 0)
     down_w = jnp.pad(down_w, ((0, ff_pad - ff_own), (0, 0)))
+    cot = lax.optimization_barrier((out_grad.astype(BF), down_other))[0]
+    down_grad = lax.all_gather(cot, CUBE, axis=0, tiled=True)
 
     ids = segment_ids[0]
     metas = [jnp.concatenate([jnp.ones((1,), F32), (ids[1:] != ids[:-1]).astype(F32)])]
@@ -387,17 +1159,13 @@
         ],
         axis=0,
     )
-    gelu_pre = dot(normed_all, gl_w[:, :win], 1, 0)
-    linear_out = dot(normed_all, gl_w[:, win:], 1, 0).astype(BF)
+    gelu_pre = dot(normed_all, gelu_w, 1, 0)
+    linear_out = dot(normed_all, lin_w, 1, 0).astype(BF)
     mixed, prev, conv_out, rec, inp = forward_call(linear_out, gelu_pre, meta, vecs, recur_w, input_w)
     proj_part = dot(mixed, proj_w, 1, 0).astype(BF)
-    hidden = inputs + scatter_sum(proj_part, "cxy", tok)
-    mixed_own = lax.dynamic_slice_in_dim(mixed, own_off, own_ch, axis=1)
-    mixed_all = lax.all_gather(mixed_own, CTX, axis=0, tiled=False)
-
-    r_second = lax.rsqrt(jnp.mean(hidden * hidden, axis=-1, keepdims=True) + 1e-06)
-    second = (hidden * r_second * gain_second).astype(BF)
-    second_all = gather_rows(second, ("lo", "cxy"))
+    hidden, second_all = middle_forward_call(n_lo, n_cx, proj_part, inputs, gain_second[None])
+    gu_w = in_order(hi, gu_mine, gu_other, 0)
+
     pre = dot(second_all, gu_w, 1, 0)
     gate_pre, up_pre = pre[:, :ff_pad], pre[:, ff_pad:]
     act_grad = dot(down_grad, down_w, 1, 1)
@@ -405,47 +1173,40 @@
     activation = (gel * up_pre).astype(BF)
     gu_low = jnp.concatenate([(act_grad * up_pre * slope).astype(BF), (act_grad * gel).astype(BF)], axis=1)
     second_part = dot(gu_low, gu_w, 1, 1).astype(BF)
-    second_grad = scatter_sum(second_part, ("lo", "cxy"), tok)
-    out_part = dot(activation, down_w, 1, 0).astype(BF)
-    output = hidden + lax.psum_scatter(out_part, CUBE, scatter_dimension=0, tiled=True).astype(F32)
-
     grad_gu = dot(second_all, gu_low, 0, 0).astype(BF)
     grad_down = dot(activation, down_grad, 0, 0).astype(BF)
 
-    def settle(partial, axis):
-        size = partial.shape[axis] // n_hi
-        mine = lax.dynamic_slice_in_dim(partial, hi * size, size, axis)
-        away = lax.dynamic_slice_in_dim(partial, (1 - hi) * size, size, axis)
-        both = (mine.astype(F32) + lax.ppermute(away, "hi", SWAP).astype(F32)).astype(BF)
-        if n_lo == 1:
-            return both, None
-        size = size // n_lo
-        mine = lax.dynamic_slice_in_dim(both, lo * size, size, axis)
-        away = lax.dynamic_slice_in_dim(both, (1 - lo) * size, size, axis)
-        return mine, lax.ppermute(away, "lo", SWAP)
-
-    gu_a, gu_b = settle(grad_gu, 0)
-    dn_a, dn_b = settle(grad_down, 1)
-    grad_gate = in_order(lo, gu_a[:, :ff_own], gu_b[:, :ff_own], 1).astype(F32)
-    grad_up = in_order(
-        lo, gu_a[:, ff_pad : ff_pad + ff_own], gu_b[:, ff_pad : ff_pad + ff_own], 1
-    ).astype(F32)
-    grad_dn = in_order(lo, dn_a[:ff_own], dn_b[:ff_own], 0).astype(F32)
-
-    hidden_part, grad_gain_two = rms_back(hidden, gain_second, second_grad)
-    hidden_grad = out_grad + hidden_part
-    branch = hidden_grad.astype(BF)
-    branch_all = gather_rows(branch, "cxy")
-
+    def half_of(partial, which, axis, parts):
+        size = partial.shape[axis] // parts
+        return lax.dynamic_slice_in_dim(partial, which * size, size, axis)
+
+    gu_stage = swap_first(half_of(grad_gu, 1 - hi, 0, n_hi))
+    dn_stage = swap_first(half_of(grad_down, 1 - hi, 1, n_hi))
+    hidden_grad, gain_two_rows, branch_all = middle_backward_call(
+        n_lo, n_cx, second_part, hidden, out_grad, gain_second[None]
+    )
+
+    branch_all, *stages = lax.optimization_barrier((branch_all,) + gu_stage + dn_stage)
+    dn_stage = swap_second(*stages[2:])
+    gu_stage = swap_second(*stages[:2])
+    inner = hi != lo
+
+    def settle(partial, got, axis):
+        both = (half_of(partial, hi, axis, n_hi).astype(F32) + got.astype(F32)).astype(BF)
+        return half_of(both, lo, axis, n_lo), lax.ppermute(half_of(both, 1 - lo, axis, n_lo), "lo", SWAP)
+
+    out_part = dot(activation, lax.optimization_barrier((down_w, gain_two_rows))[0], 1, 0).astype(BF)
+
+    own_mixed = lax.dynamic_slice_in_dim(mixed, own_off, own_ch, axis=1)
+    grad_proj = dot(own_mixed, branch_all, 0, 0).astype(BF).reshape(own_ch, n_ctx, width // n_ctx)
+    grad_proj = exchange(grad_proj.transpose(1, 0, 2), CTX).reshape(chans, width // n_ctx)
     mixed_grad = dot(branch_all, proj_w, 1, 1)
     gelu_low, linear_low, recur_wg, input_wg, sums = backward_call(
         mixed_grad, gelu_pre, conv_out, rec, inp, prev, linear_out, meta, vecs, recur_w, input_w
     )
-    branch_cols = lax.dynamic_slice_in_dim(branch_all, ctx * (width // n_ctx), width // n_ctx, axis=1)
-    grad_proj = jnp.einsum("ctr,td->crd", mixed_all, branch_cols, preferred_element_type=F32)
-    grad_proj = grad_proj.reshape(chans, width // n_ctx).astype(BF)
-    grad_proj = lax.psum_scatter(grad_proj, DP, scatter_dimension=0, tiled=True).astype(F32)
-    lows = jnp.concatenate([gelu_low, linear_low], axis=1)
+    gelu_low, linear_low, *dn_stage = lax.optimization_barrier((gelu_low, linear_low) + dn_stage)
+    got_dn = jnp.where(inner, *dn_stage)
+    got_gu = jnp.where(inner, *gu_stage)
     own_lows = jnp.concatenate(
         [
             lax.dynamic_slice_in_dim(gelu_low, own_off, own_ch, axis=1),
@@ -454,11 +1215,21 @@
         axis=1,
     )
     grad_gl = dot(normed_all, own_lows, 0, 0).astype(BF)
-    grad_gl = lax.psum_scatter(grad_gl, DP, scatter_dimension=0, tiled=True).astype(F32)
-    first_part = dot(lows, gl_w, 1, 1).astype(BF)
-    first_grad = scatter_sum(first_part, "cxy", tok)
-    input_part, grad_gain_one = rms_back(inputs, gain_first, first_grad)
-    input_grad = hidden_grad + input_part
+    first_part = (dot(gelu_low, gelu_w, 1, 1) + dot(linear_low, lin_w, 1, 1)).astype(BF)
+    grad_three = jnp.concatenate([grad_gl, grad_proj], axis=1)
+    dn_a, dn_b = settle(grad_down, got_dn, 1)
+    gu_a, gu_b = settle(grad_gu, got_gu, 0)
+    first_part, dn_a, gu_a = lax.optimization_barrier((first_part, dn_a, gu_a))
+    input_grad, gain_one_rows, output, grad_three = last_backward_call(
+        n_hi, n_lo, n_cx, first_part, out_part, grad_three, inputs, hidden_grad, gain_first[None], hidden
+    )
+    grad_gl = grad_three[:, : 2 * own_ch]
+    grad_proj = grad_three[:, 2 * own_ch :]
+    grad_gate = in_order(lo, gu_a[:, :ff_own], gu_b[:, :ff_own], 1).astype(F32)
+    grad_up = in_order(
+        lo, gu_a[:, ff_pad : ff_pad + ff_own], gu_b[:, ff_pad : ff_pad + ff_own], 1
+    ).astype(F32)
+    grad_dn = in_order(lo, dn_a[:ff_own], dn_b[:ff_own], 0).astype(F32)
 
     packed = jnp.concatenate([recur_wg, input_wg, pad_last(sums.T, 128)], axis=1)
     packed = lax.dynamic_slice_in_dim(packed, own_off, own_ch, axis=0)
@@ -468,7 +1239,7 @@
     grad_recur_w = packed[:, :bw]
     grad_input_w = packed[:, bw : 2 * bw]
     rest = packed[:, 2 * bw : 2 * bw + 8].T
-    gains = jnp.stack([grad_gain_one, grad_gain_two]).reshape(2, n_dev, piece).transpose(1, 0, 2)
+    gains = jnp.stack([jnp.sum(gain_one_rows, axis=0), jnp.sum(gain_two_rows, axis=0)]).reshape(2, n_dev, piece).transpose(1, 0, 2)
     gains = jnp.sum(exchange(gains, EVERY), axis=0)
 
     return (

time: 1280 us -> 958 us (0.75)
  waiting for transfers between devices: 803 us -> 28.6 us
  Pallas kernels: 29.9 us -> 611 us
  blocking collectives: 61.7 us -> 0 us
  other arithmetic: 78.3 us -> 34.1 us
  local copies, waits for them, and re-layouts: 89.6 us -> 58.3 us
    pallas_call x0 -> x4, Pallas kernels: none -> 581 us  [the longest x3 417 us: comm_call(): pl.pallas_call(kernel, in_specs=[any_spec] * len(raw) + [vmem] * len(args...]
    ppermute x11 -> x10, waiting for transfers between devices: 241 us -> 2.34 us  [the longest x2 2.32 us: settle(): lax.ppermute(half_of(both, 1 - lo, axis, n_lo), 'lo', SWAP)]
    all_to_all x9 -> x4, waiting for transfers between devices: 239 us -> 2.65 us  [exchange(): return lax.all_to_all(value, axes, split_axis=0, concat_axis=0, tiled=True)]
    all_gather x5 -> x1, waiting for transfers between devices: 149 us -> 0.01 us  [per_device(): down_grad = lax.all_gather(cot, CUBE, axis=0, tiled=True)]
    ppermute x1, waiting for transfers between devices: 72.3 us -> 0.01 us  [per_device(): gu_other = lax.ppermute(gu_mine, 'hi', SWAP)]
    reduce_scatter x2 -> x0, waiting for transfers between devices: 65.2 us -> none  [the longest x1 65.2 us: per_device(): lax.psum_scatter(out_part, CUBE, scatter_dimension=0, tiled=True)]
    all_to_all x2 -> x0, blocking collectives: 61.7 us -> none  [exchange(): return lax.all_to_all(value, axes, split_axis=0, concat_axis=0, tiled=True)]
    select_n x3 -> x0, local copies, waits for them, and re-layouts: 26 us -> none  [in_order(): jnp.where(flag == 0, jnp.concatenate([mine, other], axis=axis), jnp.conca...]
  transfers between devices with their start and end apart: 32 -> 19, of which waited for: 21 -> 3; matrix products, arithmetic and copies ran while one was open for 18% -> 16% of each run, Pallas kernels for 2% -> 47%
where the time goes in v3:
time: 958 us; the launch traced here: 948 us
  Pallas kernels  611 us (64%)
  matrix products  131 us (14%)
  starting transfers between devices  68.7 us (7%)
  local copies, waits for them, and re-layouts  58.3 us (6%)
  other arithmetic  34.1 us (4%)
  waiting for transfers between devices  28.6 us (3%)
  between operations  15.6 us (2%)
    pallas_call x3, Pallas kernels, comm_call(): pl.pallas_call(kernel, in_specs=[any_spec] * len(raw) + [vmem] * len(args...  417 us
    pallas_call x1, Pallas kernels, gather_start_call(): pl.pallas_call(functools.partial(gather_start, sizes), in_specs=[any_spec...  164 us
    dot_general x14, matrix products, dot(): lax.dot_general(a, b, (((ca,), (cb,)), ((), ())), preferred_element_type=...  131 us
    all_to_all x4, starting transfers between devices, exchange(): return lax.all_to_all(value, axes, split_axis=0, concat_axis=0, tiled=True)  32.1 us
    unnamed x119, local copies, waits for them, and re-layouts  26.5 us
    ppermute x1, waiting for transfers between devices, per_device(): packed = lax.ppermute(packed, EVERY, routes)  23.6 us
    pallas_call x1, Pallas kernels, backward_call(): pl.pallas_call(backward_kernel, grid=grid, in_specs=[tok] * 7 + [mspec, v...  19.5 us
  transfers between devices with their start and end apart: 19, of which 3 were waited for; matrix products, arithmetic and copies ran while one was open for 16% of the time, Pallas kernels for 47%

profile of v3, /device:TPU:1, one launch (start us, length us, event | category | flops | bytes accessed | tf_op | source)
XLA Modules:
  0.0 947.6 jit_solution(17420894568901103827)
XLA Ops:
  9.5 7.1 all-to-all-start
  28.8 164.2 %gather_start.1 = (bf16[4,4,2,80,1536]{4,3,2,1,0:T(8,128)(2,1)}, bf16[16,80,1024]{2,1,0:T(8,128)(2,1)S(1)}, bf16[4,80,3072]{2,1,0:T(8,128)(2,1)}, bf16[8,80,3072...) custom-call(bf16[80,2560]{1,0:T(8,128)(2,1)S(1)} %copy-done.24, ...), custom_call_target="tpu_custom_call" | custom-call | flops 99999997952 | bytes 100000000 | tf_op jit(solution)/shard_map/gather_start/pallas_call | solution.py:1040
  204.3 8.2 collective-permute-start.1
  213.4 3.8 fusion.39
  218.0 7.2 fusion.5.gpre_ref
  228.2 10.3 %recur_forward.1 = (bf16[1024,512]{1,0:T(8,128)(2,1)S(1)}, f32[1024,512]{1,0:T(8,128)S(1)}, f32[1024,512]{1,0:T(8,128)S(1)}, f32[1024,512]{1,0:T(8,128)S(1)}, f32[1024,512]{1,0:T(8,128)S(1)}) custom-call(bf16[1024,512]{1,0:T(8,128)(2,1)S(1)} %fusion.11.lin_ref, f32[1024,512]{1,0:T(8,128)S(1)} %fusion.5.gpre_ref, f32[1024,4]{1,0:T(8,128)S(1)} %stack.35.meta_ref, ...), custom_call_target="tpu_custom_call" | custom-call | flops 589299712 | bytes 12582912 | tf_op jit(solution)/shard_map/recur_forward/pallas_call | solution.py:190
  238.5 4.7 convolution_convert_fusion.2
  243.2 166.7 %sum_norm_gather_forward.1 = (f32[128,2560]{1,0:T(8,128)}, bf16[16,128,2560]{2,1,0:T(8,128)(2,1)}, bf16[4,128,2560]{2,1,0:T(8,128)(2,1)}) custom-call(bf16[4,2,128,2560]{3,2,1,0:T(8,128)(2,1)} %bitcast.58, f32[128,2560]{1,0:T(8,128)} %refs_1_.1, f32[1,2560]{1,0:T(1,128)} %slice.148.gain), custom_call_target="tpu_custom_call" | custom-call | flops 1000000000 | bytes 1000000 | tf_op jit(solution)/shard_map/sum_norm_gather_forward/pallas_call | solution.py:741
  410.0 3.7 maximum_select_fusion.1
  413.7 3.4 pad.12
  417.1 19.4 %fusion.20 = f32[2048,1024]{0,1:T(8,128)} fusion(bf16[2048,2560]{1,0:T(8,128)(2,1)} %bitcast.74, bf16[1280,1024]{1,0:T(8,128)(2,1)} %collective-permute-done.2, bf16[1280,1024]{1,0:T(8,128)(2,1)} %bitcast.52, pred[]{:T(512)S(6)} %eq.31), kind=kOutput, calls=%fused_computation.48 | convolution fusion | flops 10761011200 | bytes 24117248 | tf_op jit(solution)/shard_map/dot_general | solution.py:24
  436.5 15.0 %multiply_convert_fusion.2 = (bf16[2048,512]{0,1:T(8,128)(2,1)}, bf16[2048,512]{0,1:T(8,128)(2,1)}, bf16[2048,512]{0,1:T(8,128)(2,1)}) fusion(f32[2048,1024]{0,1:T(8,128)} %fusion.20, bf16[2048,2560]{1,0:T(8,128)(2,1)} %all-gather.2.cloned.1.call-done, bf16[480,2560]{1,0:T(8,128)(2,1)} %maximum_select_fusion.1), kind=kOutput, calls=%fused_computation.13 | convolution fusion | flops 5393874944 | bytes 27623424 | tf_op jit(solution)/shard_map/dot_general | solution.py:24
  451.5 15.7 %convolution_convert_fusion.3 = bf16[2560,1024]{1,0:T(8,128)(2,1)S(1)} fusion(bf16[2048,2560]{1,0:T(8,128)(2,1)} %bitcast.75, bf16[2048,512]{0,1:T(8,128)(2,1)} %get-tuple-element.153, bf16[2048,512]{0,1:T(8,128)(2,1)} %get-tuple-element.152), kind=kOutput, calls=%fused_computation.4 | convolution fusion | flops 10748428288 | bytes 19922944 | tf_op jit(solution)/shard_map/dot_general | solution.py:24
  470.5 4.4 collective-permute-start.3
  477.0 5.8 convolution_convert_fusion.5
  489.6 19.3 %convolution_convert_fusion.1 = bf16[2048,2560]{1,0:T(8,128)(2,1)} fusion(bf16[2048,512]{0,1:T(8,128)(2,1)} %get-tuple-element.153, bf16[2048,512]{0,1:T(8,128)(2,1)} %get-tuple-element.152, bf16[1280,1024]{1,0:T(8,128)(2,1)} %collective-permute-done.2, bf16[1280,1024]{1,0:T(8,128)(2,1)} %bitcast.53, pred[]{:T(512)S(6)} %eq.31), kind=kOutput, calls=%fused_computation.1 | convolution fusion | flops 10774642688 | bytes 19922944 | tf_op jit(solution)/shard_map/dot_general | solution.py:24
  508.9 104.5 %sum_norm_gather_backward.1 = (f32[128,2560]{1,0:T(8,128)}, f32[8,2560]{1,0:T(8,128)}, bf16[8,128,2560]{2,1,0:T(8,128)(2,1)}, bf16[8,128,2560]{2,1,0:T(8,128)(2,1)}) custom-call(bf16[8,2,128,2560]{3,2,1,0:T(8,128)(2,1)} %bitcast.76, f32[128,2560]{1,0:T(8,128)} %get-tuple-element.63.hidden.refs_4_, f32[128,2560]{1,0:T(8,128)} %out_grad.1, f32[1,2560]{1,0:T(1,128)} %slice.148.gain), custom_call_target="tpu_custom_call" | custom-call | flops 99999997952 | bytes 100000000 | tf_op jit(solution)/shard_map/sum_norm_gather_backward/pallas_call | solution.py:741
  614.5 5.8 fusion.1.mg_ref
  623.4 19.5 %recur_backward.1 = (bf16[1024,512]{1,0:T(8,128)(2,1)S(1)}, bf16[1024,512]{1,0:T(8,128)(2,1)S(1)}, f32[512,256]{1,0:T(8,128)S(1)}, f32[512,256]{1,0:T(8,128)S(1)}, f32[8,512]{1,0:T(8,128)S(1)}) custom-call(f32[1024,512]{1,0:T(8,128)S(1)} %fusion.1.mg_ref, f32[1024,512]{1,0:T(8,128)S(1)} %copy-done.1, f32[1024,512]{1,0:T(8,128)S(1)} %get-tuple-element.66.conv_ref, ...), custom_call_target="tpu_custom_call" | custom-call | flops 1152385024 | bytes 15728640 | tf_op jit(solution)/shard_map/recur_backward/pallas_call | solution.py:224
  647.7 15.3 %all-to-all-start.3 = ((f32[4,80,640]{2,1,0:T(8,128)}), f32[4,80,640]{2,1,0:T(8,128)S(1)}, u32[]{:S(2)}, u32[]{:S(2)}) async-start(f32[4,80,640]{2,1,0:T(8,128)} %bitcast.23), calls=%async_computation.3 | async-start | bytes 1638400 | tf_op jit(solution)/shard_map/all_to_all | solution.py:246
  663.0 10.6 %convolution_convert_fusion = bf16[2048,2560]{1,0:T(8,128)(2,1)} fusion(bf16[2048,512]{0,1:T(8,128)(2,1)} %get-tuple-element.154, bf16[512,2560]{1,0:T(8,128)(2,1)} %pad.12), kind=kOutput, calls=%fused_computation | convolution fusion | flops 5373952000 | bytes 15204352 | tf_op jit(solution)/shard_map/dot_general | solution.py:24
  685.1 4.2 all-to-all-start.1
  689.3 3.6 collective-permute-start.11
  696.2 4.8 collective-permute-start.13
  701.7 8.8 convolution_convert_fusion.4
  710.5 5.8 fusion.7
  716.3 7.2 add_convert_fusion
  723.5 5.0 pad_maximum_fusion.sums
  728.5 23.6 %collective-permute-done.11 = f32[80,640]{1,0:T(8,128)} collective-permute-done((f32[80,640]{1,0:T(8,128)S(1)}, f32[80,640]{1,0:T(8,128)}, u32[]{:S(2)}, u32[]{:S(2)}) %collective-permute-start.11) | collective-permute-done | bytes 204832 | tf_op jit(solution)/shard_map/ppermute | solution.py:1238
  755.2 4.4 add_convert_fusion.1
  764.9 145.8 %sum_norm_backward.1 = (f32[128,2560]{1,0:T(8,128)}, f32[8,2560]{1,0:T(8,128)}, f32[640,960]{1,0:T(8,128)}, bf16[4,128,2560]{2,1,0:T(8,128)(2,1)}, f32[128,2560]{1,0:T(8,128)}, /*index=5*/bf16[8,128,2560]{2,1,0:T(8,128)(2,1)}) custom-call(bf16[4,2,128,2560]{3,2,1,0:T(8,128)(2,1)} %bitcast.59, bf16[4,640,960]{2,1,0:T(8,128)(2,1)} %pad_maximum_fusion.sums, ...), custom_call_target="tpu_custom_call" | custom-call | flops 1000000000 | bytes 1000000 | tf_op jit(solution)/shard_map/sum_norm_backward/pallas_call | solution.py:741
  912.4 5.5 all-to-all-start.2
  (218 shorter events, 98.7 us)
Async XLA Ops:
  9.5 14.4 %all-to-all-start = ((bf16[32,2,400]{2,1,0:T(2,128)(2,1)}), bf16[32,2,400]{2,1,0:T(2,128)(2,1)S(1)}, u32[]{:S(2)}, u32[]{:S(2)}) async-start(bf16[32,2,400]{2,1,0:T(2,128)(2,1)} %reshape.167), calls=%async_computation | async-start | bytes 131072 | tf_op jit(solution)/shard_map/all_to_all | solution.py:246
  16.6 419.9 %all-gather.2.cloned.1.call-start = ((), (), s32[]{:S(2)}) async-start(), calls=%async_computation.4 | async-start | bytes 11141120 | tf_op jit(solution)/shard_map/all_gather | solution.py:1141
  28.7 167.0 %copy-start.44 = (s32[1,1024]{1,0:T(1,128)S(1)}, s32[1,1024]{1,0:T(1,128)}, u32[]{:S(2)}) copy-start(s32[1,1024]{1,0:T(1,128)} %param.19) | copy-start | bytes 12292
  198.6 218.5 %collective-permute-start.2 = (bf16[1280,1024]{1,0:T(8,128)(2,1)}, bf16[1280,1024]{1,0:T(8,128)(2,1)}, u32[]{:S(2)}, u32[]{:S(2)}) collective-permute-start(bf16[1280,1024]{1,0:T(8,128)(2,1)} %bitcast.51), channel_id=1, source_target_pairs={{0,16},{16,0},{1,17},{17,1},{2,18},{18,2},{3,19},{19,3},{4,20},{20... | collective-permute-start | bytes 7864328 | tf_op jit(solution)/shard_map/ppermute | solution.py:1124
  201.4 208.5 %collective-permute-start = (bf16[240,2560]{1,0:T(8,128)(2,1)}, bf16[240,2560]{1,0:T(8,128)(2,1)}, u32[]{:S(2)}, u32[]{:S(2)}) collective-permute-start(bf16[240,2560]{1,0:T(8,128)(2,1)} %get-tuple-element.164), channel_id=1, source_target_pairs={{0,0},{1,4},{2,8},{3,12},{4,1},{5,5},{6,9},{7,13},{8,2},{9,6},{10,... | collective-permute-start | bytes 3686408 | tf_op jit(solution)/shard_map/ppermute | solution.py:1135
  204.3 205.7 %collective-permute-start.1 = (bf16[240,2560]{1,0:T(8,128)(2,1)}, bf16[240,2560]{1,0:T(8,128)(2,1)}, u32[]{:S(2)}, u32[]{:S(2)}) collective-permute-start(bf16[240,2560]{1,0:T(8,128)(2,1)} %get-tuple-element.165), channel_id=1, source_target_pairs={{0,4},{1,0},{2,12},{3,8},{4,5},{5,1},{6,13},{7,9},{8,6},{9,2},{10,... | collective-permute-start | bytes 3686408 | tf_op jit(solution)/shard_map/ppermute | solution.py:1136
  213.4 14.8 %copy-start.19 = (f32[16,512]{1,0:T(8,128)}, f32[16,512]{1,0:T(8,128)S(1)}, u32[]{:S(2)}) copy-start(f32[16,512]{1,0:T(8,128)S(1)} %concatenate.75.vec_ref) | copy-start | bytes 98308
  218.0 10.2 %copy-start.8 = (bf16[512,256]{1,0:T(8,128)(2,1)}, bf16[512,256]{1,0:T(8,128)(2,1)S(1)}, u32[]{:S(2)}) copy-start(bf16[512,256]{1,0:T(8,128)(2,1)S(1)} %get-tuple-element.157.iw_ref) | copy-start | bytes 786436
  218.0 10.2 %copy-start.10 = (bf16[512,256]{1,0:T(8,128)(2,1)}, bf16[512,256]{1,0:T(8,128)(2,1)S(1)}, u32[]{:S(2)}) copy-start(bf16[512,256]{1,0:T(8,128)(2,1)S(1)} %get-tuple-element.158.rw_ref) | copy-start | bytes 786436
  228.1 10.3 %copy-start.12 = (bf16[1024,512]{1,0:T(8,128)(2,1)}, bf16[1024,512]{1,0:T(8,128)(2,1)S(1)}, u32[]{:S(2)}) copy-start(bf16[1024,512]{1,0:T(8,128)(2,1)S(1)} %fusion.11.lin_ref) | copy-start | bytes 3145732
  436.5 40.5 %slice-start.1 = ((s8[10485760]{0:T(1024)(128)(4,1)}), s8[4194304]{0:T(1024)(128)(4,1)S(1)}, s32[]{:S(2)}) async-start(s8[10485760]{0:T(1024)(128)(4,1)} %bitcast.72), calls=%async_computation.6 | async-start | bytes 8388608
  436.5 40.5 %slice-start.2 = ((s8[10485760]{0:T(1024)(128)(4,1)}), s8[4194304]{0:T(1024)(128)(4,1)S(1)}, s32[]{:S(2)}) async-start(s8[10485760]{0:T(1024)(128)(4,1)} %bitcast.72), calls=%async_computation.7 | async-start | bytes 8388608
  451.5 25.5 %slice-start.3 = ((s8[10485760]{0:T(1024)(128)(4,1)}), s8[2097152]{0:T(1024)(128)(4,1)S(1)}, s32[]{:S(2)}) async-start(s8[10485760]{0:T(1024)(128)(4,1)} %bitcast.72), calls=%async_computation.8 | async-start | bytes 4194304
  467.2 9.8 %copy-start.46 = (bf16[2048,512]{0,1:T(8,128)(2,1)S(1)}, bf16[2048,512]{0,1:T(8,128)(2,1)}, u32[]{:S(2)}) copy-start(bf16[2048,512]{0,1:T(8,128)(2,1)} %get-tuple-element.154) | copy-start | bytes 6291460
  470.5 143.9 %collective-permute-start.3 = (bf16[1280,1024]{1,0:T(8,128)(2,1)}, bf16[1280,1024]{1,0:T(8,128)(2,1)}, u32[]{:S(2)}, u32[]{:S(2)}) collective-permute-start(bf16[1280,1024]{1,0:T(8,128)(2,1)} %constant_dynamic-slice_fusion.8), channel_id=1, source_target_pairs={{0,8},{24,16},{1,9},{25,17},{2,10},{26,18},{3,11},{27,19},{4,12},{... | collective-permute-start | bytes 7864328 | tf_op jit(solution)/shard_map/ppermute | solution.py:1059
  474.9 139.6 %collective-permute-start.4 = (bf16[1280,1024]{1,0:T(8,128)(2,1)}, bf16[1280,1024]{1,0:T(8,128)(2,1)}, u32[]{:S(2)}, u32[]{:S(2)}) collective-permute-start(bf16[1280,1024]{1,0:T(8,128)(2,1)} %constant_dynamic-slice_fusion.8), channel_id=1, source_target_pairs={{8,16},{16,8},{9,17},{17,9},{10,18},{18,10},{11,19},{19,11},{12,20... | collective-permute-start | bytes 7864328 | tf_op jit(solution)/shard_map/ppermute | solution.py:1059
  485.5 128.9 %collective-permute-start.5 = (bf16[512,1280]{1,0:T(8,128)(2,1)}, bf16[512,1280]{1,0:T(8,128)(2,1)}, u32[]{:S(2)}, u32[]{:S(2)}) collective-permute-start(bf16[512,1280]{1,0:T(8,128)(2,1)} %constant_dynamic-slice_fusion.7), channel_id=1, source_target_pairs={{0,8},{24,16},{1,9},{25,17},{2,10},{26,18},{3,11},{27,19},{4,12},{... | collective-permute-start | bytes 3932168 | tf_op jit(solution)/shard_map/ppermute | solution.py:1059
  487.8 126.6 %collective-permute-start.6 = (bf16[512,1280]{1,0:T(8,128)(2,1)}, bf16[512,1280]{1,0:T(8,128)(2,1)}, u32[]{:S(2)}, u32[]{:S(2)}) collective-permute-start(bf16[512,1280]{1,0:T(8,128)(2,1)} %constant_dynamic-slice_fusion.7), channel_id=1, source_target_pairs={{8,16},{16,8},{9,17},{17,9},{10,18},{18,10},{11,19},{19,11},{12,20... | collective-permute-start | bytes 3932168 | tf_op jit(solution)/shard_map/ppermute | solution.py:1059
  620.3 72.6 %collective-permute-start.7 = (bf16[512,1280]{1,0:T(8,128)(2,1)}, bf16[512,1280]{1,0:T(8,128)(2,1)}, u32[]{:S(2)}, u32[]{:S(2)}) collective-permute-start(bf16[512,1280]{1,0:T(8,128)(2,1)} %collective-permute-done.5), channel_id=1, source_target_pairs={{8,16},{16,8},{9,17},{17,9},{10,18},{18,10},{11,19},{19,11},{12,20... | collective-permute-start | bytes 3932168 | tf_op jit(solution)/shard_map/ppermute | solution.py:1063
  622.1 70.9 %collective-permute-start.8 = (bf16[512,1280]{1,0:T(8,128)(2,1)}, bf16[512,1280]{1,0:T(8,128)(2,1)}, u32[]{:S(2)}, u32[]{:S(2)}) collective-permute-start(bf16[512,1280]{1,0:T(8,128)(2,1)} %collective-permute-done.6), channel_id=1, source_target_pairs={{8,0},{16,24},{9,1},{17,25},{10,2},{18,26},{11,3},{19,27},{12,4},{... | collective-permute-start | bytes 3932168 | tf_op jit(solution)/shard_map/ppermute | solution.py:1063
  647.7 29.4 %slice-start.6 = ((s8[5242880]{0:T(1024)(128)(4,1)}), s8[1048576]{0:T(1024)(128)(4,1)S(1)}, s32[]{:S(2)}) async-start(s8[5242880]{0:T(1024)(128)(4,1)} %bitcast.83), calls=%async_computation.11 | async-start | bytes 2097152
  647.7 37.4 %all-to-all-start.3 = ((f32[4,80,640]{2,1,0:T(8,128)}), f32[4,80,640]{2,1,0:T(8,128)S(1)}, u32[]{:S(2)}, u32[]{:S(2)}) async-start(f32[4,80,640]{2,1,0:T(8,128)} %bitcast.23), calls=%async_computation.3 | async-start | bytes 1638400 | tf_op jit(solution)/shard_map/all_to_all | solution.py:246
  663.0 14.1 %copy-start.30 = (bf16[1024,512]{1,0:T(8,128)(2,1)S(1)}, bf16[1024,512]{1,0:T(8,128)(2,1)}, u32[]{:S(2)}) copy-start(bf16[1024,512]{1,0:T(8,128)(2,1)} %copy-done.29) | copy-start | bytes 3145732
  663.0 14.1 %slice-start.7 = ((s8[5242880]{0:T(1024)(128)(4,1)}), s8[4194304]{0:T(1024)(128)(4,1)S(1)}, s32[]{:S(2)}) async-start(s8[5242880]{0:T(1024)(128)(4,1)} %bitcast.83), calls=%async_computation.12 | async-start | bytes 8388608
  673.6 81.5 %collective-permute-start.10 = (bf16[1280,1024]{1,0:T(8,128)(2,1)}, bf16[1280,1024]{1,0:T(8,128)(2,1)}, u32[]{:S(2)}, u32[]{:S(2)}) collective-permute-start(bf16[1280,1024]{1,0:T(8,128)(2,1)} %collective-permute-done.4), channel_id=1, source_target_pairs={{8,0},{16,24},{9,1},{17,25},{10,2},{18,26},{11,3},{19,27},{12,4},{... | collective-permute-start | bytes 7864328 | tf_op jit(solution)/shard_map/ppermute | solution.py:1063
  674.9 80.2 %collective-permute-start.9 = (bf16[1280,1024]{1,0:T(8,128)(2,1)}, bf16[1280,1024]{1,0:T(8,128)(2,1)}, u32[]{:S(2)}, u32[]{:S(2)}) collective-permute-start(bf16[1280,1024]{1,0:T(8,128)(2,1)} %collective-permute-done.3), channel_id=1, source_target_pairs={{8,16},{16,8},{9,17},{17,9},{10,18},{18,10},{11,19},{19,11},{12,20... | collective-permute-start | bytes 7864328 | tf_op jit(solution)/shard_map/ppermute | solution.py:1063
  685.1 38.4 %all-to-all-start.1 = ((bf16[8,320,320]{2,1,0:T(8,128)(2,1)}), bf16[8,320,320]{2,1,0:T(8,128)(2,1)S(1)}, u32[]{:S(2)}, u32[]{:S(2)}) async-start(bf16[8,320,320]{2,1,0:T(8,128)(2,1)} %bitcast.57), calls=%async_computation.1 | async-start | bytes 3932160 | tf_op jit(solution)/shard_map/all_to_all | solution.py:246
  689.3 62.8 %collective-permute-start.11 = (f32[80,640]{1,0:T(8,128)S(1)}, f32[80,640]{1,0:T(8,128)}, u32[]{:S(2)}, u32[]{:S(2)}) collective-permute-start(f32[80,640]{1,0:T(8,128)S(1)} %reduce_sum.49), channel_id=1, source_target_pairs={{0,0},{1,4},{2,8},{3,12},{4,16},{5,20},{6,24},{7,28},{8,1},{9,5},{... | collective-permute-start | bytes 614408 | tf_op jit(solution)/shard_map/ppermute | solution.py:1238
  696.2 67.8 %collective-permute-start.13 = (bf16[512,640]{1,0:T(8,128)(2,1)}, bf16[512,640]{1,0:T(8,128)(2,1)S(1)}, u32[]{:S(2)}, u32[]{:S(2)}) collective-permute-start(bf16[512,640]{1,0:T(8,128)(2,1)} %get-tuple-element.166), channel_id=1, source_target_pairs={{0,8},{8,0},{1,9},{9,1},{2,10},{10,2},{3,11},{11,3},{4,12},{12,4},... | collective-permute-start | bytes 1966088 | tf_op jit(solution)/shard_map/ppermute | solution.py:1196
  760.9 166.4 %collective-permute-start.12 = (bf16[640,1024]{1,0:T(8,128)(2,1)}, bf16[640,1024]{1,0:T(8,128)(2,1)}, u32[]{:S(2)}, u32[]{:S(2)}) collective-permute-start(bf16[640,1024]{1,0:T(8,128)(2,1)} %get-tuple-element.159), channel_id=1, source_target_pairs={{0,8},{8,0},{1,9},{9,1},{2,10},{10,2},{3,11},{11,3},{4,12},{12,4},... | collective-permute-start | bytes 3932168 | tf_op jit(solution)/shard_map/ppermute | solution.py:1196
  764.0 146.7 %copy-start.40 = (bf16[512,640]{1,0:T(8,128)(2,1)}, bf16[512,640]{1,0:T(8,128)(2,1)S(1)}, u32[]{:S(2)}) copy-start(bf16[512,640]{1,0:T(8,128)(2,1)S(1)} %collective-permute-done.13) | copy-start | bytes 1966084
  912.4 14.4 %all-to-all-start.2 = ((f32[32,2,80]{2,1,0:T(2,128)}), f32[32,2,80]{2,1,0:T(2,128)S(1)}, u32[]{:S(2)}, u32[]{:S(2)}) async-start(f32[32,2,80]{2,1,0:T(2,128)} %maximum_bitcast_fusion), calls=%async_computation.2 | async-start | bytes 65536 | tf_op jit(solution)/shard_map/all_to_all | solution.py:246
  (42 other events, 213.1 us)
Sparse Core Ops, SparseCore 0:
  195.7 165.0 all-gather.1

commit v4 on v3

--- a/solution.py
+++ b/solution.py
@@ -236,7 +236,7 @@
         ],
         compiler_params=pltpu.CompilerParams(vmem_limit_bytes=40 << 20),
         cost_estimate=pl.CostEstimate(
-            flops=tokens * win * (8 * bw + 150), bytes_accessed=tokens * win * 30, transcendentals=tokens * win * 6
+            flops=tokens * win, bytes_accessed=tokens * win, transcendentals=0
         ),
         name="recur_backward",
     )(mg, gpre, conv, rec, inp, prev, lin, meta, vecs, rw, iw)
@@ -318,15 +318,18 @@
     def partners(self):
         return [self.partner(bit) for bit in self.bits]
 
-    def orders(self):
-        return [self.bits[i:] + self.bits[:i] for i in range(len(self.bits))]
+    def orders(self, light):
+        if light is None or not self.cube:
+            return [self.bits[i:] + self.bits[:i] for i in range(len(self.bits))]
+        near = [self.near[i:] + self.near[:i] for i in range(len(self.near))]
+        return [[self.far] + o if light == "first" else o + [self.far] for o in near]
 
 
 class Spread:
-    def __init__(self, group, src, out, sems):
+    def __init__(self, group, src, out, sems, light=None):
         self.group, self.src, self.out = group, src, out
         self.keep, self.out_sems, self.in_sems, self.pass_sems, self.mate_sems = sems
-        self.orders = group.orders()
+        self.orders = group.orders(light)
         self.lanes = lane_slices(src.shape[-1], len(self.orders))
         self.moves = []
         index = 0
@@ -404,11 +407,11 @@
 
 
 class Fold:
-    def __init__(self, group, part, mate_buf, scratch):
+    def __init__(self, group, part, mate_buf, scratch, light=None):
         self.group, self.part, self.mate_buf = group, part, mate_buf
         (self.mine, self.far, self.stage, self.total,
          self.load_sems, self.pass_sems, self.mate_sems, self.out_sems, self.in_sems, self.stage_sems) = scratch
-        self.orders = group.orders()
+        self.orders = group.orders(light)
         self.lanes = lane_slices(part.shape[-1], len(self.orders))
         self.rows = self.total.shape[0]
         self.moves = []
@@ -608,20 +611,29 @@
         self.load_sems, self.out_sems, self.in_sems = sems
 
     @staticmethod
-    def scratch(count, rows, cols):
+    def scratch(parts, count, rows, cols):
         hops = 2 * (count - 1)
-        return [pltpu.VMEM((count, rows, cols), BF), pltpu.VMEM((hops, rows, cols), BF)] + dma_sems(count, hops, hops)
-
-    def load(self, d):
-        return pltpu.make_async_copy(self.part.at[d], self.blocks.at[d], self.load_sems.at[d])
+        return [pltpu.VMEM((count, rows, cols), BF), pltpu.VMEM((hops, rows, cols), BF)] + dma_sems(
+            parts * count, hops, hops
+        )
+
+    def loads(self, d):
+        first = 0
+        for i, part in enumerate(self.part):
+            cols = part.shape[2]
+            dst = self.blocks.at[d, :, pl.ds(first, cols)] if len(self.part) > 1 else self.blocks.at[d]
+            yield pltpu.make_async_copy(part.at[d], dst, self.load_sems.at[len(self.part) * d + i])
+            first += cols
 
     def begin(self):
         for d in range(self.count):
-            self.load(d).start()
+            for copy in self.loads(d):
+                copy.start()
 
     def ready(self):
         for d in range(self.count):
-            self.load(d).wait()
+            for copy in self.loads(d):
+                copy.wait()
 
     def sides(self, k):
         last = self.count - 1
@@ -677,13 +689,84 @@
 N_CHAIN = 5
 
 
-def last_backward(n_lo, n_cx, n_hi, with_out, part, sums, *refs):
+def everywhere(n_hi, n_lo, n_cx):
+    n_ctx = 2 * n_cx
+    n_cube = n_lo * n_ctx
+    number = (lax.axis_index("hi") * n_lo + lax.axis_index("lo")) * n_ctx + lax.axis_index("cxy") * 2
+    number = number + lax.axis_index("core")
+
+    def device(i):
+        return {
+            "hi": i // n_cube, "lo": lax.rem(i, n_cube) // n_ctx, "cxy": lax.rem(i, n_ctx) // 2, "core": lax.rem(i, 2),
+        }
+
+    return number, device, n_hi * n_cube
+
+
+def meet_all(number, device, n_dev):
+    barrier = pltpu.get_barrier_semaphore()
+
+    def greet(i, held):
+        other = device(lax.rem(number + i, n_dev))
+        pl.semaphore_signal(barrier, inc=1, device_id=other, device_id_type=pl.DeviceIdType.MESH)
+        return held
+
+    lax.fori_loop(1, n_dev, greet, 0)
+    pl.semaphore_wait(barrier, n_dev - 1)
+
+
+def ff_block(u, n_lo, n_cx):
+    lo, ctx = u // (2 * n_cx), u % (2 * n_cx)
+    return (ctx % 2) * (n_lo * n_cx) + lo * n_cx + ctx // 2
+
+
+class Exchange:
+    def __init__(self, number, device, n_dev, src, came, sems, split):
+        self.number, self.device, self.n_dev, self.split = number, device, n_dev, split
+        self.src, self.came, (self.out_sems, self.in_sems) = src, came, sems
+
+    def copy(self, i):
+        to = lax.rem(self.number + i, self.n_dev)
+        src = self.src.at[to] if self.split else self.src
+        return send(src, self.came.at[self.number], self.out_sems.at[i], self.in_sems.at[i], self.device(to))
+
+    def start(self):
+        def run(i, held):
+            self.copy(i).start()
+            return held
+
+        lax.fori_loop(1, self.n_dev, run, 0)
+
+    def recv(self):
+        def run(i, held):
+            source = lax.rem(self.number - i + self.n_dev, self.n_dev)
+            land = self.came.at[source]
+            send(land, land, self.out_sems.at[i], self.in_sems.at[i], self.device(source)).wait_recv()
+            return held
+
+        lax.fori_loop(1, self.n_dev, run, 0)
+
+    def end(self):
+        def run(i, held):
+            self.copy(i).wait_send()
+            return held
+
+        lax.fori_loop(1, self.n_dev, run, 0)
+
+
+N_CHAIN = 5
+
+
+def last_backward(n_lo, n_cx, n_hi, with_out, n_sums, part, *refs):
+    sums, packed, refs = refs[:n_sums], refs[n_sums], refs[n_sums + 1 :]
     if with_out:
-        out_part, inputs, hidden_grad, gain, hidden, input_grad, gain_grad, summed, mate_a, output, mate_b, *scratch = refs
+        (out_part, inputs, hidden_grad, gain, hidden, input_grad, gain_rows, packed_sum, summed, mate_a, output, mate_b,
+         *scratch) = refs
     else:
-        inputs, hidden_grad, gain, hidden, input_grad, gain_grad, summed, mate_a, *scratch = refs
+        inputs, hidden_grad, gain, hidden, input_grad, gain_rows, packed_sum, summed, mate_a, *scratch = refs
     fold_a, rest = scratch[:N_FOLD], scratch[N_FOLD:]
-    chain_s, fold_b = rest[:N_CHAIN], rest[N_CHAIN:]
+    chain_s, rest = rest[:N_CHAIN], rest[N_CHAIN:]
+    (pack_came, p_own, p_out, p_in), fold_b = rest[:4], rest[4:]
     cube = Group(n_lo, n_cx, True)
     plane = Group(n_lo, n_cx, False)
     n_dp = n_hi * n_lo
@@ -695,8 +778,16 @@
     chain.begin()
     first.begin()
     if with_out:
-        outs = Fold(cube, out_part, mate_b, fold_b)
+        outs = Fold(cube, out_part, mate_b, fold_b, "last")
         outs.begin()
+    others = [lax.rem(z + i, n_dp) for i in range(1, n_dp)]
+    pushes = [
+        send(packed.at[d], pack_came.at[i + 1], p_out.at[i], p_in.at[i], along(d)) for i, d in enumerate(others)
+    ]
+    own_pack = pltpu.make_async_copy(packed.at[z], pack_came.at[0], p_own)
+    own_pack.start()
+    for push in pushes:
+        push.start()
     hops = n_dp - 1
     chain.ready()
     chain.start(0)
@@ -708,16 +799,16 @@
     for k in range(hops - 1):
         chain.take(k, summed)
         chain.start(k + 1)
+        if k + 1 < len(plane.bits):
+            first.take(k + 1)
         if with_out and k + 1 < len(cube.bits):
             outs.take(k)
-        if k + 1 < len(plane.bits):
-            first.take(k + 1)
     for s in range(hops, len(plane.bits)):
         first.take(s)
-    gain_grad[...] = jnp.zeros_like(gain_grad)
+    gain_rows[...] = jnp.zeros_like(gain_rows)
 
     def norm(at):
-        norm_back(inputs, gain, first.total, hidden_grad, input_grad, gain_grad, at)
+        norm_back(inputs, gain, first.total, hidden_grad, input_grad, gain_rows, at)
 
     each_rows(first.rows, norm)
     if with_out:
@@ -728,7 +819,15 @@
             output[at, :] = hidden[at, :] + outs.total[at, :]
 
         each_rows(outs.rows, finish)
+    own_pack.wait()
+    value = pack_came[0]
+    for i, push in enumerate(pushes):
+        push.wait_recv()
+        value = value + pack_came[i + 1]
+    packed_sum[...] = value
     chain.take(hops - 1, summed)
+    for push in pushes:
+        push.wait_send()
     first.end()
     if with_out:
         outs.end()
@@ -787,7 +886,7 @@
     return hidden_grad, gain_grad, branch_all.reshape(-1, width)
 
 
-def last_backward_call(n_hi, n_lo, n_cx, part, out_part, sums, inputs, hidden_grad, gain, hidden):
+def last_backward_call(n_hi, n_lo, n_cx, part, out_part, sums, packed, inputs, hidden_grad, gain, hidden):
     tok, width = inputs.shape
     near = n_cx.bit_length() - 1
     far = near + n_lo - 1
@@ -795,25 +894,31 @@
     with_out = n_lo * n_cx <= 8
     rows = jax.ShapeDtypeStruct((tok, width), F32)
     sds = lambda *shape: jax.ShapeDtypeStruct(shape, BF)
-    sums = sums.reshape(n_dp, -1, sums.shape[1])
-    raw = (part.reshape(n_cx, 2, tok, width), sums)
-    outs = [(rows, True), (jax.ShapeDtypeStruct((8, width), F32), True),
-            (jax.ShapeDtypeStruct(sums.shape[1:], F32), True), (sds(n_cx, tok, width), False)]
-    scratch = Fold.scratch(near, near, tok, width) + Chain.scratch(*sums.shape)
+    full = lambda *shape: jax.ShapeDtypeStruct(shape, F32)
+    if any(p.shape[1] % 128 for p in sums):
+        sums = [jnp.concatenate(sums, axis=1)]
+    sums = [p.reshape(n_dp, -1, p.shape[1]) for p in sums]
+    summed_shape = (*sums[0].shape[1:2], sum(p.shape[2] for p in sums))
+    packed = packed.reshape(n_dp, -1, packed.shape[1])
+    raw = (part.reshape(n_cx, 2, tok, width), *sums, packed)
+    outs = [(rows, True), (full(8, width), True), (full(*packed.shape[1:]), True), (full(*summed_shape), True),
+            (sds(n_cx, tok, width), False)]
+    scratch = Fold.scratch(near, near, tok, width) + Chain.scratch(len(sums), n_dp, *summed_shape)
+    scratch += [pltpu.VMEM(packed.shape, F32)] + dma_sems(0, n_dp - 1, n_dp - 1)
     if with_out:
         raw += (out_part.reshape(n_lo * n_cx, 2, tok, width),)
         outs += [(rows, True), (sds(n_lo * n_cx, tok, width), False)]
-        scratch += Fold.scratch(far, far, tok, width)
+        scratch += Fold.scratch(far, near, tok, width)
     got = comm_call(
-        functools.partial(last_backward, n_lo, n_cx, n_hi, with_out), "sum_norm_backward", 3,
+        functools.partial(last_backward, n_lo, n_cx, n_hi, with_out, len(sums)), "sum_norm_backward", 3,
         raw, (inputs, hidden_grad, gain, hidden), outs, scratch, 1,
     )
-    input_grad, gain_grad, summed = got[:3]
+    input_grad, gain_rows, packed_sum, summed = got[:4]
     if with_out:
-        output = got[4]
+        output = got[5]
     else:
         output = hidden + lax.psum_scatter(out_part, CUBE, scatter_dimension=0, tiled=True).astype(F32)
-    return input_grad, gain_grad, output, summed
+    return input_grad, gain_rows, packed_sum, output, summed
 
 
 class Line:
@@ -877,10 +982,11 @@
     return head * ((n_dev - n_ctx) // (HEADS - span))
 
 
-def gather_start(sizes, gelu_w, lin_w, proj, rgate, igate, normed, down, gate_w, up_w,
-                 gl_out, gu_out, pg_z, pg_win, normed_all, down_other,
+def gather_start(sizes, gelu_w, lin_w, proj, rgate, igate, small, down, gate_w, up_w, inputs,
+                 gl_out, gu_out, pg_z, pg_win, normed_all, down_other, small_all,
                  gu_send, own_pg, own_gl, own_rest, gl_s, gl_r, mate_s, mate_r, gu_s, gu_r, win_s, win_r,
-                 zp_s, zp_r, zg_s, zg_r, zm_s, zm_r, dn_s, dn_r, *spread_s):
+                 zp_s, zp_r, zg_s, zg_r, zm_s, zm_r, dn_s, dn_r,
+                 normed, small_came, sm_own, sm_s, sm_r, *spread_s):
     n_hi, n_lo, n_cx, n_core, own_ch, bw, span = sizes
     n_ctx = n_cx * n_core
     n_cube = n_lo * n_ctx
@@ -899,18 +1005,12 @@
     in_plane = lambda c: {"cxy": c // n_core, "core": lax.rem(c, n_core)}
     in_cube = lambda u: {"lo": u // n_ctx, **in_plane(lax.rem(u, n_ctx))}
 
-    barrier = pltpu.get_barrier_semaphore()
-
-    def greet(i, held):
-        other = lax.rem(number + i, n_dev)
-        pl.semaphore_signal(
-            barrier, inc=1, device_id={"hi": other // n_cube, **in_cube(lax.rem(other, n_cube))},
-            device_id_type=pl.DeviceIdType.MESH,
-        )
-        return held
-
-    lax.fori_loop(1, n_dev, greet, 0)
-    pl.semaphore_wait(barrier, n_dev - 1)
+    _, device, _ = everywhere(n_hi, n_lo, n_cx)
+    meet_all(number, device, n_dev)
+    vectors = Exchange(number, device, n_dev, small, small_came, (sm_s, sm_r), False)
+    vectors.start()
+    own_small = pltpu.make_async_copy(small, small_came.at[number], sm_own)
+    own_small.start()
 
     pg_parts = [(proj, 0, width), (rgate, width, bw), (igate, width + bw, bw)]
     pg_own = [
@@ -942,6 +1042,19 @@
     for copy in pg_own:
         copy.wait()
     line.run(pg_part, pg_sems, 0, "start")
+    own_small.wait()
+    vectors.recv()
+    piece = width // n_dev
+    for d in range(n_dev):
+        small_all[:, d * piece : (d + 1) * piece] = small_came[d, :, 0:piece]
+    gain = small_all[0:1, :].astype(F32)
+
+    def norm(at):
+        x = inputs[at, :]
+        r = lax.rsqrt(jnp.mean(x * x, axis=-1, keepdims=True) + 1e-06)
+        normed[at, :] = (x * r * gain).astype(BF)
+
+    each_rows(normed.shape[0], norm)
     rows = Spread(Group(n_lo, n_cx, False), normed, normed_all, spread_s)
     rows.begin()
     for copy in gl_own:
@@ -959,7 +1072,7 @@
     ff_pad = gu_send.shape[2] // 2
     shard_rows = gate_w.shape[0]
     for u in range(n_cube):
-        first = (u % n_ctx) * (n_lo * ff_own) + (u // n_ctx) * ff_own
+        first = ff_block(u, n_lo, n_cx) * ff_own
         for i, ref in enumerate((gate_w, up_w)):
             gu_send[u, :, i * ff_pad : i * ff_pad + ff_own] = ref[:, first : first + ff_own]
             if ff_pad > ff_own:
@@ -1022,9 +1135,10 @@
         line.run(gl_part, gl_sems, k, "sent")
         line.run(gl_part, gl_sems, k, "mate_recv")
     down_copy.wait()
-
-
-def gather_start_call(sizes, gelu_w, lin_w, proj, rgate, igate, normed, down, gate_w, up_w, ff_pad):
+    vectors.end()
+
+
+def gather_start_call(sizes, gelu_w, lin_w, proj, rgate, igate, small, down, gate_w, up_w, inputs, ff_pad):
     n_hi, n_lo, n_cx, n_core, own_ch, bw, span = sizes
     n_ctx = n_cx * n_core
     n_cube = n_lo * n_ctx
@@ -1037,22 +1151,24 @@
     vmem = pl.BlockSpec(memory_space=pltpu.VMEM)
     pg_width = width + 2 * bw
     hops = 2 * (n_dp - 1)
-    gl_out, gu_out, _, pg_win, normed_all, down_other = pl.pallas_call(
+    gl_out, gu_out, _, pg_win, normed_all, down_other, small_all = pl.pallas_call(
         functools.partial(gather_start, sizes),
-        in_specs=[any_spec] * 7 + [vmem] * 2,
-        out_specs=[any_spec] * 6,
+        in_specs=[any_spec] * 7 + [vmem] * 3,
+        out_specs=[any_spec] * 6 + [vmem],
         out_shape=[
             sds(n_dp, n_cx, n_core, shard, 2 * wide), sds(n_cube, shard, 2 * ff_pad), sds(n_dp, shard, pg_width),
-            sds(n_ctx, shard, pg_width), sds(n_ctx, *normed.shape), sds(*down.shape),
+            sds(n_ctx, shard, pg_width), sds(n_ctx, *inputs.shape), sds(*down.shape),
+            sds(small.shape[0], width),
         ],
         scratch_shapes=[pltpu.VMEM((n_cube, shard, 2 * ff_pad), BF)]
         + dma_sems(3, 2, 2, 2 * n_cx, 2 * n_cx, 0, 0, n_cube, n_cube, n_ctx, n_ctx, hops, hops, hops, hops, hops, hops, 0, 0)
-        + Spread.sems(near, near),
+        + [pltpu.VMEM(inputs.shape, BF), pltpu.VMEM((n_dp * n_ctx, *small.shape), BF)]
+        + dma_sems(0, n_dp * n_ctx, n_dp * n_ctx) + Spread.sems(near, near),
         compiler_params=pltpu.CompilerParams(collective_id=4, has_side_effects=True, vmem_limit_bytes=40 << 20),
         cost_estimate=pl.CostEstimate(flops=10**11, bytes_accessed=10**8, transcendentals=0),
         name="gather_start",
-    )(gelu_w, lin_w, proj, rgate, igate, normed, down, gate_w, up_w)
-    return gl_out.reshape(width, 2 * wide), gu_out.reshape(-1, 2 * ff_pad), pg_win.reshape(-1, pg_width), normed_all.reshape(-1, width), down_other
+    )(gelu_w, lin_w, proj, rgate, igate, small, down, gate_w, up_w, inputs)
+    return gl_out.reshape(width, 2 * wide), gu_out.reshape(-1, 2 * ff_pad), pg_win.reshape(-1, pg_width), normed_all.reshape(-1, width), down_other, small_all
 
 
 def swap_first(value):
@@ -1099,19 +1215,16 @@
         + [v[None] for v in (conv_bias, recur_gate_b, input_gate_b, decay_param)],
         axis=0,
     )
-    small_all = exchange(jnp.broadcast_to(small[None], (n_dev,) + small.shape), EVERY)
-    small_all = small_all.transpose(1, 0, 2).reshape(small.shape[0], width).astype(F32)
+    small = jnp.pad(small, ((0, 16 - small.shape[0]), (0, 128 - piece)))
+
+    sizes = (n_hi, n_lo, n_cx, n_core, own_ch, bw, span)
+    gl_w, gu_mine, pg_win, normed_all, down_other, small_all = gather_start_call(
+        sizes, gelu_in_w, linear_in_w, out_proj_w, recur_gate_w, input_gate_w, small, mlp_down_w,
+        mlp_gate_w, mlp_up_w, inputs, ff_pad,
+    )
+    small_all = small_all.astype(F32)
     gain_first = small_all[0]
     gain_second = small_all[1]
-
-    r_first = lax.rsqrt(jnp.mean(inputs * inputs, axis=-1, keepdims=True) + 1e-06)
-    normed = (inputs * r_first * gain_first).astype(BF)
-
-    sizes = (n_hi, n_lo, n_cx, n_core, own_ch, bw, span)
-    gl_w, gu_mine, pg_win, normed_all, down_other = gather_start_call(
-        sizes, gelu_in_w, linear_in_w, out_proj_w, recur_gate_w, input_gate_w, normed, mlp_down_w,
-        mlp_gate_w, mlp_up_w, ff_pad,
-    )
     wide = win + bw
     chip_off = (head0 - chip_head(cx, own_ch, bw, span)) * bw
     gelu_w = lax.dynamic_slice_in_dim(gl_w[:, :wide], chip_off, win, axis=1)
@@ -1123,19 +1236,10 @@
 
     gu_other = lax.ppermute(gu_mine, "hi", SWAP)
     n_cube = n_lo * n_ctx
-    half = n_cube // 2
-    to_a, to_b = [], []
-    place = lambda t: (t % n_lo) * n_ctx + t // n_lo
-    for q in range(n_cube):
-        lower, upper = q // 2, q // 2 + half
-        near, far = (lower, upper) if q % 2 == 0 else (upper, lower)
-        to_a.append((q, place(near)))
-        to_b.append((q, place(far)))
-    same = hi == core
-    down_a = lax.ppermute(jnp.where(same, mlp_down_w, down_other), CUBE, to_a)
-    down_b = lax.ppermute(jnp.where(same, down_other, mlp_down_w), CUBE, to_b)
-    slot = ctx * n_lo + lo
-    down_w = in_order((slot >= half).astype(jnp.int32), down_a, down_b, 0)
+    keeps = hi == core
+    down_keep = jnp.where(keeps, mlp_down_w, down_other)
+    down_came = lax.ppermute(jnp.where(keeps, down_other, mlp_down_w), "core", SWAP)
+    down_w = in_order(core, down_keep, down_came, 0)
     down_w = jnp.pad(down_w, ((0, ff_pad - ff_own), (0, 0)))
     cot = lax.optimization_barrier((out_grad.astype(BF), down_other))[0]
     down_grad = lax.all_gather(cot, CUBE, axis=0, tiled=True)
@@ -1145,7 +1249,7 @@
     for k in range(1, CONV):
         metas.append(jnp.concatenate([jnp.zeros((k,), F32), (ids[k:] == ids[:-k]).astype(F32)]))
     meta = jnp.stack(metas, axis=1)
-    vec_win = lax.dynamic_slice_in_dim(small_all[2:], ch0, win, axis=1)
+    vec_win = lax.dynamic_slice_in_dim(small_all[2:10], ch0, win, axis=1)
     decay_win = vec_win[7:8]
     place_in = jnp.arange(win) - own_off
     own_mask = ((place_in >= 0) & (place_in < own_ch)).astype(F32)[None]
@@ -1173,15 +1277,13 @@
     activation = (gel * up_pre).astype(BF)
     gu_low = jnp.concatenate([(act_grad * up_pre * slope).astype(BF), (act_grad * gel).astype(BF)], axis=1)
     second_part = dot(gu_low, gu_w, 1, 1).astype(BF)
-    grad_gu = dot(second_all, gu_low, 0, 0).astype(BF)
-    grad_down = dot(activation, down_grad, 0, 0).astype(BF)
 
     def half_of(partial, which, axis, parts):
         size = partial.shape[axis] // parts
         return lax.dynamic_slice_in_dim(partial, which * size, size, axis)
 
-    gu_stage = swap_first(half_of(grad_gu, 1 - hi, 0, n_hi))
-    dn_stage = swap_first(half_of(grad_down, 1 - hi, 1, n_hi))
+    gu_stage = swap_first(dot(half_of(second_all, 1 - hi, 1, n_hi), gu_low, 0, 0).astype(BF))
+    dn_stage = swap_first(dot(activation, half_of(down_grad, 1 - hi, 1, n_hi), 0, 0).astype(BF))
     hidden_grad, gain_two_rows, branch_all = middle_backward_call(
         n_lo, n_cx, second_part, hidden, out_grad, gain_second[None]
     )
@@ -1191,22 +1293,39 @@
     gu_stage = swap_second(*stages[:2])
     inner = hi != lo
 
+    late_second, late_cot = lax.optimization_barrier((second_all, down_grad, branch_all))[:2]
+    own_gu = dot(half_of(late_second, hi, 1, n_hi), gu_low, 0, 0).astype(BF)
+    own_dn = dot(activation, half_of(late_cot, hi, 1, n_hi), 0, 0).astype(BF)
+
+    turns = [
+        [
+            (u, ((u % n_ctx // 2 + s) % 2) * n_ctx + ff_block(u, n_lo, n_cx) // 2)
+            for u in range(n_cube)
+        ]
+        for s in range(2)
+    ]
+
     def settle(partial, got, axis):
-        both = (half_of(partial, hi, axis, n_hi).astype(F32) + got.astype(F32)).astype(BF)
-        return half_of(both, lo, axis, n_lo), lax.ppermute(half_of(both, 1 - lo, axis, n_lo), "lo", SWAP)
+        both = (partial.astype(F32) + got.astype(F32)).astype(BF)
+        odd = lax.rem(cx, 2)
+        return tuple(lax.ppermute(half_of(both, lax.rem(odd + s, 2), axis, n_lo), CUBE, turns[s]) for s in range(2))
 
     out_part = dot(activation, lax.optimization_barrier((down_w, gain_two_rows))[0], 1, 0).astype(BF)
 
     own_mixed = lax.dynamic_slice_in_dim(mixed, own_off, own_ch, axis=1)
     grad_proj = dot(own_mixed, branch_all, 0, 0).astype(BF).reshape(own_ch, n_ctx, width // n_ctx)
-    grad_proj = exchange(grad_proj.transpose(1, 0, 2), CTX).reshape(chans, width // n_ctx)
+    grad_proj = grad_proj.transpose(1, 0, 2)
     mixed_grad = dot(branch_all, proj_w, 1, 1)
+    mixed_grad, own_gu, own_dn, out_part, grad_proj = lax.optimization_barrier(
+        (mixed_grad, own_gu, own_dn, out_part, grad_proj)
+    )
+    grad_proj = exchange(grad_proj, CTX).reshape(chans, width // n_ctx)
     gelu_low, linear_low, recur_wg, input_wg, sums = backward_call(
         mixed_grad, gelu_pre, conv_out, rec, inp, prev, linear_out, meta, vecs, recur_w, input_w
     )
-    gelu_low, linear_low, *dn_stage = lax.optimization_barrier((gelu_low, linear_low) + dn_stage)
-    got_dn = jnp.where(inner, *dn_stage)
-    got_gu = jnp.where(inner, *gu_stage)
+    gelu_low, linear_low, *stages = lax.optimization_barrier((gelu_low, linear_low, *dn_stage, *gu_stage))
+    got_dn = jnp.where(inner, *stages[:2])
+    got_gu = jnp.where(inner, *stages[2:])
     own_lows = jnp.concatenate(
         [
             lax.dynamic_slice_in_dim(gelu_low, own_off, own_ch, axis=1),
@@ -1215,14 +1334,19 @@
         axis=1,
     )
     grad_gl = dot(normed_all, own_lows, 0, 0).astype(BF)
-    first_part = (dot(gelu_low, gelu_w, 1, 1) + dot(linear_low, lin_w, 1, 1)).astype(BF)
-    grad_three = jnp.concatenate([grad_gl, grad_proj], axis=1)
-    dn_a, dn_b = settle(grad_down, got_dn, 1)
-    gu_a, gu_b = settle(grad_gu, got_gu, 0)
-    first_part, dn_a, gu_a = lax.optimization_barrier((first_part, dn_a, gu_a))
-    input_grad, gain_one_rows, output, grad_three = last_backward_call(
-        n_hi, n_lo, n_cx, first_part, out_part, grad_three, inputs, hidden_grad, gain_first[None], hidden
+    first_part = dot(
+        jnp.concatenate([gelu_low, linear_low], axis=1), jnp.concatenate([gelu_w, lin_w], axis=1), 1, 1
+    ).astype(BF)
+    dn_a, dn_b = settle(own_dn, got_dn, 1)
+    gu_a, gu_b = settle(own_gu, got_gu, 0)
+    first_part, dn_a, dn_b = lax.optimization_barrier((first_part, dn_a, dn_b))
+    packed = jnp.concatenate([recur_wg, input_wg, pad_last(sums.T, 128)], axis=1)
+    packed = lax.dynamic_slice_in_dim(packed, own_off, own_ch, axis=0)
+    input_grad, gain_one_rows, packed, output, grad_three = last_backward_call(
+        n_hi, n_lo, n_cx, first_part, out_part, (grad_gl, grad_proj), packed, inputs, hidden_grad, gain_first[None], hidden
     )
+    routes = [(d * n_ctx + c, c * n_dp + d) for d in range(n_dp) for c in range(n_ctx)]
+    packed = lax.ppermute(packed, EVERY, routes)
     grad_gl = grad_three[:, : 2 * own_ch]
     grad_proj = grad_three[:, 2 * own_ch :]
     grad_gate = in_order(lo, gu_a[:, :ff_own], gu_b[:, :ff_own], 1).astype(F32)
@@ -1231,16 +1355,11 @@
     ).astype(F32)
     grad_dn = in_order(lo, dn_a[:ff_own], dn_b[:ff_own], 0).astype(F32)
 
-    packed = jnp.concatenate([recur_wg, input_wg, pad_last(sums.T, 128)], axis=1)
-    packed = lax.dynamic_slice_in_dim(packed, own_off, own_ch, axis=0)
-    packed = jnp.sum(exchange(packed.reshape(n_dp, own_ch // n_dp, packed.shape[1]), DP), axis=0)
-    routes = [(d * n_ctx + c, c * n_dp + d) for d in range(n_dp) for c in range(n_ctx)]
-    packed = lax.ppermute(packed, EVERY, routes)
     grad_recur_w = packed[:, :bw]
     grad_input_w = packed[:, bw : 2 * bw]
     rest = packed[:, 2 * bw : 2 * bw + 8].T
-    gains = jnp.stack([jnp.sum(gain_one_rows, axis=0), jnp.sum(gain_two_rows, axis=0)]).reshape(2, n_dev, piece).transpose(1, 0, 2)
-    gains = jnp.sum(exchange(gains, EVERY), axis=0)
+    gains = jnp.stack([jnp.sum(gain_one_rows, axis=0), jnp.sum(gain_two_rows, axis=0)])
+    gains = jnp.sum(exchange(gains.reshape(2, n_dev, piece).transpose(1, 0, 2), EVERY), axis=0)
 
     return (
         output,

time: 958 us -> 896 us (0.935)
  Pallas kernels: 611 us -> 571 us
  starting transfers between devices: 68.7 us -> 44.3 us
    pallas_call x3, Pallas kernels: 417 us -> 367 us  [comm_call(): pl.pallas_call(kernel, in_specs=[any_spec] * len(raw) + [vmem] * len(args...]
    ppermute x2, waiting for transfers between devices: 0.01 us -> 27.8 us  [swap_second(): lax.ppermute(crossed, DP, [(1, 0), (2, 3)])]
    all_to_all x4 -> x2, starting transfers between devices: 32.1 us -> 15.1 us  [exchange(): return lax.all_to_all(value, axes, split_axis=0, concat_axis=0, tiled=True)]
    ppermute x1, waiting for transfers between devices: 23.6 us -> 8.27 us  [per_device(): packed = lax.ppermute(packed, EVERY, routes)]
    unnamed x119 -> x139, local copies, waits for them, and re-layouts: 26.5 us -> 36.2 us
    pallas_call x1, Pallas kernels: 164 us -> 174 us  [gather_start_call(): pl.pallas_call(functools.partial(gather_start, sizes), in_specs=[any_spec...]
    dot_general x14 -> x15, matrix products: 131 us -> 130 us  [dot(): lax.dot_general(a, b, (((ca,), (cb,)), ((), ())), preferred_element_type=...]
  transfers between devices with their start and end apart: 19 -> 18, of which waited for: 3 -> 2; matrix products, arithmetic and copies ran while one was open for 16% -> 17% of each run, Pallas kernels for 47% -> 45%
where the time goes in v4:
time: 896 us; the launch traced here: 885 us
  Pallas kernels  571 us (64%)
  matrix products  130 us (15%)
  local copies, waits for them, and re-layouts  63.3 us (7%)
  starting transfers between devices  44.3 us (5%)
  waiting for transfers between devices  36.2 us (4%)
  other arithmetic  24.7 us (3%)
  between operations  15.4 us (2%)
    pallas_call x3, Pallas kernels, comm_call(): pl.pallas_call(kernel, in_specs=[any_spec] * len(raw) + [vmem] * len(args...  367 us
    pallas_call x1, Pallas kernels, gather_start_call(): pl.pallas_call(functools.partial(gather_start, sizes), in_specs=[any_spec...  174 us
    dot_general x15, matrix products, dot(): lax.dot_general(a, b, (((ca,), (cb,)), ((), ())), preferred_element_type=...  130 us
    unnamed x139, local copies, waits for them, and re-layouts  36.2 us
    ppermute x2, waiting for transfers between devices, swap_second(): lax.ppermute(crossed, DP, [(1, 0), (2, 3)])  27.8 us
    pallas_call x1, Pallas kernels, backward_call(): pl.pallas_call(backward_kernel, grid=grid, in_specs=[tok] * 7 + [mspec, v...  19.4 us
  transfers between devices with their start and end apart: 18, of which 2 were waited for; matrix products, arithmetic and copies ran while one was open for 17% of the time, Pallas kernels for 45%

profile of v4, /device:TPU:1, one launch (start us, length us, event | category | flops | bytes accessed | tf_op | source)
XLA Modules:
  0.0 885.1 jit_solution(12434212260640930956)
XLA Ops:
  20.7 173.9 %gather_start.1 = (bf16[4,4,2,80,1536]{4,3,2,1,0:T(8,128)(2,1)}, bf16[16,80,1024]{2,1,0:T(8,128)(2,1)S(1)}, bf16[4,80,3072]{2,1,0:T(8,128)(2,1)}, bf16[8,80,3072...) custom-call(bf16[80,2560]{1,0:T(8,128)(2,1)S(1)} %copy-done.32, ...), custom_call_target="tpu_custom_call" | custom-call | flops 99999997952 | bytes 100000000 | tf_op jit(solution)/shard_map/gather_start/pallas_call | solution.py:1154
  199.1 3.6 fusion.57
  203.2 7.3 convolution_convert_fusion.6.lin_ref
  210.7 5.2 fusion.65.gpre_ref
  216.0 10.3 %recur_forward.1 = (bf16[1024,512]{1,0:T(8,128)(2,1)S(1)}, f32[1024,512]{1,0:T(8,128)S(1)}, f32[1024,512]{1,0:T(8,128)S(1)}, f32[1024,512]{1,0:T(8,128)S(1)}, f32[1024,512]{1,0:T(8,128)S(1)}) custom-call(bf16[1024,512]{1,0:T(8,128)(2,1)S(1)} %convolution_convert_fusion.6.lin_ref, f32[1024,512]{1,0:T(8,128)S(1)} %fusion.65.gpre_ref, ...), custom_call_target="tpu_custom_call" | custom-call | flops 589299712 | bytes 12582912 | tf_op jit(solution)/shard_map/recur_forward/pallas_call | solution.py:190
  226.3 5.2 convolution_convert_fusion.2
  232.1 125.6 %sum_norm_gather_forward.1 = (f32[128,2560]{1,0:T(8,128)}, bf16[16,128,2560]{2,1,0:T(8,128)(2,1)}, bf16[4,128,2560]{2,1,0:T(8,128)(2,1)}) custom-call(bf16[4,2,128,2560]{3,2,1,0:T(8,128)(2,1)} %bitcast.53, f32[128,2560]{1,0:T(8,128)} %refs_3_.1, f32[1,2560]{1,0:T(1,128)} %get-tuple-element.195.gain), custom_call_target="tpu_custom_call" | custom-call | flops 1000000000 | bytes 1000000 | tf_op jit(solution)/shard_map/sum_norm_gather_forward/pallas_call | solution.py:840
  362.5 18.6 %fusion.36 = f32[2048,1024]{0,1:T(8,128)} fusion(bf16[2048,2560]{1,0:T(8,128)(2,1)} %bitcast.69, bf16[1280,1024]{1,0:T(8,128)(2,1)} %collective-permute-done.1, bf16[1280,1024]{1,0:T(8,128)(2,1)S(1)} %bitcast.48, pred[]{:T(512)S(6)} %eq.31), kind=kOutput, calls=%fused_computation.55 | convolution fusion | flops 10761011200 | bytes 24117248 | tf_op jit(solution)/shard_map/dot_general | solution.py:24
  381.1 13.3 %multiply_convert_fusion.2 = (bf16[2048,512]{0,1:T(8,128)(2,1)S(1)}, bf16[2048,512]{0,1:T(8,128)(2,1)S(1)}, bf16[2048,512]{0,1:T(8,128)(2,1)S(1)}) fusion(f32[2048,1024]{0,1:T(8,128)} %fusion.36, bf16[2048,2560]{1,0:T(8,128)(2,1)} %all-gather.2.cloned.1.call-done, bf16[480,2560]{1,0:T(8,128)(2,1)} %copy-done.39), kind=kOutput, calls=%fused_computation.22 | convolution fusion | flops 5393874944 | bytes 27623424 | tf_op jit(solution)/shard_map/dot_general | solution.py:24
  394.5 12.8 %fusion.12 = bf16[1280,1024]{1,0:T(8,128)(2,1)} fusion(bf16[2048,2560]{1,0:T(8,128)(2,1)} %bitcast.70, s32[]{:T(128)S(6)} %select_n.133, bf16[2048,512]{0,1:T(8,128)(2,1)S(1)} %get-tuple-element.173, bf16[2048,512]{0,1:T(8,128)(2,1)S(1)} %get-tuple-element.172), kind=kOutput, calls=%fused_computation.27 | convolution fusion | flops 5378408448 | bytes 12058628 | tf_op jit(solution)/shard_map/dot_general | solution.py:24
  412.7 4.0 fusion.18
  420.8 17.8 %convolution_convert_fusion.1 = bf16[2048,2560]{1,0:T(8,128)(2,1)} fusion(bf16[2048,512]{0,1:T(8,128)(2,1)} %copy-done.57, bf16[2048,512]{0,1:T(8,128)(2,1)} %copy-done.55, bf16[1280,1024]{1,0:T(8,128)(2,1)} %collective-permute-done.1, bf16[1280,1024]{1,0:T(8,128)(2,1)S(1)} %bitcast.49, pred[]{:T(512)S(6)} %eq.31), kind=kOutput, calls=%fused_computation.1 | convolution fusion | flops 10774642688 | bytes 19922944 | tf_op jit(solution)/shard_map/dot_general | solution.py:24
  438.5 111.6 %sum_norm_gather_backward.1 = (f32[128,2560]{1,0:T(8,128)}, f32[8,2560]{1,0:T(8,128)}, bf16[8,128,2560]{2,1,0:T(8,128)(2,1)}, bf16[8,128,2560]{2,1,0:T(8,128)(2,1)}) custom-call(bf16[8,2,128,2560]{3,2,1,0:T(8,128)(2,1)} %bitcast.72, f32[128,2560]{1,0:T(8,128)} %get-tuple-element.75.hidden.refs_6_, f32[128,2560]{1,0:T(8,128)} %out_grad.1, ...), custom_call_target="tpu_custom_call" | custom-call | flops 99999997952 | bytes 100000000 | tf_op jit(solution)/shard_map/sum_norm_gather_backward/pallas_call | solution.py:840
  551.2 10.0 %convolution_convert_fusion = bf16[2048,2560]{1,0:T(8,128)(2,1)} fusion(bf16[2048,512]{0,1:T(8,128)(2,1)} %copy-done.53, bf16[512,2560]{1,0:T(8,128)(2,1)S(1)} %copy-done.41), kind=kOutput, calls=%fused_computation | convolution fusion | flops 5373952000 | bytes 15204352 | tf_op jit(solution)/shard_map/dot_general | solution.py:24
  568.3 6.4 fusion.21
  574.8 4.2 fusion.24.mg_ref
  579.0 3.2 convolution_convert_fusion.5
  582.2 3.2 reshape.125
  587.7 9.9 %fusion.15 = bf16[1280,1024]{1,0:T(8,128)(2,1)} fusion(bf16[2048,2560]{1,0:T(8,128)(2,1)} %bitcast.71, s32[]{:T(128)S(6)} %select_n.134, bf16[2048,512]{0,1:T(8,128)(2,1)} %copy-done.57, bf16[2048,512]{0,1:T(8,128)(2,1)S(1)} %copy-done.56), kind=kOutput, calls=%fused_computation.28 | convolution fusion | flops 5378408448 | bytes 12058628 | tf_op jit(solution)/shard_map/dot_general | solution.py:24
  597.7 4.6 all-to-all-start
  608.4 19.4 %recur_backward.1 = (bf16[1024,512]{1,0:T(8,128)(2,1)S(1)}, bf16[1024,512]{1,0:T(8,128)(2,1)S(1)}, f32[512,256]{1,0:T(8,128)S(1)}, f32[512,256]{1,0:T(8,128)S(1)}, f32[8,512]{1,0:T(8,128)S(1)}) custom-call(f32[1024,512]{1,0:T(8,128)S(1)} %copy-done.9, f32[1024,512]{1,0:T(8,128)S(1)} %copy-done.2, f32[1024,512]{1,0:T(8,128)S(1)} %copy-done.5, ...), custom_call_target="tpu_custom_call" | custom-call | flops 524288 | bytes 524288 | tf_op jit(solution)/shard_map/recur_backward/pallas_call | solution.py:224
  633.6 27.8 %collective-permute-done.9 = bf16[1280,1024]{1,0:T(8,128)(2,1)} collective-permute-done((bf16[1280,1024]{1,0:T(8,128)(2,1)}, bf16[1280,1024]{1,0:T(8,128)(2,1)}, u32[]{:S(2)}, u32[]{:S(2)}) %collective-permute-start.9) | collective-permute-done | bytes 2621472 | tf_op jit(solution)/shard_map/ppermute | solution.py:1179
  664.5 3.8 collective-permute-start.10
  670.6 3.6 add_convert_fusion
  676.0 3.5 collective-permute-start.13
  679.6 7.4 convolution_convert_fusion.3
  686.9 4.9 convolution_convert_fusion.4
  691.8 4.8 pad_maximum_fusion.refs_0_
  696.6 130.2 %sum_norm_backward.1 = (f32[128,2560]{1,0:T(8,128)}, f32[8,2560]{1,0:T(8,128)}, f32[80,640]{1,0:T(8,128)}, f32[640,960]{1,0:T(8,128)}, bf16[4,128,2560]{2,1,0:T(...) custom-call(bf16[4,2,128,2560]{3,2,1,0:T(8,128)(2,1)} %bitcast.54, ...), custom_call_target="tpu_custom_call" | custom-call | flops 1000000000 | bytes 1000000 | tf_op jit(solution)/shard_map/sum_norm_backward/pallas_call | solution.py:840
  828.5 10.5 %all-to-all-start.1 = ((f32[32,2,80]{2,1,0:T(2,128)}), f32[32,2,80]{2,1,0:T(2,128)S(1)}, u32[]{:S(2)}, u32[]{:S(2)}) async-start(f32[32,2,80]{2,1,0:T(2,128)} %maximum_bitcast_fusion), calls=%async_computation.1 | async-start | bytes 65536 | tf_op jit(solution)/shard_map/all_to_all | solution.py:246
  843.8 3.5 collective-permute-start.12
  853.1 8.3 collective-permute-done.12
  (225 shorter events, 91.2 us)
Async XLA Ops:
  7.2 373.9 %all-gather.2.cloned.1.call-start = ((), (), s32[]{:S(2)}) async-start(), calls=%async_computation.2 | async-start | bytes 11141120 | tf_op jit(solution)/shard_map/all_gather | solution.py:1245
  20.7 175.5 %copy-start.13 = (bf16[240,2560]{1,0:T(8,128)(2,1)S(1)}, bf16[240,2560]{1,0:T(8,128)(2,1)}, u32[]{:S(2)}) copy-start(bf16[240,2560]{1,0:T(8,128)(2,1)} %down.1) | copy-start | bytes 3686404
  196.1 165.4 %collective-permute-start.1 = (bf16[1280,1024]{1,0:T(8,128)(2,1)}, bf16[1280,1024]{1,0:T(8,128)(2,1)}, u32[]{:S(2)}, u32[]{:S(2)}) collective-permute-start(bf16[1280,1024]{1,0:T(8,128)(2,1)} %bitcast.47), channel_id=1, source_target_pairs={{0,16},{16,0},{1,17},{17,1},{2,18},{18,2},{3,19},{19,3},{4,20},{20... | collective-permute-start | bytes 7864328 | tf_op jit(solution)/shard_map/ppermute | solution.py:1237
  197.8 159.9 %collective-permute-start = (bf16[240,2560]{1,0:T(8,128)(2,1)}, bf16[240,2560]{1,0:T(8,128)(2,1)S(1)}, u32[]{:S(2)}, u32[]{:S(2)}) collective-permute-start(bf16[240,2560]{1,0:T(8,128)(2,1)} %get-tuple-element.185), channel_id=1, source_target_pairs={{0,1},{1,0},{2,3},{3,2},{4,5},{5,4},{6,7},{7,6},{8,9},{9,8},{10,11... | collective-permute-start | bytes 3686408 | tf_op jit(solution)/shard_map/ppermute | solution.py:1241
  198.9 17.0 %copy-start.10 = (f32[1024,4]{1,0:T(8,128)}, f32[1024,4]{1,0:T(8,128)S(1)}, u32[]{:S(2)}) copy-start(f32[1024,4]{1,0:T(8,128)S(1)} %stack.35.meta_ref) | copy-start | bytes 49156
  199.1 16.8 %copy-start.26 = (f32[16,512]{1,0:T(8,128)}, f32[16,512]{1,0:T(8,128)S(1)}, u32[]{:S(2)}) copy-start(f32[16,512]{1,0:T(8,128)S(1)} %concatenate.81.vec_ref) | copy-start | bytes 98308
  232.1 125.6 %copy-start.40 = (bf16[240,2560]{1,0:T(8,128)(2,1)S(1)}, bf16[240,2560]{1,0:T(8,128)(2,1)}, u32[]{:S(2)}) copy-start(bf16[240,2560]{1,0:T(8,128)(2,1)} %get-tuple-element.184) | copy-start | bytes 3686404
  381.1 31.6 %slice-start = ((s8[10485760]{0:T(1024)(128)(4,1)}), s8[2097152]{0:T(1024)(128)(4,1)S(1)}, s32[]{:S(2)}) async-start(s8[10485760]{0:T(1024)(128)(4,1)} %bitcast.67), calls=%async_computation.3 | async-start | bytes 4194304
  381.1 31.6 %slice-start.1 = ((s8[10485760]{0:T(1024)(128)(4,1)}), s8[4194304]{0:T(1024)(128)(4,1)S(1)}, s32[]{:S(2)}) async-start(s8[10485760]{0:T(1024)(128)(4,1)} %bitcast.67), calls=%async_computation.4 | async-start | bytes 8388608
  394.5 18.2 %copy-start.53 = (bf16[2048,512]{0,1:T(8,128)(2,1)}, bf16[2048,512]{0,1:T(8,128)(2,1)S(1)}, u32[]{:S(2)}) copy-start(bf16[2048,512]{0,1:T(8,128)(2,1)S(1)} %get-tuple-element.174) | copy-start | bytes 6291460
  394.5 18.2 %slice-start.2 = ((s8[10485760]{0:T(1024)(128)(4,1)}), s8[4194304]{0:T(1024)(128)(4,1)S(1)}, s32[]{:S(2)}) async-start(s8[10485760]{0:T(1024)(128)(4,1)} %bitcast.67), calls=%async_computation.5 | async-start | bytes 8388608
  407.3 153.9 %collective-permute-start.2 = (bf16[1280,1024]{1,0:T(8,128)(2,1)}, bf16[1280,1024]{1,0:T(8,128)(2,1)}, u32[]{:S(2)}, u32[]{:S(2)}) collective-permute-start(bf16[1280,1024]{1,0:T(8,128)(2,1)} %fusion.12), channel_id=1, source_target_pairs={{0,8},{24,16},{1,9},{25,17},{2,10},{26,18},{3,11},{27,19},{4,12},{... | collective-permute-start | bytes 7864328 | tf_op jit(solution)/shard_map/ppermute | solution.py:1175
  410.1 151.2 %collective-permute-start.3 = (bf16[1280,1024]{1,0:T(8,128)(2,1)}, bf16[1280,1024]{1,0:T(8,128)(2,1)}, u32[]{:S(2)}, u32[]{:S(2)}) collective-permute-start(bf16[1280,1024]{1,0:T(8,128)(2,1)} %fusion.12), channel_id=1, source_target_pairs={{8,16},{16,8},{9,17},{17,9},{10,18},{18,10},{11,19},{19,11},{12,20... | collective-permute-start | bytes 7864328 | tf_op jit(solution)/shard_map/ppermute | solution.py:1175
  416.7 144.6 %collective-permute-start.4 = (bf16[512,1280]{1,0:T(8,128)(2,1)}, bf16[512,1280]{1,0:T(8,128)(2,1)}, u32[]{:S(2)}, u32[]{:S(2)}) collective-permute-start(bf16[512,1280]{1,0:T(8,128)(2,1)} %fusion.18), channel_id=1, source_target_pairs={{0,8},{24,16},{1,9},{25,17},{2,10},{26,18},{3,11},{27,19},{4,12},{... | collective-permute-start | bytes 3932168 | tf_op jit(solution)/shard_map/ppermute | solution.py:1175
  419.0 142.3 %collective-permute-start.5 = (bf16[512,1280]{1,0:T(8,128)(2,1)}, bf16[512,1280]{1,0:T(8,128)(2,1)}, u32[]{:S(2)}, u32[]{:S(2)}) collective-permute-start(bf16[512,1280]{1,0:T(8,128)(2,1)} %fusion.18), channel_id=1, source_target_pairs={{8,16},{16,8},{9,17},{17,9},{10,18},{18,10},{11,19},{19,11},{12,20... | collective-permute-start | bytes 3932168 | tf_op jit(solution)/shard_map/ppermute | solution.py:1175
  438.5 112.7 %copy-start.41 = (bf16[512,2560]{1,0:T(8,128)(2,1)S(1)}, bf16[512,2560]{1,0:T(8,128)(2,1)}, u32[]{:S(2)}) copy-start(bf16[512,2560]{1,0:T(8,128)(2,1)} %pad.17) | copy-start | bytes 7864324
  551.2 17.1 %copy-start.54 = (bf16[2048,512]{0,1:T(8,128)(2,1)S(1)}, bf16[2048,512]{0,1:T(8,128)(2,1)}, u32[]{:S(2)}) copy-start(bf16[2048,512]{0,1:T(8,128)(2,1)} %copy-done.53) | copy-start | bytes 6291460
  561.3 13.5 %slice-start.5 = ((s8[5242880]{0:T(1024)(128)(4,1)}), s8[4194304]{0:T(1024)(128)(4,1)S(1)}, s32[]{:S(2)}) async-start(s8[5242880]{0:T(1024)(128)(4,1)} %bitcast.78), calls=%async_computation.8 | async-start | bytes 8388608
  561.3 13.5 %copy-start.51 = (bf16[8,80,3072]{2,1,0:T(8,128)(2,1)S(1)}, bf16[8,80,3072]{2,1,0:T(8,128)(2,1)}, u32[]{:S(2)}) copy-start(bf16[8,80,3072]{2,1,0:T(8,128)(2,1)} %get-tuple-element.71) | copy-start | bytes 11796484
  561.3 13.5 %slice-start.6 = ((s8[5242880]{0:T(1024)(128)(4,1)}), s8[1048576]{0:T(1024)(128)(4,1)S(1)}, s32[]{:S(2)}) async-start(s8[5242880]{0:T(1024)(128)(4,1)} %bitcast.78), calls=%async_computation.9 | async-start | bytes 2097152
  561.3 72.2 %collective-permute-start.6 = (bf16[512,1280]{1,0:T(8,128)(2,1)}, bf16[512,1280]{1,0:T(8,128)(2,1)}, u32[]{:S(2)}, u32[]{:S(2)}) collective-permute-start(bf16[512,1280]{1,0:T(8,128)(2,1)} %collective-permute-done.4), channel_id=1, source_target_pairs={{8,16},{16,8},{9,17},{17,9},{10,18},{18,10},{11,19},{19,11},{12,20... | collective-permute-start | bytes 3932168 | tf_op jit(solution)/shard_map/ppermute | solution.py:1179
  563.2 70.4 %collective-permute-start.7 = (bf16[512,1280]{1,0:T(8,128)(2,1)}, bf16[512,1280]{1,0:T(8,128)(2,1)}, u32[]{:S(2)}, u32[]{:S(2)}) collective-permute-start(bf16[512,1280]{1,0:T(8,128)(2,1)} %collective-permute-done.5), channel_id=1, source_target_pairs={{8,0},{16,24},{9,1},{17,25},{10,2},{18,26},{11,3},{19,27},{12,4},{... | collective-permute-start | bytes 3932168 | tf_op jit(solution)/shard_map/ppermute | solution.py:1179
  564.7 68.8 %collective-permute-start.8 = (bf16[1280,1024]{1,0:T(8,128)(2,1)}, bf16[1280,1024]{1,0:T(8,128)(2,1)}, u32[]{:S(2)}, u32[]{:S(2)}) collective-permute-start(bf16[1280,1024]{1,0:T(8,128)(2,1)} %collective-permute-done.2), channel_id=1, source_target_pairs={{8,16},{16,8},{9,17},{17,9},{10,18},{18,10},{11,19},{19,11},{12,20... | collective-permute-start | bytes 7864328 | tf_op jit(solution)/shard_map/ppermute | solution.py:1179
  566.9 94.5 %collective-permute-start.9 = (bf16[1280,1024]{1,0:T(8,128)(2,1)}, bf16[1280,1024]{1,0:T(8,128)(2,1)}, u32[]{:S(2)}, u32[]{:S(2)}) collective-permute-start(bf16[1280,1024]{1,0:T(8,128)(2,1)} %collective-permute-done.3), channel_id=1, source_target_pairs={{8,0},{16,24},{9,1},{17,25},{10,2},{18,26},{11,3},{19,27},{12,4},{... | collective-permute-start | bytes 7864328 | tf_op jit(solution)/shard_map/ppermute | solution.py:1179
  597.7 94.1 %all-to-all-start = ((bf16[8,320,320]{2,1,0:T(8,128)(2,1)}), bf16[8,320,320]{2,1,0:T(8,128)(2,1)}, u32[]{:S(2)}, u32[]{:S(2)}) async-start(bf16[8,320,320]{2,1,0:T(8,128)(2,1)} %bitcast.52), calls=%async_computation | async-start | bytes 3932160 | tf_op jit(solution)/shard_map/all_to_all | solution.py:246
  631.3 30.1 %copy-start.48 = (bf16[512,1280]{1,0:T(8,128)(2,1)S(1)}, bf16[512,1280]{1,0:T(8,128)(2,1)}, u32[]{:S(2)}) copy-start(bf16[512,1280]{1,0:T(8,128)(2,1)} %fusion.21) | copy-start | bytes 3932164
  664.5 32.2 %collective-permute-start.10 = (bf16[512,640]{1,0:T(8,128)(2,1)}, bf16[512,640]{1,0:T(8,128)(2,1)}, u32[]{:S(2)}, u32[]{:S(2)}) collective-permute-start(bf16[512,640]{1,0:T(8,128)(2,1)} %get-tuple-element.191), channel_id=1, source_target_pairs={{0,0},{1,4},{2,8},{3,12},{4,1},{5,5},{6,9},{7,13},{8,2},{9,6},{10,... | collective-permute-start | bytes 1966088 | tf_op jit(solution)/shard_map/ppermute | solution.py:1311
  668.3 28.4 %collective-permute-start.11 = (bf16[512,640]{1,0:T(8,128)(2,1)}, bf16[512,640]{1,0:T(8,128)(2,1)}, u32[]{:S(2)}, u32[]{:S(2)}) collective-permute-start(bf16[512,640]{1,0:T(8,128)(2,1)} %get-tuple-element.190), channel_id=1, source_target_pairs={{0,8},{1,12},{2,0},{3,4},{4,9},{5,13},{6,1},{7,5},{8,10},{9,14},{1... | collective-permute-start | bytes 1966088 | tf_op jit(solution)/shard_map/ppermute | solution.py:1311
  676.0 187.4 %collective-permute-start.14 = (bf16[640,1024]{1,0:T(8,128)(2,1)}, bf16[640,1024]{1,0:T(8,128)(2,1)}, u32[]{:S(2)}, u32[]{:S(2)}) collective-permute-start(bf16[640,1024]{1,0:T(8,128)(2,1)} %get-tuple-element.180), channel_id=1, source_target_pairs={{0,8},{1,12},{2,0},{3,4},{4,9},{5,13},{6,1},{7,5},{8,10},{9,14},{1... | collective-permute-start | bytes 3932168 | tf_op jit(solution)/shard_map/ppermute | solution.py:1311
  676.0 188.8 %collective-permute-start.13 = (bf16[640,1024]{1,0:T(8,128)(2,1)}, bf16[640,1024]{1,0:T(8,128)(2,1)}, u32[]{:S(2)}, u32[]{:S(2)}) collective-permute-start(bf16[640,1024]{1,0:T(8,128)(2,1)} %get-tuple-element.179), channel_id=1, source_target_pairs={{0,0},{1,4},{2,8},{3,12},{4,1},{5,5},{6,9},{7,13},{8,2},{9,6},{10,... | collective-permute-start | bytes 3932168 | tf_op jit(solution)/shard_map/ppermute | solution.py:1311
  828.5 24.0 %all-to-all-start.1 = ((f32[32,2,80]{2,1,0:T(2,128)}), f32[32,2,80]{2,1,0:T(2,128)S(1)}, u32[]{:S(2)}, u32[]{:S(2)}) async-start(f32[32,2,80]{2,1,0:T(2,128)} %maximum_bitcast_fusion), calls=%async_computation.1 | async-start | bytes 65536 | tf_op jit(solution)/shard_map/all_to_all | solution.py:246
  843.8 17.6 %collective-permute-start.12 = (f32[80,640]{1,0:T(8,128)S(1)}, f32[80,640]{1,0:T(8,128)S(1)}, u32[]{:S(2)}, u32[]{:S(2)}) collective-permute-start(f32[80,640]{1,0:T(8,128)S(1)} %copy-done.52), channel_id=1, source_target_pairs={{0,0},{1,4},{2,8},{3,12},{4,16},{5,20},{6,24},{7,28},{8,1},{9,5},{... | collective-permute-start | bytes 614408 | tf_op jit(solution)/shard_map/ppermute | solution.py:1349
  (51 other events, 215.3 us)
Sparse Core Ops, SparseCore 0:
  196.2 122.6 all-gather.1

commit v5 on v4

--- a/solution.py
+++ b/solution.py
@@ -911,7 +911,7 @@
         scratch += Fold.scratch(far, near, tok, width)
     got = comm_call(
         functools.partial(last_backward, n_lo, n_cx, n_hi, with_out, len(sums)), "sum_norm_backward", 3,
-        raw, (inputs, hidden_grad, gain, hidden), outs, scratch, 1,
+        raw, (inputs, hidden_grad, gain, hidden), outs, scratch, 100,
     )
     input_grad, gain_rows, packed_sum, summed = got[:4]
     if with_out:
@@ -1305,8 +1305,10 @@
         for s in range(2)
     ]
 
-    def settle(partial, got, axis):
-        both = (partial.astype(F32) + got.astype(F32)).astype(BF)
+    def both_halves(partial, got):
+        return (partial.astype(F32) + got.astype(F32)).astype(BF)
+
+    def settle(both, axis):
         odd = lax.rem(cx, 2)
         return tuple(lax.ppermute(half_of(both, lax.rem(odd + s, 2), axis, n_lo), CUBE, turns[s]) for s in range(2))
 
@@ -1323,9 +1325,8 @@
     gelu_low, linear_low, recur_wg, input_wg, sums = backward_call(
         mixed_grad, gelu_pre, conv_out, rec, inp, prev, linear_out, meta, vecs, recur_w, input_w
     )
-    gelu_low, linear_low, *stages = lax.optimization_barrier((gelu_low, linear_low, *dn_stage, *gu_stage))
+    gelu_low, linear_low, *stages = lax.optimization_barrier((gelu_low, linear_low, *dn_stage))
     got_dn = jnp.where(inner, *stages[:2])
-    got_gu = jnp.where(inner, *stages[2:])
     own_lows = jnp.concatenate(
         [
             lax.dynamic_slice_in_dim(gelu_low, own_off, own_ch, axis=1),
@@ -1337,14 +1338,18 @@
     first_part = dot(
         jnp.concatenate([gelu_low, linear_low], axis=1), jnp.concatenate([gelu_w, lin_w], axis=1), 1, 1
     ).astype(BF)
-    dn_a, dn_b = settle(own_dn, got_dn, 1)
-    gu_a, gu_b = settle(own_gu, got_gu, 0)
-    first_part, dn_a, dn_b = lax.optimization_barrier((first_part, dn_a, dn_b))
+    first_part, grad_gl, *gu_stage = lax.optimization_barrier((first_part, grad_gl, *gu_stage))
+    got_gu = jnp.where(inner, *gu_stage)
+    dn_a, dn_b = settle(both_halves(own_dn, got_dn), 1)
+    gu_sum = both_halves(own_gu, got_gu)
+    first_part, dn_a, dn_b, gu_sum = lax.optimization_barrier((first_part, dn_a, dn_b, gu_sum))
+    gu_a, gu_b = settle(gu_sum, 0)
     packed = jnp.concatenate([recur_wg, input_wg, pad_last(sums.T, 128)], axis=1)
     packed = lax.dynamic_slice_in_dim(packed, own_off, own_ch, axis=0)
     input_grad, gain_one_rows, packed, output, grad_three = last_backward_call(
         n_hi, n_lo, n_cx, first_part, out_part, (grad_gl, grad_proj), packed, inputs, hidden_grad, gain_first[None], hidden
     )
+    gain_one_rows, gu_a, gu_b = lax.optimization_barrier((gain_one_rows, gu_a, gu_b))
     routes = [(d * n_ctx + c, c * n_dp + d) for d in range(n_dp) for c in range(n_ctx)]
     packed = lax.ppermute(packed, EVERY, routes)
     grad_gl = grad_three[:, : 2 * own_ch]

time: 896 us -> 888 us (level)
  waiting for transfers between devices: 36.2 us -> 5.51 us
  starting transfers between devices: 44.3 us -> 62.1 us
  Pallas kernels: 571 us -> 583 us
    ppermute x4, starting transfers between devices: 8.93 us -> 36.8 us  [settle(): lax.ppermute(half_of(both, lax.rem(odd + s, 2), axis, n_lo), CUBE, turns[s])]
    ppermute x2, waiting for transfers between devices: 27.8 us -> 0.01 us  [swap_second(): lax.ppermute(crossed, DP, [(1, 0), (2, 3)])]
    pallas_call x3, Pallas kernels: 367 us -> 380 us  [comm_call(): pl.pallas_call(kernel, in_specs=[any_spec] * len(raw) + [vmem] * len(args...]
    unnamed x139 -> x151, local copies, waits for them, and re-layouts: 36.2 us -> 35.9 us
  transfers between devices with their start and end apart: 18 -> 18, of which waited for: 2 -> 1; matrix products, arithmetic and copies ran while one was open for 17% -> 17% of each run, Pallas kernels for 45% -> 47%
where the time goes in v5:
time: 888 us; the launch traced here: 878 us
  Pallas kernels  583 us (66%)
  matrix products  128 us (14%)
  starting transfers between devices  62.1 us (7%)
  local copies, waits for them, and re-layouts  59.6 us (7%)
  other arithmetic  24.2 us (3%)
  between operations  15.6 us (2%)
    pallas_call x3, Pallas kernels, comm_call(): pl.pallas_call(kernel, in_specs=[any_spec] * len(raw) + [vmem] * len(args...  380 us
    pallas_call x1, Pallas kernels, gather_start_call(): pl.pallas_call(functools.partial(gather_start, sizes), in_specs=[any_spec...  174 us
    dot_general x15, matrix products, dot(): lax.dot_general(a, b, (((ca,), (cb,)), ((), ())), preferred_element_type=...  128 us
    ppermute x4, starting transfers between devices, settle(): lax.ppermute(half_of(both, lax.rem(odd + s, 2), axis, n_lo), CUBE, turns[s])  36.8 us
    unnamed x151, local copies, waits for them, and re-layouts  35.9 us
    pallas_call x1, Pallas kernels, backward_call(): pl.pallas_call(backward_kernel, grid=grid, in_specs=[tok] * 7 + [mspec, v...  19.4 us
  transfers between devices with their start and end apart: 18, of which 1 were waited for; matrix products, arithmetic and copies ran while one was open for 17% of the time, Pallas kernels for 47%

profile of v5, /device:TPU:1, one launch (start us, length us, event | category | flops | bytes accessed | tf_op | source)
XLA Modules:
  0.0 878.4 jit_solution(2763732419190138983)
XLA Ops:
  20.7 173.9 %gather_start.1 = (bf16[4,4,2,80,1536]{4,3,2,1,0:T(8,128)(2,1)}, bf16[16,80,1024]{2,1,0:T(8,128)(2,1)S(1)}, bf16[4,80,3072]{2,1,0:T(8,128)(2,1)}, bf16[8,80,3072...) custom-call(bf16[80,2560]{1,0:T(8,128)(2,1)S(1)} %copy-done.32, ...), custom_call_target="tpu_custom_call" | custom-call | flops 99999997952 | bytes 100000000 | tf_op jit(solution)/shard_map/gather_start/pallas_call | solution.py:1154
  199.2 3.6 fusion.57
  203.2 7.3 convolution_convert_fusion.6.lin_ref
  210.7 5.2 fusion.65.gpre_ref
  216.0 10.3 %recur_forward.1 = (bf16[1024,512]{1,0:T(8,128)(2,1)S(1)}, f32[1024,512]{1,0:T(8,128)S(1)}, f32[1024,512]{1,0:T(8,128)S(1)}, f32[1024,512]{1,0:T(8,128)S(1)}, f32[1024,512]{1,0:T(8,128)S(1)}) custom-call(bf16[1024,512]{1,0:T(8,128)(2,1)S(1)} %convolution_convert_fusion.6.lin_ref, f32[1024,512]{1,0:T(8,128)S(1)} %fusion.65.gpre_ref, ...), custom_call_target="tpu_custom_call" | custom-call | flops 589299712 | bytes 12582912 | tf_op jit(solution)/shard_map/recur_forward/pallas_call | solution.py:190
  226.3 5.2 convolution_convert_fusion.2
  232.2 125.5 %sum_norm_gather_forward.1 = (f32[128,2560]{1,0:T(8,128)}, bf16[16,128,2560]{2,1,0:T(8,128)(2,1)}, bf16[4,128,2560]{2,1,0:T(8,128)(2,1)}) custom-call(bf16[4,2,128,2560]{3,2,1,0:T(8,128)(2,1)} %bitcast.52, f32[128,2560]{1,0:T(8,128)} %refs_3_.1, f32[1,2560]{1,0:T(1,128)} %get-tuple-element.207.gain), custom_call_target="tpu_custom_call" | custom-call | flops 1000000000 | bytes 1000000 | tf_op jit(solution)/shard_map/sum_norm_gather_forward/pallas_call | solution.py:840
  362.5 18.5 %fusion.36 = f32[2048,1024]{0,1:T(8,128)} fusion(bf16[2048,2560]{1,0:T(8,128)(2,1)} %bitcast.69, bf16[1280,1024]{1,0:T(8,128)(2,1)} %collective-permute-done.1, bf16[1280,1024]{1,0:T(8,128)(2,1)S(1)} %bitcast.48, pred[]{:T(512)S(6)} %eq.31), kind=kOutput, calls=%fused_computation.55 | convolution fusion | flops 10761011200 | bytes 24117248 | tf_op jit(solution)/shard_map/dot_general | solution.py:24
  381.0 13.3 %multiply_convert_fusion.2 = (bf16[2048,512]{0,1:T(8,128)(2,1)S(1)}, bf16[2048,512]{0,1:T(8,128)(2,1)S(1)}, bf16[2048,512]{0,1:T(8,128)(2,1)S(1)}) fusion(f32[2048,1024]{0,1:T(8,128)} %fusion.36, bf16[2048,2560]{1,0:T(8,128)(2,1)} %all-gather.2.cloned.1.call-done, bf16[480,2560]{1,0:T(8,128)(2,1)} %copy-done.39), kind=kOutput, calls=%fused_computation.22 | convolution fusion | flops 5393874944 | bytes 27623424 | tf_op jit(solution)/shard_map/dot_general | solution.py:24
  394.3 12.9 %fusion.12 = bf16[1280,1024]{1,0:T(8,128)(2,1)} fusion(bf16[2048,2560]{1,0:T(8,128)(2,1)} %bitcast.70, s32[]{:T(128)S(6)} %select_n.133, bf16[2048,512]{0,1:T(8,128)(2,1)S(1)} %get-tuple-element.185, bf16[2048,512]{0,1:T(8,128)(2,1)S(1)} %get-tuple-element.184), kind=kOutput, calls=%fused_computation.27 | convolution fusion | flops 5378408448 | bytes 12058628 | tf_op jit(solution)/shard_map/dot_general | solution.py:24
  412.5 4.0 fusion.18
  420.6 17.9 %convolution_convert_fusion.1 = bf16[2048,2560]{1,0:T(8,128)(2,1)} fusion(bf16[2048,512]{0,1:T(8,128)(2,1)} %copy-done.62, bf16[2048,512]{0,1:T(8,128)(2,1)} %copy-done.60, bf16[1280,1024]{1,0:T(8,128)(2,1)} %collective-permute-done.1, bf16[1280,1024]{1,0:T(8,128)(2,1)S(1)} %bitcast.49, pred[]{:T(512)S(6)} %eq.31), kind=kOutput, calls=%fused_computation.1 | convolution fusion | flops 10774642688 | bytes 19922944 | tf_op jit(solution)/shard_map/dot_general | solution.py:24
  438.5 111.5 %sum_norm_gather_backward.1 = (f32[128,2560]{1,0:T(8,128)}, f32[8,2560]{1,0:T(8,128)}, bf16[8,128,2560]{2,1,0:T(8,128)(2,1)}, bf16[8,128,2560]{2,1,0:T(8,128)(2,1)}) custom-call(bf16[8,2,128,2560]{3,2,1,0:T(8,128)(2,1)} %bitcast.73, f32[128,2560]{1,0:T(8,128)} %get-tuple-element.81.hidden.refs_6_, f32[128,2560]{1,0:T(8,128)} %out_grad.1, ...), custom_call_target="tpu_custom_call" | custom-call | flops 99999997952 | bytes 100000000 | tf_op jit(solution)/shard_map/sum_norm_gather_backward/pallas_call | solution.py:840
  551.7 10.3 %convolution_convert_fusion = bf16[2048,2560]{1,0:T(8,128)(2,1)} fusion(bf16[2048,512]{0,1:T(8,128)(2,1)} %copy-done.58, bf16[512,2560]{1,0:T(8,128)(2,1)S(1)} %copy-done.41), kind=kOutput, calls=%fused_computation | convolution fusion | flops 5373952000 | bytes 15204352 | tf_op jit(solution)/shard_map/dot_general | solution.py:24
  562.1 4.2 fusion.24.mg_ref
  569.5 4.0 fusion.21
  573.5 3.2 convolution_convert_fusion.5
  576.7 3.2 reshape.125
  582.2 10.0 %fusion.15 = bf16[1280,1024]{1,0:T(8,128)(2,1)} fusion(bf16[2048,2560]{1,0:T(8,128)(2,1)} %bitcast.71, s32[]{:T(128)S(6)} %select_n.134, bf16[2048,512]{0,1:T(8,128)(2,1)} %copy-done.62, bf16[2048,512]{0,1:T(8,128)(2,1)S(1)} %copy-done.61), kind=kOutput, calls=%fused_computation.28 | convolution fusion | flops 5378408448 | bytes 12058628 | tf_op jit(solution)/shard_map/dot_general | solution.py:24
  595.9 4.6 all-to-all-start
  606.6 19.4 %recur_backward.1 = (bf16[1024,512]{1,0:T(8,128)(2,1)S(1)}, bf16[1024,512]{1,0:T(8,128)(2,1)S(1)}, f32[512,256]{1,0:T(8,128)S(1)}, f32[512,256]{1,0:T(8,128)S(1)}, f32[8,512]{1,0:T(8,128)S(1)}) custom-call(f32[1024,512]{1,0:T(8,128)S(1)} %copy-done.8, f32[1024,512]{1,0:T(8,128)S(1)} %copy-done.1, f32[1024,512]{1,0:T(8,128)S(1)} %copy-done.4, ...), custom_call_target="tpu_custom_call" | custom-call | flops 524288 | bytes 524288 | tf_op jit(solution)/shard_map/recur_backward/pallas_call | solution.py:224
  634.0 3.8 collective-permute-start.10
  637.8 15.2 %collective-permute-start.11 = (bf16[512,640]{1,0:T(8,128)(2,1)S(1)}, bf16[512,640]{1,0:T(8,128)(2,1)S(1)}, u32[]{:S(2)}, u32[]{:S(2)}) collective-permute-start(bf16[512,640]{1,0:T(8,128)(2,1)S(1)} %get-tuple-element.202), channel_id=1, source_target_pairs={{0,8},{1,12},{2,0},{3,4},{4,9},{5,13},{6,1},{7,5},{8,10},{9,14},{1... | collective-permute-start | bytes 1966088 | tf_op jit(solution)/shard_map/ppermute | solution.py:1313
  653.7 7.4 convolution_convert_fusion.3
  661.1 4.9 convolution_convert_fusion.4
  666.0 3.7 add_convert_fusion
  671.7 5.0 collective-permute-start.12
  676.7 12.8 %collective-permute-start.13 = (bf16[640,1024]{1,0:T(8,128)(2,1)}, bf16[640,1024]{1,0:T(8,128)(2,1)}, u32[]{:S(2)}, u32[]{:S(2)}) collective-permute-start(bf16[640,1024]{1,0:T(8,128)(2,1)} %get-tuple-element.194), channel_id=1, source_target_pairs={{0,8},{1,12},{2,0},{3,4},{4,9},{5,13},{6,1},{7,5},{8,10},{9,14},{1... | collective-permute-start | bytes 3932168 | tf_op jit(solution)/shard_map/ppermute | solution.py:1313
  689.5 4.8 pad_maximum_fusion.refs_0_
  694.3 142.6 %sum_norm_backward.1 = (f32[128,2560]{1,0:T(8,128)}, f32[8,2560]{1,0:T(8,128)}, f32[80,640]{1,0:T(8,128)}, f32[640,960]{1,0:T(8,128)}, bf16[4,128,2560]{2,1,0:T(...) custom-call(bf16[4,2,128,2560]{3,2,1,0:T(8,128)(2,1)} %bitcast.79, ...), custom_call_target="tpu_custom_call" | custom-call | flops 99999997952 | bytes 100000000 | tf_op jit(solution)/shard_map/sum_norm_backward/pallas_call | solution.py:840
  846.5 5.4 collective-permute-done.14
  865.2 3.3 copy.63
  (239 shorter events, 85.9 us)
Async XLA Ops:
  7.2 373.8 %all-gather.2.cloned.1.call-start = ((), (), s32[]{:S(2)}) async-start(), calls=%async_computation.2 | async-start | bytes 11141120 | tf_op jit(solution)/shard_map/all_gather | solution.py:1245
  20.7 175.5 %copy-start.13 = (bf16[240,2560]{1,0:T(8,128)(2,1)S(1)}, bf16[240,2560]{1,0:T(8,128)(2,1)}, u32[]{:S(2)}) copy-start(bf16[240,2560]{1,0:T(8,128)(2,1)} %down.1) | copy-start | bytes 3686404
  196.1 165.5 %collective-permute-start.1 = (bf16[1280,1024]{1,0:T(8,128)(2,1)}, bf16[1280,1024]{1,0:T(8,128)(2,1)}, u32[]{:S(2)}, u32[]{:S(2)}) collective-permute-start(bf16[1280,1024]{1,0:T(8,128)(2,1)} %bitcast.47), channel_id=1, source_target_pairs={{0,16},{16,0},{1,17},{17,1},{2,18},{18,2},{3,19},{19,3},{4,20},{20... | collective-permute-start | bytes 7864328 | tf_op jit(solution)/shard_map/ppermute | solution.py:1237
  197.8 159.9 %collective-permute-start = (bf16[240,2560]{1,0:T(8,128)(2,1)}, bf16[240,2560]{1,0:T(8,128)(2,1)S(1)}, u32[]{:S(2)}, u32[]{:S(2)}) collective-permute-start(bf16[240,2560]{1,0:T(8,128)(2,1)} %get-tuple-element.197), channel_id=1, source_target_pairs={{0,1},{1,0},{2,3},{3,2},{4,5},{5,4},{6,7},{7,6},{8,9},{9,8},{10,11... | collective-permute-start | bytes 3686408 | tf_op jit(solution)/shard_map/ppermute | solution.py:1241
  198.9 17.0 %copy-start.9 = (f32[1024,4]{1,0:T(8,128)}, f32[1024,4]{1,0:T(8,128)S(1)}, u32[]{:S(2)}) copy-start(f32[1024,4]{1,0:T(8,128)S(1)} %stack.35.meta_ref) | copy-start | bytes 49156
  232.2 125.5 %copy-start.40 = (bf16[240,2560]{1,0:T(8,128)(2,1)S(1)}, bf16[240,2560]{1,0:T(8,128)(2,1)}, u32[]{:S(2)}) copy-start(bf16[240,2560]{1,0:T(8,128)(2,1)} %get-tuple-element.196) | copy-start | bytes 3686404
  381.0 31.6 %slice-start.2 = ((s8[10485760]{0:T(1024)(128)(4,1)}), s8[2097152]{0:T(1024)(128)(4,1)S(1)}, s32[]{:S(2)}) async-start(s8[10485760]{0:T(1024)(128)(4,1)} %bitcast.65), calls=%async_computation.5 | async-start | bytes 4194304
  381.0 31.6 %slice-start.3 = ((s8[10485760]{0:T(1024)(128)(4,1)}), s8[4194304]{0:T(1024)(128)(4,1)S(1)}, s32[]{:S(2)}) async-start(s8[10485760]{0:T(1024)(128)(4,1)} %bitcast.65), calls=%async_computation.6 | async-start | bytes 8388608
  394.3 18.2 %copy-start.58 = (bf16[2048,512]{0,1:T(8,128)(2,1)}, bf16[2048,512]{0,1:T(8,128)(2,1)S(1)}, u32[]{:S(2)}) copy-start(bf16[2048,512]{0,1:T(8,128)(2,1)S(1)} %get-tuple-element.186) | copy-start | bytes 6291460
  394.3 18.2 %slice-start.4 = ((s8[10485760]{0:T(1024)(128)(4,1)}), s8[4194304]{0:T(1024)(128)(4,1)S(1)}, s32[]{:S(2)}) async-start(s8[10485760]{0:T(1024)(128)(4,1)} %bitcast.65), calls=%async_computation.7 | async-start | bytes 8388608
  407.2 154.8 %collective-permute-start.2 = (bf16[1280,1024]{1,0:T(8,128)(2,1)}, bf16[1280,1024]{1,0:T(8,128)(2,1)}, u32[]{:S(2)}, u32[]{:S(2)}) collective-permute-start(bf16[1280,1024]{1,0:T(8,128)(2,1)} %fusion.12), channel_id=1, source_target_pairs={{0,8},{24,16},{1,9},{25,17},{2,10},{26,18},{3,11},{27,19},{4,12},{... | collective-permute-start | bytes 7864328 | tf_op jit(solution)/shard_map/ppermute | solution.py:1175
  410.0 152.0 %collective-permute-start.3 = (bf16[1280,1024]{1,0:T(8,128)(2,1)}, bf16[1280,1024]{1,0:T(8,128)(2,1)}, u32[]{:S(2)}, u32[]{:S(2)}) collective-permute-start(bf16[1280,1024]{1,0:T(8,128)(2,1)} %fusion.12), channel_id=1, source_target_pairs={{8,16},{16,8},{9,17},{17,9},{10,18},{18,10},{11,19},{19,11},{12,20... | collective-permute-start | bytes 7864328 | tf_op jit(solution)/shard_map/ppermute | solution.py:1175
  416.5 145.5 %collective-permute-start.4 = (bf16[512,1280]{1,0:T(8,128)(2,1)}, bf16[512,1280]{1,0:T(8,128)(2,1)}, u32[]{:S(2)}, u32[]{:S(2)}) collective-permute-start(bf16[512,1280]{1,0:T(8,128)(2,1)} %fusion.18), channel_id=1, source_target_pairs={{0,8},{24,16},{1,9},{25,17},{2,10},{26,18},{3,11},{27,19},{4,12},{... | collective-permute-start | bytes 3932168 | tf_op jit(solution)/shard_map/ppermute | solution.py:1175
  418.9 143.1 %collective-permute-start.5 = (bf16[512,1280]{1,0:T(8,128)(2,1)}, bf16[512,1280]{1,0:T(8,128)(2,1)}, u32[]{:S(2)}, u32[]{:S(2)}) collective-permute-start(bf16[512,1280]{1,0:T(8,128)(2,1)} %fusion.18), channel_id=1, source_target_pairs={{8,16},{16,8},{9,17},{17,9},{10,18},{18,10},{11,19},{19,11},{12,20... | collective-permute-start | bytes 3932168 | tf_op jit(solution)/shard_map/ppermute | solution.py:1175
  438.5 113.1 %copy-start.41 = (bf16[512,2560]{1,0:T(8,128)(2,1)S(1)}, bf16[512,2560]{1,0:T(8,128)(2,1)}, u32[]{:S(2)}) copy-start(bf16[512,2560]{1,0:T(8,128)(2,1)} %pad.17) | copy-start | bytes 7864324
  551.7 17.8 %slice-start.5 = ((s8[10485760]{0:T(1024)(128)(4,1)}), s8[4194304]{0:T(1024)(128)(4,1)S(1)}, s32[]{:S(2)}) async-start(s8[10485760]{0:T(1024)(128)(4,1)} %bitcast.67), calls=%async_computation.8 | async-start | bytes 8388608
  551.7 17.8 %slice-start.6 = ((s8[10485760]{0:T(1024)(128)(4,1)}), s8[4194304]{0:T(1024)(128)(4,1)S(1)}, s32[]{:S(2)}) async-start(s8[10485760]{0:T(1024)(128)(4,1)} %bitcast.67), calls=%async_computation.9 | async-start | bytes 8388608
  566.3 65.5 %collective-permute-start.6 = (bf16[512,1280]{1,0:T(8,128)(2,1)}, bf16[512,1280]{1,0:T(8,128)(2,1)}, u32[]{:S(2)}, u32[]{:S(2)}) collective-permute-start(bf16[512,1280]{1,0:T(8,128)(2,1)} %collective-permute-done.4), channel_id=1, source_target_pairs={{8,16},{16,8},{9,17},{17,9},{10,18},{18,10},{11,19},{19,11},{12,20... | collective-permute-start | bytes 3932168 | tf_op jit(solution)/shard_map/ppermute | solution.py:1179
  568.2 63.6 %collective-permute-start.7 = (bf16[512,1280]{1,0:T(8,128)(2,1)}, bf16[512,1280]{1,0:T(8,128)(2,1)}, u32[]{:S(2)}, u32[]{:S(2)}) collective-permute-start(bf16[512,1280]{1,0:T(8,128)(2,1)} %collective-permute-done.5), channel_id=1, source_target_pairs={{8,0},{16,24},{9,1},{17,25},{10,2},{18,26},{11,3},{19,27},{12,4},{... | collective-permute-start | bytes 3932168 | tf_op jit(solution)/shard_map/ppermute | solution.py:1179
  592.2 73.8 %collective-permute-start.8 = (bf16[1280,1024]{1,0:T(8,128)(2,1)}, bf16[1280,1024]{1,0:T(8,128)(2,1)}, u32[]{:S(2)}, u32[]{:S(2)}) collective-permute-start(bf16[1280,1024]{1,0:T(8,128)(2,1)} %collective-permute-done.2), channel_id=1, source_target_pairs={{8,16},{16,8},{9,17},{17,9},{10,18},{18,10},{11,19},{19,11},{12,20... | collective-permute-start | bytes 7864328 | tf_op jit(solution)/shard_map/ppermute | solution.py:1179
  594.6 71.4 %collective-permute-start.9 = (bf16[1280,1024]{1,0:T(8,128)(2,1)}, bf16[1280,1024]{1,0:T(8,128)(2,1)}, u32[]{:S(2)}, u32[]{:S(2)}) collective-permute-start(bf16[1280,1024]{1,0:T(8,128)(2,1)} %collective-permute-done.3), channel_id=1, source_target_pairs={{8,0},{16,24},{9,1},{17,25},{10,2},{18,26},{11,3},{19,27},{12,4},{... | collective-permute-start | bytes 7864328 | tf_op jit(solution)/shard_map/ppermute | solution.py:1179
  595.9 93.6 %all-to-all-start = ((bf16[8,320,320]{2,1,0:T(8,128)(2,1)}), bf16[8,320,320]{2,1,0:T(8,128)(2,1)}, u32[]{:S(2)}, u32[]{:S(2)}) async-start(bf16[8,320,320]{2,1,0:T(8,128)(2,1)} %bitcast.51), calls=%async_computation | async-start | bytes 3932160 | tf_op jit(solution)/shard_map/all_to_all | solution.py:246
  631.8 21.9 %copy-start.45 = (bf16[2560,512]{1,0:T(8,128)(2,1)S(1)}, bf16[2560,512]{1,0:T(8,128)(2,1)}, u32[]{:S(2)}) copy-start(bf16[2560,512]{1,0:T(8,128)(2,1)} %copy-done.44) | copy-start | bytes 7864324
  633.8 19.2 %copy-start.23 = (bf16[1024,512]{1,0:T(8,128)(2,1)S(1)}, bf16[1024,512]{1,0:T(8,128)(2,1)}, u32[]{:S(2)}) copy-start(bf16[1024,512]{1,0:T(8,128)(2,1)} %copy-done.22) | copy-start | bytes 3145732
  633.8 19.5 %copy-start.21 = (bf16[1024,512]{1,0:T(8,128)(2,1)S(1)}, bf16[1024,512]{1,0:T(8,128)(2,1)}, u32[]{:S(2)}) copy-start(bf16[1024,512]{1,0:T(8,128)(2,1)} %copy-done.20) | copy-start | bytes 3145732
  633.8 19.9 %copy-start.43 = (bf16[2560,512]{1,0:T(8,128)(2,1)S(1)}, bf16[2560,512]{1,0:T(8,128)(2,1)}, u32[]{:S(2)}) copy-start(bf16[2560,512]{1,0:T(8,128)(2,1)} %copy-done.42) | copy-start | bytes 7864324
  634.0 35.8 %collective-permute-start.10 = (bf16[512,640]{1,0:T(8,128)(2,1)S(1)}, bf16[512,640]{1,0:T(8,128)(2,1)S(1)}, u32[]{:S(2)}, u32[]{:S(2)}) collective-permute-start(bf16[512,640]{1,0:T(8,128)(2,1)S(1)} %get-tuple-element.203), channel_id=1, source_target_pairs={{0,0},{1,4},{2,8},{3,12},{4,1},{5,5},{6,9},{7,13},{8,2},{9,6},{10,... | collective-permute-start | bytes 1966088 | tf_op jit(solution)/shard_map/ppermute | solution.py:1313
  637.8 32.0 %collective-permute-start.11 = (bf16[512,640]{1,0:T(8,128)(2,1)S(1)}, bf16[512,640]{1,0:T(8,128)(2,1)S(1)}, u32[]{:S(2)}, u32[]{:S(2)}) collective-permute-start(bf16[512,640]{1,0:T(8,128)(2,1)S(1)} %get-tuple-element.202), channel_id=1, source_target_pairs={{0,8},{1,12},{2,0},{3,4},{4,9},{5,13},{6,1},{7,5},{8,10},{9,14},{1... | collective-permute-start | bytes 1966088 | tf_op jit(solution)/shard_map/ppermute | solution.py:1313
  671.7 182.3 %collective-permute-start.12 = (bf16[640,1024]{1,0:T(8,128)(2,1)}, bf16[640,1024]{1,0:T(8,128)(2,1)}, u32[]{:S(2)}, u32[]{:S(2)}) collective-permute-start(bf16[640,1024]{1,0:T(8,128)(2,1)} %get-tuple-element.195), channel_id=1, source_target_pairs={{0,0},{1,4},{2,8},{3,12},{4,1},{5,5},{6,9},{7,13},{8,2},{9,6},{10,... | collective-permute-start | bytes 3932168 | tf_op jit(solution)/shard_map/ppermute | solution.py:1313
  676.7 177.4 %collective-permute-start.13 = (bf16[640,1024]{1,0:T(8,128)(2,1)}, bf16[640,1024]{1,0:T(8,128)(2,1)}, u32[]{:S(2)}, u32[]{:S(2)}) collective-permute-start(bf16[640,1024]{1,0:T(8,128)(2,1)} %get-tuple-element.194), channel_id=1, source_target_pairs={{0,8},{1,12},{2,0},{3,4},{4,9},{5,13},{6,1},{7,5},{8,10},{9,14},{1... | collective-permute-start | bytes 3932168 | tf_op jit(solution)/shard_map/ppermute | solution.py:1313
  836.9 15.0 %collective-permute-start.14 = (f32[80,640]{1,0:T(8,128)}, f32[80,640]{1,0:T(8,128)S(1)}, u32[]{:S(2)}, u32[]{:S(2)}) collective-permute-start(f32[80,640]{1,0:T(8,128)} %get-tuple-element.122), channel_id=1, source_target_pairs={{0,0},{1,4},{2,8},{3,12},{4,16},{5,20},{6,24},{7,28},{8,1},{9,5},{... | collective-permute-start | bytes 614408 | tf_op jit(solution)/shard_map/ppermute | solution.py:1354
  854.8 13.6 %all-to-all-start.1 = ((f32[32,2,80]{2,1,0:T(2,128)}), f32[32,2,80]{2,1,0:T(2,128)S(1)}, u32[]{:S(2)}, u32[]{:S(2)}) async-start(f32[32,2,80]{2,1,0:T(2,128)} %maximum_bitcast_fusion), calls=%async_computation.1 | async-start | bytes 65536 | tf_op jit(solution)/shard_map/all_to_all | solution.py:246
  (59 other events, 289.6 us)
Sparse Core Ops, SparseCore 0:
  196.2 122.5 all-gather.1

commit v6 on v5

--- a/solution.py
+++ b/solution.py
@@ -921,6 +921,52 @@
     return input_grad, gain_rows, packed_sum, output, summed
 
 
+class Swap:
+    def __init__(self, own, near_tmp, far_tmp, got, sems):
+        self.own, self.near_tmp, self.far_tmp, self.got = own, near_tmp, far_tmp, got
+        self.s1, self.r1, self.s2, self.r2 = sems
+        hi, lo = lax.axis_index("hi"), lax.axis_index("lo")
+        self.inner = hi + lo == 1
+        self.outer = hi + lo != 1
+        self.beside = {"lo": 1 - lo}
+        self.over = {"hi": 1 - hi, "lo": 1 - lo}
+
+    @staticmethod
+    def sems():
+        return dma_sems(0, 2, 2, 2)
+
+    def first(self, action):
+        for cond, land, spot, target in (
+            (self.outer, self.near_tmp, 0, self.beside), (self.inner, self.far_tmp, 1, self.over)
+        ):
+            @pl.when(cond)
+            def _():
+                copy = send(self.own, land, self.s1, self.r1.at[spot], target)
+                copy.start() if action == "start" else copy.wait_send()
+
+    def arrived(self):
+        @pl.when(self.inner)
+        def _():
+            send(self.near_tmp, self.near_tmp, self.s1, self.r1.at[0], self.beside).wait_recv()
+            send(self.far_tmp, self.far_tmp, self.s1, self.r1.at[1], self.over).wait_recv()
+
+    def second(self, action):
+        @pl.when(self.inner)
+        def _():
+            for src, spot, target in ((self.near_tmp, 0, self.over), (self.far_tmp, 1, self.beside)):
+                copy = send(src, self.got, self.s2.at[spot], self.r2.at[spot], target)
+                copy.start() if action == "start" else copy.wait_send()
+
+    def done(self):
+        @pl.when(self.inner)
+        def _():
+            send(self.got, self.got, self.s2.at[0], self.r2.at[0], self.over).wait_recv()
+
+        @pl.when(self.outer)
+        def _():
+            send(self.got, self.got, self.s2.at[1], self.r2.at[1], self.beside).wait_recv()
+
+
 class Line:
     def __init__(self, n_hi, n_lo):
         self.n_lo = n_lo
@@ -983,9 +1029,9 @@
 
 
 def gather_start(sizes, gelu_w, lin_w, proj, rgate, igate, small, down, gate_w, up_w, inputs,
-                 gl_out, gu_out, pg_z, pg_win, normed_all, down_other, small_all,
+                 gl_out, gu_out, pg_z, pg_win, normed_all, down_other, small_all, near_tmp, far_tmp,
                  gu_send, own_pg, own_gl, own_rest, gl_s, gl_r, mate_s, mate_r, gu_s, gu_r, win_s, win_r,
-                 zp_s, zp_r, zg_s, zg_r, zm_s, zm_r, dn_s, dn_r,
+                 zp_s, zp_r, zg_s, zg_r, zm_s, zm_r, d0, d1, d2, d3,
                  normed, small_came, sm_own, sm_s, sm_r, *spread_s):
     n_hi, n_lo, n_cx, n_core, own_ch, bw, span = sizes
     n_ctx = n_cx * n_core
@@ -1109,11 +1155,13 @@
         to = lax.rem(spot + s, n_cube)
         gu_copies.append(send(gu_send.at[to], gu_out.at[spot], gu_s.at[s], gu_r.at[s], in_cube(to)))
         gu_copies[-1].start()
-    down_copy = send(down, down_other, dn_s, dn_r, across())
+    swap = Swap(down, near_tmp, far_tmp, down_other, (d0, d1, d2, d3))
+    swap.first("start")
     for k in range(2, steps):
         line.run(gl_part, gl_sems, k - 1, "recv")
         line.run(gl_part, gl_sems, k, "start")
-    down_copy.start()
+    swap.arrived()
+    swap.second("start")
     line.run(gl_part, gl_sems, steps - 1, "recv")
     rows.end()
     for s in range(1, n_ctx):
@@ -1134,7 +1182,9 @@
         line.run(pg_part, pg_sems, k, "sent")
         line.run(gl_part, gl_sems, k, "sent")
         line.run(gl_part, gl_sems, k, "mate_recv")
-    down_copy.wait()
+    swap.first("wait")
+    swap.second("wait")
+    swap.done()
     vectors.end()
 
 
@@ -1151,18 +1201,18 @@
     vmem = pl.BlockSpec(memory_space=pltpu.VMEM)
     pg_width = width + 2 * bw
     hops = 2 * (n_dp - 1)
-    gl_out, gu_out, _, pg_win, normed_all, down_other, small_all = pl.pallas_call(
+    gl_out, gu_out, _, pg_win, normed_all, down_other, small_all, _, _ = pl.pallas_call(
         functools.partial(gather_start, sizes),
         in_specs=[any_spec] * 7 + [vmem] * 3,
-        out_specs=[any_spec] * 6 + [vmem],
+        out_specs=[any_spec] * 6 + [vmem] + [any_spec] * 2,
         out_shape=[
             sds(n_dp, n_cx, n_core, shard, 2 * wide), sds(n_cube, shard, 2 * ff_pad), sds(n_dp, shard, pg_width),
             sds(n_ctx, shard, pg_width), sds(n_ctx, *inputs.shape), sds(*down.shape),
-            sds(small.shape[0], width),
+            sds(small.shape[0], width), sds(*down.shape), sds(*down.shape),
         ],
         scratch_shapes=[pltpu.VMEM((n_cube, shard, 2 * ff_pad), BF)]
-        + dma_sems(3, 2, 2, 2 * n_cx, 2 * n_cx, 0, 0, n_cube, n_cube, n_ctx, n_ctx, hops, hops, hops, hops, hops, hops, 0, 0)
-        + [pltpu.VMEM(inputs.shape, BF), pltpu.VMEM((n_dp * n_ctx, *small.shape), BF)]
+        + dma_sems(3, 2, 2, 2 * n_cx, 2 * n_cx, 0, 0, n_cube, n_cube, n_ctx, n_ctx, hops, hops, hops, hops, hops, hops)
+        + Swap.sems() + [pltpu.VMEM(inputs.shape, BF), pltpu.VMEM((n_dp * n_ctx, *small.shape), BF)]
         + dma_sems(0, n_dp * n_ctx, n_dp * n_ctx) + Spread.sems(near, near),
         compiler_params=pltpu.CompilerParams(collective_id=4, has_side_effects=True, vmem_limit_bytes=40 << 20),
         cost_estimate=pl.CostEstimate(flops=10**11, bytes_accessed=10**8, transcendentals=0),

time: 888 us -> 886 us (level)
    unnamed x151 -> x153, local copies, waits for them, and re-layouts: 35.9 us -> 33.1 us
  transfers between devices with their start and end apart: 18 -> 18, of which waited for: 1 -> 2; matrix products, arithmetic and copies ran while one was open for 17% -> 17% of each run, Pallas kernels for 47% -> 47%
where the time goes in v6:
time: 886 us; the launch traced here: 876 us
  Pallas kernels  579 us (65%)
  matrix products  127 us (14%)
  starting transfers between devices  64.8 us (7%)
  local copies, waits for them, and re-layouts  57 us (6%)
  other arithmetic  25.6 us (3%)
  between operations  15.6 us (2%)
    pallas_call x3, Pallas kernels, comm_call(): pl.pallas_call(kernel, in_specs=[any_spec] * len(raw) + [vmem] * len(args...  380 us
    pallas_call x1, Pallas kernels, gather_start_call(): pl.pallas_call(functools.partial(gather_start, sizes), in_specs=[any_spec...  170 us
    dot_general x15, matrix products, dot(): lax.dot_general(a, b, (((ca,), (cb,)), ((), ())), preferred_element_type=...  127 us
    ppermute x4, starting transfers between devices, settle(): lax.ppermute(half_of(both, lax.rem(odd + s, 2), axis, n_lo), CUBE, turns[s])  36.1 us
    unnamed x153, local copies, waits for them, and re-layouts  33.1 us
    pallas_call x1, Pallas kernels, backward_call(): pl.pallas_call(backward_kernel, grid=grid, in_specs=[tok] * 7 + [mspec, v...  19.4 us
  transfers between devices with their start and end apart: 18, of which 2 were waited for; matrix products, arithmetic and copies ran while one was open for 17% of the time, Pallas kernels for 47%

profile of v6, /device:TPU:1, one launch (start us, length us, event | category | flops | bytes accessed | tf_op | source)
XLA Modules:
  0.0 875.8 jit_solution(7247974728576995769)
XLA Ops:
  20.7 169.6 %gather_start.1 = (bf16[4,4,2,80,1536]{4,3,2,1,0:T(8,128)(2,1)}, bf16[16,80,1024]{2,1,0:T(8,128)(2,1)}, bf16[4,80,3072]{2,1,0:T(8,128)(2,1)}, bf16[8,80,3072]{2,...) custom-call(bf16[80,2560]{1,0:T(8,128)(2,1)S(1)} %copy-done.30, ...), custom_call_target="tpu_custom_call" | custom-call | flops 99999997952 | bytes 100000000 | tf_op jit(solution)/shard_map/gather_start/pallas_call | solution.py:1204
  197.1 3.8 fusion.57
  201.4 7.3 convolution_convert_fusion.6.lin_ref
  208.9 2.9 fusion.65.gpre_ref
  211.8 10.3 %recur_forward.1 = (bf16[1024,512]{1,0:T(8,128)(2,1)S(1)}, f32[1024,512]{1,0:T(8,128)S(1)}, f32[1024,512]{1,0:T(8,128)S(1)}, f32[1024,512]{1,0:T(8,128)S(1)}, f32[1024,512]{1,0:T(8,128)S(1)}) custom-call(bf16[1024,512]{1,0:T(8,128)(2,1)S(1)} %convolution_convert_fusion.6.lin_ref, f32[1024,512]{1,0:T(8,128)S(1)} %fusion.65.gpre_ref, ...), custom_call_target="tpu_custom_call" | custom-call | flops 589299712 | bytes 12582912 | tf_op jit(solution)/shard_map/recur_forward/pallas_call | solution.py:190
  222.1 5.2 convolution_convert_fusion.2
  227.9 124.7 %sum_norm_gather_forward.1 = (f32[128,2560]{1,0:T(8,128)}, bf16[16,128,2560]{2,1,0:T(8,128)(2,1)}, bf16[4,128,2560]{2,1,0:T(8,128)(2,1)}) custom-call(bf16[4,2,128,2560]{3,2,1,0:T(8,128)(2,1)} %bitcast.49, f32[128,2560]{1,0:T(8,128)} %refs_3_.1, f32[1,2560]{1,0:T(1,128)} %get-tuple-element.207.gain), custom_call_target="tpu_custom_call" | custom-call | flops 1000000000 | bytes 1000000 | tf_op jit(solution)/shard_map/sum_norm_gather_forward/pallas_call | solution.py:840
  357.5 19.5 %fusion.36 = f32[2048,1024]{0,1:T(8,128)} fusion(bf16[2048,2560]{1,0:T(8,128)(2,1)} %bitcast.66, bf16[1280,1024]{1,0:T(8,128)(2,1)} %collective-permute-done.1, bf16[1280,1024]{1,0:T(8,128)(2,1)} %bitcast.70, pred[]{:T(512)S(6)} %eq.31), kind=kOutput, calls=%fused_computation.55 | convolution fusion | flops 10761011200 | bytes 24117248 | tf_op jit(solution)/shard_map/dot_general | solution.py:24
  377.0 13.2 %multiply_convert_fusion.2 = (bf16[2048,512]{0,1:T(8,128)(2,1)S(1)}, bf16[2048,512]{0,1:T(8,128)(2,1)S(1)}, bf16[2048,512]{0,1:T(8,128)(2,1)S(1)}) fusion(f32[2048,1024]{0,1:T(8,128)} %fusion.36, bf16[2048,2560]{1,0:T(8,128)(2,1)} %all-gather.2.cloned.1.call-done, bf16[480,2560]{1,0:T(8,128)(2,1)S(1)} %maximum_select_fusion.1), kind=kOutput, calls=%fused_computation.22 | convolution fusion | flops 5393874944 | bytes 27623424 | tf_op jit(solution)/shard_map/dot_general | solution.py:24
  390.2 12.9 %fusion.12 = bf16[1280,1024]{1,0:T(8,128)(2,1)} fusion(bf16[2048,2560]{1,0:T(8,128)(2,1)} %bitcast.67, s32[]{:T(128)S(6)} %select_n.133, bf16[2048,512]{0,1:T(8,128)(2,1)S(1)} %get-tuple-element.185, bf16[2048,512]{0,1:T(8,128)(2,1)S(1)} %get-tuple-element.184), kind=kOutput, calls=%fused_computation.27 | convolution fusion | flops 5378408448 | bytes 12058628 | tf_op jit(solution)/shard_map/dot_general | solution.py:24
  408.0 4.0 fusion.18
  416.1 18.3 %convolution_convert_fusion.1 = bf16[2048,2560]{1,0:T(8,128)(2,1)} fusion(bf16[2048,512]{0,1:T(8,128)(2,1)} %copy-done.61, bf16[2048,512]{0,1:T(8,128)(2,1)} %copy-done.59, bf16[1280,1024]{1,0:T(8,128)(2,1)} %collective-permute-done.1, bf16[1280,1024]{1,0:T(8,128)(2,1)S(1)} %bitcast.71, pred[]{:T(512)S(6)} %eq.31), kind=kOutput, calls=%fused_computation.1 | convolution fusion | flops 10774642688 | bytes 19922944 | tf_op jit(solution)/shard_map/dot_general | solution.py:24
  434.4 111.5 %sum_norm_gather_backward.1 = (f32[128,2560]{1,0:T(8,128)}, f32[8,2560]{1,0:T(8,128)}, bf16[8,128,2560]{2,1,0:T(8,128)(2,1)}, bf16[8,128,2560]{2,1,0:T(8,128)(2,1)}) custom-call(bf16[8,2,128,2560]{3,2,1,0:T(8,128)(2,1)} %bitcast.73, f32[128,2560]{1,0:T(8,128)} %get-tuple-element.81.hidden.refs_6_, f32[128,2560]{1,0:T(8,128)} %out_grad.1, ...), custom_call_target="tpu_custom_call" | custom-call | flops 99999997952 | bytes 100000000 | tf_op jit(solution)/shard_map/sum_norm_gather_backward/pallas_call | solution.py:840
  547.5 10.3 %convolution_convert_fusion = bf16[2048,2560]{1,0:T(8,128)(2,1)} fusion(bf16[2048,512]{0,1:T(8,128)(2,1)} %copy-done.57, bf16[512,2560]{1,0:T(8,128)(2,1)S(1)} %copy-done.38), kind=kOutput, calls=%fused_computation | convolution fusion | flops 5373952000 | bytes 15204352 | tf_op jit(solution)/shard_map/dot_general | solution.py:24
  557.9 4.2 fusion.24.mg_ref
  565.3 4.0 fusion.21
  569.3 3.2 convolution_convert_fusion.5
  572.5 3.2 reshape.125
  578.0 10.0 %fusion.15 = bf16[1280,1024]{1,0:T(8,128)(2,1)} fusion(bf16[2048,2560]{1,0:T(8,128)(2,1)} %bitcast.68, s32[]{:T(128)S(6)} %select_n.134, bf16[2048,512]{0,1:T(8,128)(2,1)} %copy-done.61, bf16[2048,512]{0,1:T(8,128)(2,1)S(1)} %copy-done.60), kind=kOutput, calls=%fused_computation.28 | convolution fusion | flops 5378408448 | bytes 12058628 | tf_op jit(solution)/shard_map/dot_general | solution.py:24
  591.7 4.7 all-to-all-start
  602.4 19.4 %recur_backward.1 = (bf16[1024,512]{1,0:T(8,128)(2,1)S(1)}, bf16[1024,512]{1,0:T(8,128)(2,1)S(1)}, f32[512,256]{1,0:T(8,128)S(1)}, f32[512,256]{1,0:T(8,128)S(1)}, f32[8,512]{1,0:T(8,128)S(1)}) custom-call(f32[1024,512]{1,0:T(8,128)S(1)} %copy-done.8, f32[1024,512]{1,0:T(8,128)S(1)} %copy-done.1, f32[1024,512]{1,0:T(8,128)S(1)} %copy-done.4, ...), custom_call_target="tpu_custom_call" | custom-call | flops 524288 | bytes 524288 | tf_op jit(solution)/shard_map/recur_backward/pallas_call | solution.py:224
  629.8 3.8 collective-permute-start.10
  633.7 15.1 %collective-permute-start.11 = (bf16[512,640]{1,0:T(8,128)(2,1)S(1)}, bf16[512,640]{1,0:T(8,128)(2,1)S(1)}, u32[]{:S(2)}, u32[]{:S(2)}) collective-permute-start(bf16[512,640]{1,0:T(8,128)(2,1)S(1)} %get-tuple-element.202), channel_id=1, source_target_pairs={{0,8},{1,12},{2,0},{3,4},{4,9},{5,13},{6,1},{7,5},{8,10},{9,14},{1... | collective-permute-start | bytes 1966088 | tf_op jit(solution)/shard_map/ppermute | solution.py:1363
  649.5 7.4 convolution_convert_fusion.3
  656.9 4.9 convolution_convert_fusion.4
  662.8 3.7 add_convert_fusion
  668.4 4.3 collective-permute-start.12
  672.7 12.9 %collective-permute-start.13 = (bf16[640,1024]{1,0:T(8,128)(2,1)}, bf16[640,1024]{1,0:T(8,128)(2,1)}, u32[]{:S(2)}, u32[]{:S(2)}) collective-permute-start(bf16[640,1024]{1,0:T(8,128)(2,1)} %get-tuple-element.194), channel_id=1, source_target_pairs={{0,8},{1,12},{2,0},{3,4},{4,9},{5,13},{6,1},{7,5},{8,10},{9,14},{1... | collective-permute-start | bytes 3932168 | tf_op jit(solution)/shard_map/ppermute | solution.py:1363
  685.6 4.8 pad_maximum_fusion.refs_0_
  690.4 143.4 %sum_norm_backward.1 = (f32[128,2560]{1,0:T(8,128)}, f32[8,2560]{1,0:T(8,128)}, f32[80,640]{1,0:T(8,128)}, f32[640,960]{1,0:T(8,128)}, bf16[4,128,2560]{2,1,0:T(...) custom-call(bf16[4,2,128,2560]{3,2,1,0:T(8,128)(2,1)} %bitcast.81, ...), custom_call_target="tpu_custom_call" | custom-call | flops 99999997952 | bytes 100000000 | tf_op jit(solution)/shard_map/sum_norm_backward/pallas_call | solution.py:840
  843.4 5.9 collective-permute-done.14
  862.5 3.3 copy.63
  (242 shorter events, 88.7 us)
Async XLA Ops:
  7.2 369.8 %all-gather.2.cloned.1.call-start = ((), (), s32[]{:S(2)}) async-start(), calls=%async_computation.2 | async-start | bytes 11141120 | tf_op jit(solution)/shard_map/all_gather | solution.py:1295
  20.7 170.9 %copy-start.13 = (bf16[240,2560]{1,0:T(8,128)(2,1)S(1)}, bf16[240,2560]{1,0:T(8,128)(2,1)}, u32[]{:S(2)}) copy-start(bf16[240,2560]{1,0:T(8,128)(2,1)} %down.1) | copy-start | bytes 3686404
  190.3 167.1 %collective-permute-start.1 = (bf16[1280,1024]{1,0:T(8,128)(2,1)}, bf16[1280,1024]{1,0:T(8,128)(2,1)}, u32[]{:S(2)}, u32[]{:S(2)}) collective-permute-start(bf16[1280,1024]{1,0:T(8,128)(2,1)} %bitcast.69), channel_id=1, source_target_pairs={{0,16},{16,0},{1,17},{17,1},{2,18},{18,2},{3,19},{19,3},{4,20},{20... | collective-permute-start | bytes 7864328 | tf_op jit(solution)/shard_map/ppermute | solution.py:1287
  193.1 159.5 %collective-permute-start = (bf16[240,2560]{1,0:T(8,128)(2,1)}, bf16[240,2560]{1,0:T(8,128)(2,1)S(1)}, u32[]{:S(2)}, u32[]{:S(2)}) collective-permute-start(bf16[240,2560]{1,0:T(8,128)(2,1)} %get-tuple-element.197), channel_id=1, source_target_pairs={{0,1},{1,0},{2,3},{3,2},{4,5},{5,4},{6,7},{7,6},{8,9},{9,8},{10,11... | collective-permute-start | bytes 3686408 | tf_op jit(solution)/shard_map/ppermute | solution.py:1291
  196.8 14.9 %copy-start.9 = (f32[1024,4]{1,0:T(8,128)}, f32[1024,4]{1,0:T(8,128)S(1)}, u32[]{:S(2)}) copy-start(f32[1024,4]{1,0:T(8,128)S(1)} %stack.35.meta_ref) | copy-start | bytes 49156
  227.9 125.8 %copy-start.37 = (bf16[240,2560]{1,0:T(8,128)(2,1)S(1)}, bf16[240,2560]{1,0:T(8,128)(2,1)}, u32[]{:S(2)}) copy-start(bf16[240,2560]{1,0:T(8,128)(2,1)} %get-tuple-element.196) | copy-start | bytes 3686404
  376.9 31.0 %slice-start.2 = ((s8[10485760]{0:T(1024)(128)(4,1)}), s8[2097152]{0:T(1024)(128)(4,1)S(1)}, s32[]{:S(2)}) async-start(s8[10485760]{0:T(1024)(128)(4,1)} %bitcast.62), calls=%async_computation.5 | async-start | bytes 4194304
  377.0 31.0 %slice-start.3 = ((s8[10485760]{0:T(1024)(128)(4,1)}), s8[4194304]{0:T(1024)(128)(4,1)S(1)}, s32[]{:S(2)}) async-start(s8[10485760]{0:T(1024)(128)(4,1)} %bitcast.62), calls=%async_computation.6 | async-start | bytes 8388608
  390.2 17.8 %copy-start.57 = (bf16[2048,512]{0,1:T(8,128)(2,1)}, bf16[2048,512]{0,1:T(8,128)(2,1)S(1)}, u32[]{:S(2)}) copy-start(bf16[2048,512]{0,1:T(8,128)(2,1)S(1)} %get-tuple-element.186) | copy-start | bytes 6291460
  390.2 17.8 %slice-start.4 = ((s8[10485760]{0:T(1024)(128)(4,1)}), s8[4194304]{0:T(1024)(128)(4,1)S(1)}, s32[]{:S(2)}) async-start(s8[10485760]{0:T(1024)(128)(4,1)} %bitcast.62), calls=%async_computation.7 | async-start | bytes 8388608
  403.1 154.8 %collective-permute-start.2 = (bf16[1280,1024]{1,0:T(8,128)(2,1)}, bf16[1280,1024]{1,0:T(8,128)(2,1)}, u32[]{:S(2)}, u32[]{:S(2)}) collective-permute-start(bf16[1280,1024]{1,0:T(8,128)(2,1)} %fusion.12), channel_id=1, source_target_pairs={{0,8},{24,16},{1,9},{25,17},{2,10},{26,18},{3,11},{27,19},{4,12},{... | collective-permute-start | bytes 7864328 | tf_op jit(solution)/shard_map/ppermute | solution.py:1225
  405.9 152.0 %collective-permute-start.3 = (bf16[1280,1024]{1,0:T(8,128)(2,1)}, bf16[1280,1024]{1,0:T(8,128)(2,1)}, u32[]{:S(2)}, u32[]{:S(2)}) collective-permute-start(bf16[1280,1024]{1,0:T(8,128)(2,1)} %fusion.12), channel_id=1, source_target_pairs={{8,16},{16,8},{9,17},{17,9},{10,18},{18,10},{11,19},{19,11},{12,20... | collective-permute-start | bytes 7864328 | tf_op jit(solution)/shard_map/ppermute | solution.py:1225
  412.0 145.8 %collective-permute-start.4 = (bf16[512,1280]{1,0:T(8,128)(2,1)}, bf16[512,1280]{1,0:T(8,128)(2,1)}, u32[]{:S(2)}, u32[]{:S(2)}) collective-permute-start(bf16[512,1280]{1,0:T(8,128)(2,1)} %fusion.18), channel_id=1, source_target_pairs={{0,8},{24,16},{1,9},{25,17},{2,10},{26,18},{3,11},{27,19},{4,12},{... | collective-permute-start | bytes 3932168 | tf_op jit(solution)/shard_map/ppermute | solution.py:1225
  414.4 143.5 %collective-permute-start.5 = (bf16[512,1280]{1,0:T(8,128)(2,1)}, bf16[512,1280]{1,0:T(8,128)(2,1)}, u32[]{:S(2)}, u32[]{:S(2)}) collective-permute-start(bf16[512,1280]{1,0:T(8,128)(2,1)} %fusion.18), channel_id=1, source_target_pairs={{8,16},{16,8},{9,17},{17,9},{10,18},{18,10},{11,19},{19,11},{12,20... | collective-permute-start | bytes 3932168 | tf_op jit(solution)/shard_map/ppermute | solution.py:1225
  434.4 113.1 %copy-start.38 = (bf16[512,2560]{1,0:T(8,128)(2,1)S(1)}, bf16[512,2560]{1,0:T(8,128)(2,1)}, u32[]{:S(2)}) copy-start(bf16[512,2560]{1,0:T(8,128)(2,1)} %pad.17) | copy-start | bytes 7864324
  547.5 17.7 %slice-start.5 = ((s8[10485760]{0:T(1024)(128)(4,1)}), s8[4194304]{0:T(1024)(128)(4,1)S(1)}, s32[]{:S(2)}) async-start(s8[10485760]{0:T(1024)(128)(4,1)} %bitcast.64), calls=%async_computation.8 | async-start | bytes 8388608
  547.5 17.7 %slice-start.6 = ((s8[10485760]{0:T(1024)(128)(4,1)}), s8[4194304]{0:T(1024)(128)(4,1)S(1)}, s32[]{:S(2)}) async-start(s8[10485760]{0:T(1024)(128)(4,1)} %bitcast.64), calls=%async_computation.9 | async-start | bytes 8388608
  562.1 65.5 %collective-permute-start.6 = (bf16[512,1280]{1,0:T(8,128)(2,1)}, bf16[512,1280]{1,0:T(8,128)(2,1)}, u32[]{:S(2)}, u32[]{:S(2)}) collective-permute-start(bf16[512,1280]{1,0:T(8,128)(2,1)} %collective-permute-done.4), channel_id=1, source_target_pairs={{8,16},{16,8},{9,17},{17,9},{10,18},{18,10},{11,19},{19,11},{12,20... | collective-permute-start | bytes 3932168 | tf_op jit(solution)/shard_map/ppermute | solution.py:1229
  564.0 63.7 %collective-permute-start.7 = (bf16[512,1280]{1,0:T(8,128)(2,1)}, bf16[512,1280]{1,0:T(8,128)(2,1)}, u32[]{:S(2)}, u32[]{:S(2)}) collective-permute-start(bf16[512,1280]{1,0:T(8,128)(2,1)} %collective-permute-done.5), channel_id=1, source_target_pairs={{8,0},{16,24},{9,1},{17,25},{10,2},{18,26},{11,3},{19,27},{12,4},{... | collective-permute-start | bytes 3932168 | tf_op jit(solution)/shard_map/ppermute | solution.py:1229
  588.1 73.8 %collective-permute-start.8 = (bf16[1280,1024]{1,0:T(8,128)(2,1)}, bf16[1280,1024]{1,0:T(8,128)(2,1)}, u32[]{:S(2)}, u32[]{:S(2)}) collective-permute-start(bf16[1280,1024]{1,0:T(8,128)(2,1)} %collective-permute-done.2), channel_id=1, source_target_pairs={{8,16},{16,8},{9,17},{17,9},{10,18},{18,10},{11,19},{19,11},{12,20... | collective-permute-start | bytes 7864328 | tf_op jit(solution)/shard_map/ppermute | solution.py:1229
  590.4 72.3 %collective-permute-start.9 = (bf16[1280,1024]{1,0:T(8,128)(2,1)}, bf16[1280,1024]{1,0:T(8,128)(2,1)}, u32[]{:S(2)}, u32[]{:S(2)}) collective-permute-start(bf16[1280,1024]{1,0:T(8,128)(2,1)} %collective-permute-done.3), channel_id=1, source_target_pairs={{8,0},{16,24},{9,1},{17,25},{10,2},{18,26},{11,3},{19,27},{12,4},{... | collective-permute-start | bytes 7864328 | tf_op jit(solution)/shard_map/ppermute | solution.py:1229
  591.7 93.9 %all-to-all-start = ((bf16[8,320,320]{2,1,0:T(8,128)(2,1)}), bf16[8,320,320]{2,1,0:T(8,128)(2,1)}, u32[]{:S(2)}, u32[]{:S(2)}) async-start(bf16[8,320,320]{2,1,0:T(8,128)(2,1)} %bitcast.48), calls=%async_computation | async-start | bytes 3932160 | tf_op jit(solution)/shard_map/all_to_all | solution.py:246
  627.6 21.9 %copy-start.42 = (bf16[2560,512]{1,0:T(8,128)(2,1)S(1)}, bf16[2560,512]{1,0:T(8,128)(2,1)}, u32[]{:S(2)}) copy-start(bf16[2560,512]{1,0:T(8,128)(2,1)} %copy-done.41) | copy-start | bytes 7864324
  629.6 19.2 %copy-start.23 = (bf16[1024,512]{1,0:T(8,128)(2,1)S(1)}, bf16[1024,512]{1,0:T(8,128)(2,1)}, u32[]{:S(2)}) copy-start(bf16[1024,512]{1,0:T(8,128)(2,1)} %copy-done.22) | copy-start | bytes 3145732
  629.6 19.5 %copy-start.21 = (bf16[1024,512]{1,0:T(8,128)(2,1)S(1)}, bf16[1024,512]{1,0:T(8,128)(2,1)}, u32[]{:S(2)}) copy-start(bf16[1024,512]{1,0:T(8,128)(2,1)} %copy-done.20) | copy-start | bytes 3145732
  629.6 19.9 %copy-start.40 = (bf16[2560,512]{1,0:T(8,128)(2,1)S(1)}, bf16[2560,512]{1,0:T(8,128)(2,1)}, u32[]{:S(2)}) copy-start(bf16[2560,512]{1,0:T(8,128)(2,1)} %copy-done.39) | copy-start | bytes 7864324
  629.8 36.6 %collective-permute-start.10 = (bf16[512,640]{1,0:T(8,128)(2,1)S(1)}, bf16[512,640]{1,0:T(8,128)(2,1)S(1)}, u32[]{:S(2)}, u32[]{:S(2)}) collective-permute-start(bf16[512,640]{1,0:T(8,128)(2,1)S(1)} %get-tuple-element.203), channel_id=1, source_target_pairs={{0,0},{1,4},{2,8},{3,12},{4,1},{5,5},{6,9},{7,13},{8,2},{9,6},{10,... | collective-permute-start | bytes 1966088 | tf_op jit(solution)/shard_map/ppermute | solution.py:1363
  633.7 32.8 %collective-permute-start.11 = (bf16[512,640]{1,0:T(8,128)(2,1)S(1)}, bf16[512,640]{1,0:T(8,128)(2,1)S(1)}, u32[]{:S(2)}, u32[]{:S(2)}) collective-permute-start(bf16[512,640]{1,0:T(8,128)(2,1)S(1)} %get-tuple-element.202), channel_id=1, source_target_pairs={{0,8},{1,12},{2,0},{3,4},{4,9},{5,13},{6,1},{7,5},{8,10},{9,14},{1... | collective-permute-start | bytes 1966088 | tf_op jit(solution)/shard_map/ppermute | solution.py:1363
  668.4 183.0 %collective-permute-start.12 = (bf16[640,1024]{1,0:T(8,128)(2,1)}, bf16[640,1024]{1,0:T(8,128)(2,1)}, u32[]{:S(2)}, u32[]{:S(2)}) collective-permute-start(bf16[640,1024]{1,0:T(8,128)(2,1)} %get-tuple-element.195), channel_id=1, source_target_pairs={{0,0},{1,4},{2,8},{3,12},{4,1},{5,5},{6,9},{7,13},{8,2},{9,6},{10,... | collective-permute-start | bytes 3932168 | tf_op jit(solution)/shard_map/ppermute | solution.py:1363
  672.7 178.7 %collective-permute-start.13 = (bf16[640,1024]{1,0:T(8,128)(2,1)}, bf16[640,1024]{1,0:T(8,128)(2,1)}, u32[]{:S(2)}, u32[]{:S(2)}) collective-permute-start(bf16[640,1024]{1,0:T(8,128)(2,1)} %get-tuple-element.194), channel_id=1, source_target_pairs={{0,8},{1,12},{2,0},{3,4},{4,9},{5,13},{6,1},{7,5},{8,10},{9,14},{1... | collective-permute-start | bytes 3932168 | tf_op jit(solution)/shard_map/ppermute | solution.py:1363
  833.8 15.5 %collective-permute-start.14 = (f32[80,640]{1,0:T(8,128)}, f32[80,640]{1,0:T(8,128)S(1)}, u32[]{:S(2)}, u32[]{:S(2)}) collective-permute-start(f32[80,640]{1,0:T(8,128)} %get-tuple-element.122), channel_id=1, source_target_pairs={{0,0},{1,4},{2,8},{3,12},{4,16},{5,20},{6,24},{7,28},{8,1},{9,5},{... | collective-permute-start | bytes 614408 | tf_op jit(solution)/shard_map/ppermute | solution.py:1404
  852.2 13.6 %all-to-all-start.1 = ((f32[32,2,80]{2,1,0:T(2,128)}), f32[32,2,80]{2,1,0:T(2,128)S(1)}, u32[]{:S(2)}, u32[]{:S(2)}) async-start(f32[32,2,80]{2,1,0:T(2,128)} %maximum_bitcast_fusion), calls=%async_computation.1 | async-start | bytes 65536 | tf_op jit(solution)/shard_map/all_to_all | solution.py:246
  (60 other events, 304.9 us)
Sparse Core Ops, SparseCore 0:
  190.4 125.9 all-gather.1
